TPU v7x, 256 devices: a whole 4x4x8 slice. The times are simulated.
256 devices in a mesh: tm: 128 (over z, y, x), rhs: 2 (over core).
Axes of the slice: x: 4, y: 4, z: 8, core: 2. Of those that a mesh axis runs over, the one named last changes fastest.
Arguments:
- diag: float32 [262144, 512], P('tm', 'rhs'), as said below
- lower: float32 [262144, 512], P('tm', 'rhs'), as said below
- right_side: float32 [128, 262144], P('rhs', 'tm'), may hold values from -6 to 6
- coarse_sol: float32 [128, 65536], P('rhs', 'tm'), may hold values from -6 to 6
Outputs:
- coarse_diag: float32 [65536, 512], P('tm', 'rhs')
- coarse_lower: float32 [65536, 512], P('tm', 'rhs')
- coarse_rhs: float32 [128, 65536], P('rhs', 'tm')
- solution: float32 [128, 262144], P('rhs', 'tm')
Inputs may be any that keep to these rules, and one draw needn't show every extreme that they name: diag and lower are the diagonal and coupling blocks of a symmetric positive definite periodic block tridiagonal matrix whose eigenvalues are all at least 2; every diagonal block is symmetric. lower holds the coupling blocks of the matrix described for diag.
All inputs are finite; a program needn't handle non-finite values.
Results may differ from a plain program's by a relative error of at most 0.0003.
Values sent between devices are 32-bit elements; how exact they have to be, the bound alone decides.
A program may use at most 128 MiB of HBM per device.

v0:
```python
import jax
import jax.numpy as jnp
from jax import lax
from jax.sharding import PartitionSpec as P


def shifted(shard, axis, by):
    size = lax.axis_size(axis)
    return lax.ppermute(shard, axis, [(i, (i + by) % size) for i in range(size)])


def product(first_term, second_term):
    return jnp.dot(
        first_term, second_term, precision=lax.Precision.HIGHEST, preferred_element_type=jnp.float32
    )


def apply_inverse(factor, stacked):
    halfway = lax.linalg.triangular_solve(factor, stacked, left_side=True, lower=True)
    return lax.linalg.triangular_solve(
        factor, halfway, left_side=True, lower=True, transpose_a=True
    )


def slice_cols(matrix, first_col, col_count):
    return lax.dynamic_slice_in_dim(matrix, first_col, col_count, 1)


def slice_rows(matrix, first_row, row_count):
    return lax.dynamic_slice_in_dim(matrix, first_row, row_count, 0)


def eliminate_one(diag_block, link_block, next_link, rhs_block, first_col, col_count):
    factor = jnp.linalg.cholesky(diag_block)
    stacked = jnp.concatenate(
        [
            slice_cols(link_block, first_col, col_count),
            slice_rows(next_link, first_col, col_count).T,
            rhs_block,
        ],
        axis=1,
    )
    solved = apply_inverse(factor, stacked)
    return (
        factor,
        solved[:, :col_count],
        solved[:, col_count : 2 * col_count],
        solved[:, 2 * col_count :],
    )


def shards(diag, lower, right_side, coarse_sol):
    span_cols = diag.shape[1]
    block_order = span_cols * lax.axis_size("rhs")
    column_start = lax.axis_index("rhs") * span_cols
    next_share = shifted(lower[:block_order], "tm", -1)
    full_diag, full_lower, next_lower = (
        lax.all_gather(diag, "rhs", axis=1, tiled=True),
        lax.all_gather(lower, "rhs", axis=1, tiled=True),
        lax.all_gather(next_share, "rhs", axis=1, tiled=True),
    )
    diag_blocks = [
        full_diag[position * block_order : (position + 1) * block_order] for position in range(4)
    ]
    link_blocks = [
        full_lower[position * block_order : (position + 1) * block_order] for position in range(4)
    ]
    rhs_blocks = [
        right_side[:, position * block_order : (position + 1) * block_order].T
        for position in range(4)
    ]
    factor_one, prev_one, next_one, own_one = eliminate_one(
        diag_blocks[1], link_blocks[1], link_blocks[2], rhs_blocks[1], column_start, span_cols
    )
    factor_three, prev_three, next_three, own_three = eliminate_one(
        diag_blocks[3], link_blocks[3], next_lower, rhs_blocks[3], column_start, span_cols
    )
    came_prev, came_next, came_own = shifted((prev_three, next_three, own_three), "tm", 1)
    kept_diag = (
        slice_cols(diag_blocks[0], column_start, span_cols)
        - product(link_blocks[1].T, prev_one)
        - product(link_blocks[0], came_next)
    )
    kept_link = -product(link_blocks[0], came_prev)
    kept_rhs = (
        rhs_blocks[0] - product(link_blocks[1].T, own_one) - product(link_blocks[0], came_own)
    )
    odd_diag = (
        slice_cols(diag_blocks[2], column_start, span_cols)
        - product(link_blocks[3].T, prev_three)
        - product(link_blocks[2], next_one)
    )
    odd_link = -product(link_blocks[2], prev_one)
    odd_rhs = (
        rhs_blocks[2] - product(link_blocks[3].T, own_three) - product(link_blocks[2], own_one)
    )
    next_piece = shifted(kept_link, "tm", -1)
    odd_full, kept_link_full, odd_link_full, following = (
        lax.all_gather(odd_diag, "rhs", axis=1, tiled=True),
        lax.all_gather(kept_link, "rhs", axis=1, tiled=True),
        lax.all_gather(odd_link, "rhs", axis=1, tiled=True),
        lax.all_gather(next_piece, "rhs", axis=1, tiled=True),
    )
    factor_odd, prev_two, next_two, own_two = eliminate_one(
        odd_full, odd_link_full, following, odd_rhs, column_start, span_cols
    )
    came_prev_two, came_next_two, came_own_two = shifted((prev_two, next_two, own_two), "tm", 1)
    coarse_diag = (
        kept_diag - product(odd_link_full.T, prev_two) - product(kept_link_full, came_next_two)
    )
    coarse_lower = -product(kept_link_full, came_prev_two)
    coarse_rhs = (
        kept_rhs - product(odd_link_full.T, own_two) - product(kept_link_full, came_own_two)
    )
    kept_values = coarse_sol.T
    later_values = shifted(coarse_sol, "tm", -1).T
    odd_values = apply_inverse(
        factor_odd,
        odd_rhs - product(odd_link_full, kept_values) - product(following.T, later_values),
    )
    first_values = apply_inverse(
        factor_one,
        rhs_blocks[1]
        - product(link_blocks[1], kept_values)
        - product(link_blocks[2].T, odd_values),
    )
    third_values = apply_inverse(
        factor_three,
        rhs_blocks[3] - product(link_blocks[3], odd_values) - product(next_lower.T, later_values),
    )
    solution = jnp.concatenate([kept_values, first_values, odd_values, third_values], axis=0).T
    return (coarse_diag, coarse_lower, coarse_rhs.T, solution)


def solution(mesh):
    return jax.shard_map(
        shards,
        mesh=mesh,
        in_specs=(P("tm", "rhs"), P("tm", "rhs"), P("rhs", "tm"), P("rhs", "tm")),
        out_specs=(P("tm", "rhs"), P("tm", "rhs"), P("rhs", "tm"), P("rhs", "tm")),
        check_vma=False,
    )
```

profile of v0, /device:TPU:1, one launch (start us, length us, event | category | flops | bytes accessed | tf_op | source)
XLA Modules:
  0.0 675.7 jit_solution(9035725231035911094)
XLA Ops:
  8.3 11.1 %collective-permute-start = (f32[512,256]{1,0:T(8,128)S(1)}, f32[512,256]{1,0:T(8,128)S(1)}, u32[]{:S(2)}, u32[]{:S(2)}) collective-permute-start(f32[512,256]{1,0:T(8,128)S(1)} %slice.264), channel_id=1, source_target_pairs={{0,254},{2,0},{4,2},{6,4},{8,6},{10,8},{12,10},{14,12},{16,14},{18... | collective-permute-start | bytes 1572872 | tf_op jit(solution)/shard_map/ppermute | solution.py:9
  19.4 10.6 %collective-permute-done = f32[512,256]{1,0:T(8,128)S(1)} collective-permute-done((f32[512,256]{1,0:T(8,128)S(1)}, f32[512,256]{1,0:T(8,128)S(1)}, u32[]{:S(2)}, u32[]{:S(2)}) %collective-permute-start) | collective-permute-done | bytes 524320 | tf_op jit(solution)/shard_map/ppermute | solution.py:9
  47.5 20.3 %all-gather.8.cloned.1.call-done = f32[2048,512]{0,1:T(8,128)} async-done(((f32[2048,256]{0,1:T(8,128)}), f32[2048,512]{0,1:T(8,128)}) %all-gather.8.cloned.1.call-update) | async-done | bytes 4194320 | tf_op jit(solution)/shard_map/all_gather | solution.py:58
  75.6 11.7 %cholesky.374 = f32[128,128]{1,0:T(8,128)S(1)} custom-call(f32[128,128]{1,0:T(8,128)S(1)} %cholesky.586), custom_call_target="Cholesky" | custom-call | tf_op jit(solution)/shard_map/jit(cholesky)/cholesky | solution.py:34
  87.3 9.8 %custom-call.46 = f32[1,128,128]{1,2,0:T(8,128)S(1)} custom-call(f32[1,128,128]{2,1,0:T(8,128)S(1)} %get-tuple-element.179), custom_call_target="InvertDiagBlocksLowerTriangular" | custom-call | tf_op jit(solution)/shard_map/jit(cholesky)/cholesky | solution.py:34
  97.9 11.9 %cholesky.393 = f32[128,128]{1,0:T(8,128)S(1)} custom-call(f32[128,128]{1,0:T(8,128)S(1)} %cholesky.590), custom_call_target="Cholesky" | custom-call | tf_op jit(solution)/shard_map/jit(cholesky)/cholesky | solution.py:34
  109.9 9.8 %custom-call.47 = f32[1,128,128]{1,2,0:T(8,128)S(1)} custom-call(f32[1,128,128]{2,1,0:T(8,128)S(1)} %get-tuple-element.176), custom_call_target="InvertDiagBlocksLowerTriangular" | custom-call | tf_op jit(solution)/shard_map/jit(cholesky)/cholesky | solution.py:34
  120.4 11.7 %cholesky.414 = f32[128,128]{1,0:T(8,128)S(1)} custom-call(f32[128,128]{1,0:T(8,128)S(1)} %cholesky.595), custom_call_target="Cholesky" | custom-call | tf_op jit(solution)/shard_map/jit(cholesky)/cholesky | solution.py:34
  132.2 9.8 %custom-call.48 = f32[1,128,128]{1,2,0:T(8,128)S(1)} custom-call(f32[1,128,128]{2,1,0:T(8,128)S(1)} %get-tuple-element.173), custom_call_target="InvertDiagBlocksLowerTriangular" | custom-call | tf_op jit(solution)/shard_map/jit(cholesky)/cholesky | solution.py:34
  142.6 22.7 %cholesky.431 = f32[128,128]{1,0:T(8,128)S(1)} custom-call(f32[128,128]{1,0:T(8,128)S(1)} %convolution_subtract_fusion.30), custom_call_target="Cholesky" | custom-call | tf_op jit(solution)/shard_map/jit(cholesky)/cholesky | solution.py:34
  170.2 8.0 %while.24 = (s32[]{:T(128)}, f32[512,512]{1,0:T(8,128)S(1)}, s32[4,2]{0,1:T(2,128)S(1)}, f32[4,128,128]{2,1,0:T(8,128)S(1)}, s32[]{:T(128)}) while((s32[]{:T(128)}, f32[512,512]{1,0:T(8,128)S(1)}, s32[4,2]{0,1:T(2,128)S(1)}, f32[4,128,128]{2,1,0:T(8,128)S(1)}, s32[]{:T(128)}) %tuple.120), condition=%wide.while_cond.1, body=%wide.while_body.1.sunk | while | flops 2 | bytes 131181 | solution.py:20
  178.2 39.3 %custom-call.50 = f32[4,128,128]{1,2,0:T(8,128)S(1)} custom-call(f32[4,128,128]{2,1,0:T(8,128)S(1)} %get-tuple-element.90), custom_call_target="InvertDiagBlocksLowerTriangular" | custom-call | tf_op jit(solution)/shard_map/triangular_solve/custom-call.8 | solution.py:20
  232.2 12.1 %cholesky.446 = f32[128,128]{1,0:T(8,128)S(1)} custom-call(f32[128,128]{1,0:T(8,128)S(1)} %cholesky.599), custom_call_target="Cholesky" | custom-call | tf_op jit(solution)/shard_map/jit(cholesky)/cholesky | solution.py:34
  244.3 9.8 %custom-call.51 = f32[1,128,128]{1,2,0:T(8,128)S(1)} custom-call(f32[1,128,128]{2,1,0:T(8,128)S(1)} %get-tuple-element.169), custom_call_target="InvertDiagBlocksLowerTriangular" | custom-call | tf_op jit(solution)/shard_map/jit(cholesky)/cholesky | solution.py:34
  256.8 11.7 %cholesky.465 = f32[128,128]{1,0:T(8,128)S(1)} custom-call(f32[128,128]{1,0:T(8,128)S(1)} %cholesky.603), custom_call_target="Cholesky" | custom-call | tf_op jit(solution)/shard_map/jit(cholesky)/cholesky | solution.py:34
  268.5 9.8 %custom-call.52 = f32[1,128,128]{1,2,0:T(8,128)S(1)} custom-call(f32[1,128,128]{2,1,0:T(8,128)S(1)} %get-tuple-element.166), custom_call_target="InvertDiagBlocksLowerTriangular" | custom-call | tf_op jit(solution)/shard_map/jit(cholesky)/cholesky | solution.py:34
  279.9 11.9 %cholesky.486 = f32[128,128]{1,0:T(8,128)S(1)} custom-call(f32[128,128]{1,0:T(8,128)S(1)} %cholesky.608), custom_call_target="Cholesky" | custom-call | tf_op jit(solution)/shard_map/jit(cholesky)/cholesky | solution.py:34
  292.5 9.8 %custom-call.53 = f32[1,128,128]{1,2,0:T(8,128)S(1)} custom-call(f32[1,128,128]{2,1,0:T(8,128)S(1)} %get-tuple-element.163), custom_call_target="InvertDiagBlocksLowerTriangular" | custom-call | tf_op jit(solution)/shard_map/jit(cholesky)/cholesky | solution.py:34
  303.7 11.7 %cholesky.503 = f32[128,128]{1,0:T(8,128)S(1)} custom-call(f32[128,128]{1,0:T(8,128)S(1)} %convolution_subtract_fusion.29), custom_call_target="Cholesky" | custom-call | tf_op jit(solution)/shard_map/jit(cholesky)/cholesky | solution.py:34
  320.8 8.0 %while.25 = (s32[]{:T(128)}, f32[512,512]{1,0:T(8,128)S(1)}, s32[4,2]{0,1:T(2,128)S(1)}, f32[4,128,128]{2,1,0:T(8,128)S(1)}, s32[]{:T(128)}) while((s32[]{:T(128)}, f32[512,512]{1,0:T(8,128)S(1)}, s32[4,2]{0,1:T(2,128)S(1)}, f32[4,128,128]{2,1,0:T(8,128)S(1)}, s32[]{:T(128)}) %tuple.143), condition=%wide.while_cond.1.clone, body=%wide.while_body.1.clone.sunk | while | flops 2 | bytes 131181 | solution.py:20
  329.5 40.5 %custom-call.55 = f32[4,128,128]{1,2,0:T(8,128)S(1)} custom-call(f32[4,128,128]{2,1,0:T(8,128)} %copy-done.45), custom_call_target="InvertDiagBlocksLowerTriangular" | custom-call | tf_op jit(solution)/shard_map/triangular_solve/custom-call.8 | solution.py:20
  392.3 15.1 %collective-permute-done.2 = f32[512,256]{0,1:T(8,128)} collective-permute-done((f32[512,256]{0,1:T(8,128)}, f32[512,256]{0,1:T(8,128)}, u32[]{:S(2)}, u32[]{:S(2)}) %collective-permute-start.2) | collective-permute-done | bytes 524320 | tf_op jit(solution)/shard_map/ppermute | solution.py:9
  440.9 11.7 %cholesky.518 = f32[128,128]{1,0:T(8,128)S(1)} custom-call(f32[128,128]{1,0:T(8,128)S(1)} %cholesky.612), custom_call_target="Cholesky" | custom-call | tf_op jit(solution)/shard_map/jit(cholesky)/cholesky | solution.py:34
  454.9 11.3 %custom-call.56 = f32[1,128,128]{1,2,0:T(8,128)} custom-call(f32[1,128,128]{2,1,0:T(8,128)} %get-tuple-element.159), custom_call_target="InvertDiagBlocksLowerTriangular" | custom-call | tf_op jit(solution)/shard_map/jit(cholesky)/cholesky | solution.py:34
  470.0 13.6 %cholesky.537 = f32[128,128]{1,0:T(8,128)} custom-call(f32[128,128]{1,0:T(8,128)} %cholesky.616), custom_call_target="Cholesky" | custom-call | tf_op jit(solution)/shard_map/jit(cholesky)/cholesky | solution.py:34
  486.4 11.3 %custom-call.57 = f32[1,128,128]{1,2,0:T(8,128)} custom-call(f32[1,128,128]{2,1,0:T(8,128)} %get-tuple-element.156), custom_call_target="InvertDiagBlocksLowerTriangular" | custom-call | tf_op jit(solution)/shard_map/jit(cholesky)/cholesky | solution.py:34
  501.4 13.2 %cholesky.558 = f32[128,128]{1,0:T(8,128)} custom-call(f32[128,128]{1,0:T(8,128)} %cholesky.621), custom_call_target="Cholesky" | custom-call | tf_op jit(solution)/shard_map/jit(cholesky)/cholesky | solution.py:34
  516.7 11.3 %custom-call.58 = f32[1,128,128]{1,2,0:T(8,128)} custom-call(f32[1,128,128]{2,1,0:T(8,128)} %get-tuple-element.153), custom_call_target="InvertDiagBlocksLowerTriangular" | custom-call | tf_op jit(solution)/shard_map/jit(cholesky)/cholesky | solution.py:34
  530.9 13.3 %cholesky.575 = f32[128,128]{1,0:T(8,128)} custom-call(f32[128,128]{1,0:T(8,128)} %convolution_subtract_fusion.28), custom_call_target="Cholesky" | custom-call | tf_op jit(solution)/shard_map/jit(cholesky)/cholesky | solution.py:34
  550.6 10.2 %while.26 = (s32[]{:T(128)}, f32[512,512]{1,0:T(8,128)S(1)}, s32[4,2]{0,1:T(2,128)S(1)}, f32[4,128,128]{2,1,0:T(8,128)}, s32[]{:T(128)}) while((s32[]{:T(128)}, f32[512,512]{1,0:T(8,128)S(1)}, s32[4,2]{0,1:T(2,128)S(1)}, f32[4,128,128]{2,1,0:T(8,128)}, s32[]{:T(128)}) %tuple.144), condition=%wide.while_cond.1.clone.1, body=%wide.while_body.1.clone.1.sunk | while | flops 2 | bytes 132705 | solution.py:20
  560.8 40.8 %custom-call.60 = f32[4,128,128]{1,2,0:T(8,128)} custom-call(f32[4,128,128]{2,1,0:T(8,128)} %get-tuple-element.94), custom_call_target="InvertDiagBlocksLowerTriangular" | custom-call | tf_op jit(solution)/shard_map/triangular_solve/custom-call.8 | solution.py:20
  645.9 16.6 %collective-permute-done.4 = f32[512,256]{0,1:T(8,128)} collective-permute-done((f32[512,256]{0,1:T(8,128)S(1)}, f32[512,256]{0,1:T(8,128)}, u32[]{:S(2)}, u32[]{:S(2)}) %collective-permute-start.4) | collective-permute-done | bytes 524320 | tf_op jit(solution)/shard_map/ppermute | solution.py:9
  (359 shorter events, 207.7 us)
Async XLA Ops:
  7.2 38.5 %all-gather.12.cloned.1.call-start = ((), (), s32[]{:S(2)}) async-start(), calls=%async_computation.2 | async-start | bytes 1572864 | tf_op jit(solution)/shard_map/all_gather | solution.py:60
  8.3 21.7 %collective-permute-start = (f32[512,256]{1,0:T(8,128)S(1)}, f32[512,256]{1,0:T(8,128)S(1)}, u32[]{:S(2)}, u32[]{:S(2)}) collective-permute-start(f32[512,256]{1,0:T(8,128)S(1)} %slice.264), channel_id=1, source_target_pairs={{0,254},{2,0},{4,2},{6,4},{8,6},{10,8},{12,10},{14,12},{16,14},{18... | collective-permute-start | bytes 1572872 | tf_op jit(solution)/shard_map/ppermute | solution.py:9
  30.8 36.9 %all-gather.8.cloned.1.call-start = ((), (), s32[]{:S(2)}) async-start(), calls=%async_computation | async-start | bytes 6291456 | tf_op jit(solution)/shard_map/all_gather | solution.py:58
  33.8 183.7 %all-gather.10.cloned.1.call-start = ((), (), s32[]{:S(2)}) async-start(), calls=%async_computation.1 | async-start | bytes 6291456 | tf_op jit(solution)/shard_map/all_gather | solution.py:59
  37.3 398.3 %all-gather.16.cloned.1.call-start = ((), (), s32[]{:S(2)}) async-start(), calls=%async_computation.4 | async-start | bytes 1572864 | tf_op jit(solution)/shard_map/all_gather | solution.py:99
  315.5 3.9 copy-start.7
  320.7 50.5 %copy-start.39 = (f32[512,64]{0,1:T(8,128)S(1)}, f32[512,64]{0,1:T(8,128)}, u32[]{:S(2)}) copy-start(f32[512,64]{0,1:T(8,128)} %get-tuple-element.148) | copy-start | bytes 393220
  370.0 5.0 copy-start.15
  379.5 3.2 copy-start
  380.3 3.6 copy-start.8
  380.3 3.5 copy-start.9
  385.7 215.8 %all-gather.14.cloned.1.call-start = ((), (), s32[]{:S(2)}) async-start(), calls=%async_computation.3 | async-start | bytes 1572864 | tf_op jit(solution)/shard_map/all_gather | solution.py:101
  388.0 19.4 %collective-permute-start.2 = (f32[512,256]{0,1:T(8,128)}, f32[512,256]{0,1:T(8,128)}, u32[]{:S(2)}, u32[]{:S(2)}) collective-permute-start(f32[512,256]{0,1:T(8,128)} %get-tuple-element.147), channel_id=1, source_target_pairs={{0,2},{2,4},{4,6},{6,8},{8,10},{10,12},{12,14},{14,16},{16,18},{18... | collective-permute-start | bytes 1572872 | tf_op jit(solution)/shard_map/ppermute | solution.py:9
  392.2 213.7 %all-gather.18.cloned.1.call-start = ((), (), s32[]{:S(2)}) async-start(), calls=%async_computation.5 | async-start | bytes 1572864 | tf_op jit(solution)/shard_map/all_gather | solution.py:102
  411.4 4.4 copy-start.12
  411.4 4.4 copy-start.22
  411.4 12.9 %collective-permute-start.3 = (f32[512,256]{1,0:T(8,128)}, f32[512,256]{1,0:T(8,128)}, u32[]{:S(2)}, u32[]{:S(2)}) collective-permute-start(f32[512,256]{1,0:T(8,128)} %fusion), channel_id=1, source_target_pairs={{0,254},{2,0},{4,2},{6,4},{8,6},{10,8},{12,10},{14,12},{16,14},{18... | collective-permute-start | bytes 1572872 | tf_op jit(solution)/shard_map/ppermute | solution.py:9
  412.7 203.2 %collective-permute-start.8 = (f32[64,512]{1,0:T(8,128)}, f32[64,512]{1,0:T(8,128)}, u32[]{:S(2)}, u32[]{:S(2)}) collective-permute-start(f32[64,512]{1,0:T(8,128)} %param.16), channel_id=1, source_target_pairs={{0,254},{2,0},{4,2},{6,4},{8,6},{10,8},{12,10},{14,12},{16,14},{18... | collective-permute-start | bytes 393224 | tf_op jit(solution)/shard_map/ppermute | solution.py:9
  414.7 220.9 %collective-permute-start.6 = (f32[512,64]{0,1:T(8,128)}, f32[512,64]{0,1:T(8,128)}, u32[]{:S(2)}, u32[]{:S(2)}) collective-permute-start(f32[512,64]{0,1:T(8,128)} %pad_maximum_fusion.8), channel_id=1, source_target_pairs={{0,2},{2,4},{4,6},{6,8},{8,10},{10,12},{12,14},{14,16},{16,18},{18... | collective-permute-start | bytes 393224 | tf_op jit(solution)/shard_map/ppermute | solution.py:9
  415.6 223.9 %collective-permute-start.1 = (f32[512,256]{0,1:T(8,128)}, f32[512,256]{0,1:T(8,128)}, u32[]{:S(2)}, u32[]{:S(2)}) collective-permute-start(f32[512,256]{0,1:T(8,128)} %get-tuple-element.146), channel_id=1, source_target_pairs={{0,2},{2,4},{4,6},{6,8},{8,10},{10,12},{12,14},{14,16},{16,18},{18... | collective-permute-start | bytes 1572872 | tf_op jit(solution)/shard_map/ppermute | solution.py:9
  415.8 8.8 %copy-start.32 = (f32[64,2048]{1,0:T(8,128)S(1)}, f32[64,2048]{1,0:T(8,128)}, u32[]{:S(2)}) copy-start(f32[64,2048]{1,0:T(8,128)} %param.15) | copy-start | bytes 1572868
  415.8 8.8 %copy-start.33 = (f32[64,512]{1,0:T(8,128)S(1)}, f32[64,512]{1,0:T(8,128)}, u32[]{:S(2)}) copy-start(f32[64,512]{1,0:T(8,128)} %param.16) | copy-start | bytes 393220
  424.3 218.5 %all-gather.20.cloned.1.call-start = ((), (), s32[]{:S(2)}) async-start(), calls=%async_computation.6 | async-start | bytes 1572864 | tf_op jit(solution)/shard_map/all_gather | solution.py:100
  427.2 5.0 copy-start.26
  545.1 3.4 copy-start.6
  560.8 40.8 %copy-start.4 = (f32[512,512]{1,0:T(8,128)}, f32[512,512]{1,0:T(8,128)S(1)}, u32[]{:S(2)}) copy-start(f32[512,512]{1,0:T(8,128)S(1)} %get-tuple-element.339) | copy-start | bytes 3145732
  615.8 5.9 copy-start.1
  625.7 3.4 copy-start.17
  632.3 10.5 %collective-permute-start.7 = (f32[512,64]{0,1:T(8,128)}, f32[512,64]{0,1:T(8,128)}, u32[]{:S(2)}, u32[]{:S(2)}) collective-permute-start(f32[512,64]{0,1:T(8,128)} %pad_maximum_fusion.6), channel_id=1, source_target_pairs={{0,2},{2,4},{4,6},{6,8},{8,10},{10,12},{12,14},{14,16},{16,18},{18... | collective-permute-start | bytes 393224 | tf_op jit(solution)/shard_map/ppermute | solution.py:9
  633.2 32.4 %collective-permute-start.5 = (f32[512,256]{0,1:T(8,128)}, f32[512,256]{0,1:T(8,128)}, u32[]{:S(2)}, u32[]{:S(2)}) collective-permute-start(f32[512,256]{0,1:T(8,128)} %get-tuple-element.144), channel_id=1, source_target_pairs={{0,2},{2,4},{4,6},{6,8},{8,10},{10,12},{12,14},{14,16},{16,18},{18... | collective-permute-start | bytes 1572872 | tf_op jit(solution)/shard_map/ppermute | solution.py:9
  633.2 29.3 %collective-permute-start.4 = (f32[512,256]{0,1:T(8,128)S(1)}, f32[512,256]{0,1:T(8,128)}, u32[]{:S(2)}, u32[]{:S(2)}) collective-permute-start(f32[512,256]{0,1:T(8,128)S(1)} %get-tuple-element.145), channel_id=1, source_target_pairs={{0,2},{2,4},{4,6},{6,8},{8,10},{10,12},{12,14},{14,16},{16,18},{18... | collective-permute-start | bytes 1572872 | tf_op jit(solution)/shard_map/ppermute | solution.py:9
  642.8 19.7 %copy-start.3 = (f32[512,512]{1,0:T(8,128)S(1)}, f32[512,512]{1,0:T(8,128)}, u32[]{:S(2)}) copy-start(f32[512,512]{1,0:T(8,128)} %all-gather.20.cloned.1.call-done) | copy-start | bytes 3145732
  (30 other events, 44.3 us)
Sparse Core Ops, SparseCore 0:
  31.0 14.6 all-gather.11
  47.5 20.2 all-gather.7
  69.6 20.5 all-gather.9
  385.9 15.6 all-gather.15
  403.8 15.6 all-gather.13
  424.4 16.4 all-gather.17
  443.3 15.6 all-gather.19
where the time goes:
time: 688 us; the launch traced here: 676 us
  other arithmetic  393 us (57%)
  matrix products  97.5 us (14%)
  waiting for transfers between devices  74.5 us (11%)
  local copies, waits for them, and re-layouts  71.2 us (10%)
  between operations  23.6 us (3%)
  starting transfers between devices  15.5 us (2%)
    another operation x43, other arithmetic, eliminate_one(): factor = jnp.linalg.cholesky(diag_block)  262 us
    another operation x10, other arithmetic, apply_inverse(): lax.linalg.triangular_solve(factor, halfway, left_side=True, lower=True,...  124 us
    ppermute x9, waiting for transfers between devices, shifted(): lax.ppermute(shard, axis, [(i, (i + by) % size) for i in range(size)])  48.3 us
    dot_general x21, matrix products, product(): jnp.dot(first_term, second_term, precision=lax.Precision.HIGHEST, preferr...  48.2 us
    another operation x40, local copies, waits for them, and re-layouts, apply_inverse(): lax.linalg.triangular_solve(factor, halfway, left_side=True, lower=True,...  26.8 us
    all_gather x1, waiting for transfers between devices, shards(): lax.all_gather(diag, 'rhs', axis=1, tiled=True)  20.3 us
    unnamed x96, local copies, waits for them, and re-layouts  18.5 us
    another operation x42, matrix products, apply_inverse(): lax.linalg.triangular_solve(factor, halfway, left_side=True, lower=True,...  17.2 us
  transfers between devices with their start and end apart: 16, of which 6 were waited for; matrix products, arithmetic and copies ran while one was open for 57% of the time, Pallas kernels for 0%

commit v1 on v0

v1 whole, which is shorter than its diff:
```python
import functools

import jax
import jax.numpy as jnp
from jax import lax
from jax.experimental import pallas as pl
from jax.experimental.pallas import tpu as pltpu
from jax.sharding import PartitionSpec as P

f32, bf16 = jnp.float32, jnp.bfloat16
N = 512
HALF = 256
RHS = 128
LOWEST = 2.0
TOL = 2e-6
MAX_STEPS = 40
VMEM = pl.BlockSpec(memory_space=pltpu.VMEM)
ANY = pl.BlockSpec(memory_space=pl.ANY)
NN = (((1,), (0,)), ((), ()))
NT = (((1,), (1,)), ((), ()))


def split(x):
    high = x.astype(bf16)
    return high, (x - high.astype(f32)).astype(bf16)


def mul(a, b, dims=NN):
    one = lambda p, q: lax.dot_general(p, q, dims, preferred_element_type=f32)
    return one(a[0], b[0]) + (one(a[0], b[1]) + one(a[1], b[0]))


def identity(n):
    return (
        lax.broadcasted_iota(jnp.int32, (n, n), 0) == lax.broadcasted_iota(jnp.int32, (n, n), 1)
    ).astype(f32)


def newton(block, x_ref, d_ref):
    n = block.shape[0]
    parts = split(block)
    d_ref[0], d_ref[1] = parts
    top = jnp.maximum(jnp.max(jnp.sum(jnp.abs(block), axis=0, keepdims=True)), LOWEST)
    eye = identity(n)
    gap = (top - LOWEST) / (top + LOWEST)
    lead = 2.0 / (top + LOWEST)
    gain = 2.0 / (2.0 - gap * gap)
    x_ref[...] = (gain * lead) * (2.0 * eye - lead * block)
    gap = 0.5 * gain * gap * gap

    def more(state):
        step, gap = state
        return jnp.logical_and(gap > TOL, step < MAX_STEPS)

    def body(state):
        step, gap = state
        x = x_ref[...]
        x_parts = split(x)
        rest = split(eye - mul((d_ref[0], d_ref[1]), x_parts))
        gain = 2.0 / (2.0 - gap * gap)
        x_ref[...] = gain * (x + mul(x_parts, rest))
        return step + 1, 0.5 * gain * gap * gap

    lax.while_loop(more, body, (jnp.int32(0), gap))
    return x_ref[...]


def invert(block_ref, out_ref, x_ref, d_ref):
    first = newton(block_ref[:HALF, :HALF], x_ref, d_ref)
    cross = split(block_ref[HALF:, :HALF])
    lift = split(mul(cross, split(first)))
    out_ref[:HALF, :HALF] = first
    last = newton(block_ref[HALF:, HALF:] - mul(lift, cross, NT), x_ref, d_ref)
    low = -mul(split(last), lift)
    up = low.T
    out_ref[HALF:, HALF:] = last
    out_ref[HALF:, :HALF] = low
    out_ref[:HALF, HALF:] = up
    out_ref[:HALF, :HALF] = out_ref[:HALF, :HALF] - mul(split(up), lift)


def level_one(
    d_own, d_other, a_own, a_other, b_own, b_other, f_own, f_other, y_own, y_other,
    gv_ref, c_ref, hw_own_ref, hw_other_ref, v_ref, gzw_ref, hz_ref, w_ref,
    whole, inner, outer, x_ref, d_ref,
):
    core = lax.axis_index("rhs")
    mine = pl.multiple_of(core * HALF, HALF)
    other = pl.multiple_of(HALF - core * HALF, HALF)
    rows_mine = pl.multiple_of(core * 64, 64)
    rows_other = pl.multiple_of(64 - core * 64, 64)

    def join(own, partner):
        whole[:, pl.ds(mine, HALF)] = own
        whole[:, pl.ds(other, HALF)] = partner

    @pl.when(core == 0)
    def _():
        join(a_own[...], a_other[...])
        outer[...] = whole[...].T
        join(b_own[...], b_other[...])
        inner[...] = whole[...]

    @pl.when(core == 1)
    def _():
        join(a_own[...], a_other[...])
        inner[...] = whole[...].T
        outer[:, :HALF] = b_own[...]
        outer[:, HALF:] = b_other[...]

    join(d_own[...], d_other[...])
    invert(whole, v_ref, x_ref, d_ref)
    inverse = split(v_ref[...])
    g, h = split(inner[...]), split(outer[...])
    w_ref[pl.ds(rows_mine, 64)] = f_own[...]
    w_ref[pl.ds(rows_other, 64)] = f_other[...]

    @pl.when(core == 0)
    def _():
        hz_ref[pl.ds(rows_mine, 64)] = y_own[...]
        hz_ref[pl.ds(rows_other, 64)] = y_other[...]

    @pl.when(core == 1)
    def _():
        hz_ref[:64] = y_own[...]
        hz_ref[64:] = y_other[...]

    right = w_ref[...]
    moved = right - mul(split(hz_ref[...]), h)
    both = mul(split(jnp.concatenate([right, moved], axis=0)), inverse)
    w_ref[...] = both[RHS:]
    both = split(both)
    gzw_ref[...] = mul(both, g, NT)
    hz_ref[...] = mul((both[0][:RHS], both[1][:RHS]), h, NT)
    v = mul(inverse, g, NT)
    v_ref[...] = v
    v = split(v)
    gv_ref[...] = mul(g, v)
    c_ref[...] = -mul(h, v)
    hw = mul(h, split(mul(inverse, h, NT)))

    @pl.when(core == 0)
    def _():
        hw_own_ref[...] = hw[:, :HALF]
        hw_other_ref[...] = hw[:, HALF:]

    @pl.when(core == 1)
    def _():
        hw_own_ref[...] = hw[:, HALF:]
        hw_other_ref[...] = hw[:, :HALF]


def level_two(
    d_own, d_other, gv_own, gv_other, f_own, f_other, gzw_own, gzw_other,
    inverse_ref, zx_ref, whole, x_ref, d_ref,
):
    core = lax.axis_index("rhs")
    mine = pl.multiple_of(core * HALF, HALF)
    other = pl.multiple_of(HALF - core * HALF, HALF)
    rows_mine = pl.multiple_of(core * 64, 64)
    rows_other = pl.multiple_of(64 - core * 64, 64)
    whole[:, pl.ds(mine, HALF)] = d_own[...]
    whole[:, pl.ds(other, HALF)] = d_other[...]
    whole[...] = whole[...] - (gv_own[...] + gv_other[...])
    invert(whole, inverse_ref, x_ref, d_ref)
    for first_row in (0, RHS):
        zx_ref[pl.ds(first_row + rows_mine, 64)] = f_own[...]
        zx_ref[pl.ds(first_row + rows_other, 64)] = f_other[...]
    right = zx_ref[...] - (gzw_own[...] + gzw_other[...])
    zx_ref[...] = mul(split(right), split(inverse_ref[...]))


def survivors(
    inverse_ref, zx_ref, c_own, c_other, hw_own, hw_other, hz_own, hz_other,
    d0, f0, v_ref, w_ref,
    diag_ref, rhs_ref, out_diag_ref, out_low_ref, out_rhs_ref, x_own_ref, x_other_ref, u_ref,
    c_both, hw_both, hz_both,
):
    core = lax.axis_index("rhs")
    mine = pl.multiple_of(core * HALF, HALF)
    rows_mine = pl.multiple_of(core * 64, 64)
    rows_other = pl.multiple_of(64 - core * 64, 64)
    c_both[core] = c_own[...]
    c_both[1 - core] = c_other[...]
    hw_both[core] = hw_own[...]
    hw_both[1 - core] = hw_other[...]
    hz_both[core] = hz_own[pl.ds(rows_mine, 64)]
    hz_both[1 - core] = hz_other[pl.ds(rows_mine, 64)]
    inverse = split(inverse_ref[...])
    left, right = split(c_both[0]), split(c_both[1])
    u_left = split(mul(inverse, split(c_both[0, pl.ds(mine, HALF)]), NT))
    u_right = split(mul(inverse, split(c_both[1, pl.ds(mine, HALF)]), NT))
    out_low_ref[...] = -mul(right, u_left)
    out_diag_ref[...] = hw_both[1] + mul(right, u_right)
    diag_ref[...] = d0[...] - hw_both[0] - mul(left, u_left)
    z2 = split(zx_ref[pl.ds(rows_mine, 64)])
    out_rhs_ref[...] = hz_both[1] + mul(z2, right, NT)
    rhs_ref[...] = f0[...] - hz_both[0] - mul(z2, left, NT)
    x2 = zx_ref[RHS:]
    w_ref_new = w_ref[...] - mul(split(x2), split(v_ref[...]), NT)
    x_own_ref[...] = w_ref_new
    u_ref[...] = zx_ref[pl.ds(RHS + rows_mine, 64)]
    x_other_ref[...] = x_own_ref[pl.ds(rows_other, 64)]


def shape(*dims):
    return jax.ShapeDtypeStruct(dims, f32)


def local(body, outs, scratch, flops, args):
    size = sum(a.size for a in args) + sum(o.size for o in outs)
    return pl.pallas_call(
        body,
        out_shape=outs,
        in_specs=[VMEM] * len(args),
        out_specs=[VMEM] * len(outs),
        scratch_shapes=scratch,
        compiler_params=pltpu.CompilerParams(vmem_limit_bytes=56 << 20),
        cost_estimate=pl.CostEstimate(flops=flops, bytes_accessed=4 * size, transcendentals=0),
    )(*args)


def newton_scratch():
    return [pltpu.VMEM((HALF, HALF), f32), pltpu.VMEM((2, HALF, HALF), bf16)]


def exchange_body(windows, count, *refs):
    sources, targets = refs[:count], refs[count : count + len(windows)]
    send, recv = refs[count + len(windows) :]
    core = lax.axis_index("rhs")
    partner = {"rhs": 1 - core}
    barrier = pltpu.get_barrier_semaphore()
    pl.semaphore_signal(barrier, inc=1, device_id=partner, device_id_type=pl.DeviceIdType.MESH)
    pl.semaphore_wait(barrier, 1)
    copies = []
    for index, (source, window) in enumerate(windows):
        copies.append(
            pltpu.make_async_remote_copy(
                src_ref=window(sources[source], core),
                dst_ref=targets[index],
                send_sem=send.at[index],
                recv_sem=recv.at[index],
                device_id=partner,
                device_id_type=pl.DeviceIdType.MESH,
            )
        )
        copies[-1].start()
    for copy in copies:
        copy.wait()


def exchange(arrays, windows, outs, collective_id):
    return pl.pallas_call(
        functools.partial(exchange_body, windows, len(arrays)),
        out_shape=outs,
        in_specs=[ANY] * len(arrays),
        out_specs=[ANY] * len(outs),
        scratch_shapes=[pltpu.SemaphoreType.DMA((len(windows),))] * 2,
        compiler_params=pltpu.CompilerParams(collective_id=collective_id, has_side_effects=True),
    )(*arrays)


def rows_of(first, second):
    return lambda ref, core: ref.at[pl.ds(pl.multiple_of(first + core * (second - first), N), N)]


def columns_of(first, second):
    return lambda ref, core: ref.at[:, pl.ds(pl.multiple_of(first + core * (second - first), N), N)]


def all_of(ref, core):
    return ref


def shards(diag, lower, right_side, coarse_sol):
    core = lax.axis_index("rhs")
    runs = lax.axis_size("tm")
    back = lambda source: [
        (2 * ((i + 1) % runs) + source, 2 * i + 1) for i in range(runs)
    ]
    both = ("tm", "rhs")
    next_left, next_right = (lax.ppermute(lower[:N], both, back(source)) for source in (0, 1))
    later_left, later_right = (lax.ppermute(coarse_sol, both, back(source)) for source in (0, 1))

    d_other, a_other, b_part, d2_other, f_other, f2_other, y_part = exchange(
        (diag, lower, right_side, coarse_sol),
        (
            (0, rows_of(3 * N, N)),
            (1, rows_of(3 * N, N)),
            (1, rows_of(2 * N, 2 * N)),
            (0, rows_of(2 * N, 2 * N)),
            (2, columns_of(3 * N, N)),
            (2, columns_of(2 * N, 2 * N)),
            (3, all_of),
        ),
        [shape(N, HALF)] * 4 + [shape(64, N)] * 3,
        1,
    )
    own_rows = lambda array, first, second: lax.dynamic_slice_in_dim(
        array, first + core * (second - first), N, 0
    )
    d_own, a_own = own_rows(diag, N, 3 * N), own_rows(lower, N, 3 * N)
    f_own = lax.dynamic_slice_in_dim(right_side, N + core * 2 * N, N, 1)
    b_own = jnp.where(core == 0, lower[2 * N : 3 * N], next_left)
    b_other = jnp.where(core == 0, b_part, next_right)
    y_own = jnp.where(core == 0, coarse_sol, later_left)
    y_other = jnp.where(core == 0, y_part, later_right)
    gv, c, hw_own, hw_send, v, gzw, hz, w = local(
        level_one,
        [shape(N, N), shape(N, N), shape(N, HALF), shape(N, HALF), shape(N, N),
         shape(2 * RHS, N), shape(RHS, N), shape(RHS, N)],
        [pltpu.VMEM((N, N), f32)] * 3 + newton_scratch(),
        2 * N**3 * 24,
        (d_own, d_other, a_own, a_other, b_own, b_other, f_own, f_other, y_own, y_other),
    )
    gv_other, gzw_other = exchange(
        (gv, gzw), ((0, all_of), (1, all_of)), [shape(N, N), shape(2 * RHS, N)], 2
    )
    swap = lambda x: lax.ppermute(x, "rhs", [(0, 1), (1, 0)])
    c_other, hw_other, hz_other = swap(c), swap(hw_send), swap(hz)
    inverse, zx = local(
        level_two,
        [shape(N, N), shape(2 * RHS, N)],
        [pltpu.VMEM((N, N), f32)] + newton_scratch(),
        2 * N**3 * 24,
        (diag[2 * N : 3 * N], d2_other, gv, gv_other,
         right_side[:, 2 * N : 3 * N], f2_other, gzw, gzw_other),
    )
    diag_part, rhs_part, out_diag, out_low, out_rhs, x_own, x_send, u = local(
        survivors,
        [shape(N, HALF), shape(64, N), shape(N, HALF), shape(N, HALF), shape(64, N),
         shape(RHS, N), shape(64, N), shape(64, N)],
        [pltpu.VMEM((2, N, N), f32), pltpu.VMEM((2, N, HALF), f32), pltpu.VMEM((2, 64, N), f32)],
        2 * N**3 * 9,
        (inverse, zx, c, c_other, hw_own, hw_other, hz, hz_other,
         diag[:N], right_side[:, :N], v, w),
    )
    forward = lambda x: lax.ppermute(x, "tm", [(i, (i + 1) % runs) for i in range(runs)])
    coarse_lower, came_diag, came_rhs = forward(out_low), forward(out_diag), forward(out_rhs)
    x_other = swap(x_send)
    x_mine = lax.dynamic_slice_in_dim(x_own, core * 64, 64, 0)
    first = jnp.where(core == 0, x_mine, x_other)
    third = jnp.where(core == 0, x_other, x_mine)
    solution = jnp.concatenate([coarse_sol, first, u, third], axis=1)
    return diag_part - came_diag, coarse_lower, rhs_part - came_rhs, solution


def solution(mesh):
    return jax.shard_map(
        shards,
        mesh=mesh,
        in_specs=(P("tm", "rhs"), P("tm", "rhs"), P("rhs", "tm"), P("rhs", "tm")),
        out_specs=(P("tm", "rhs"), P("tm", "rhs"), P("rhs", "tm"), P("rhs", "tm")),
        check_vma=False,
    )
```

time: 688 us -> 122 us (0.18); the launches traced: 676 us -> 121 us
  other arithmetic: 393 us -> 11.2 us
  matrix products: 97.5 us -> 0 us
  local copies, waits for them, and re-layouts: 71.2 us -> 4.86 us
  Pallas kernels: 0 us -> 55 us
  waiting for transfers between devices: 74.5 us -> 29.4 us
  between operations: 23.6 us -> 0.77 us
    another operation x53 -> x0, other arithmetic: 385 us -> none  [the longest x43 262 us: eliminate_one(): factor = jnp.linalg.cholesky(diag_block)]
    pallas_call x0 -> x5, Pallas kernels: none -> 55 us  [the longest x3 43.4 us: local(): pl.pallas_call(body, out_shape=outs, in_specs=[VMEM] * len(args), out_spe...]
    another operation x102 -> x0, matrix products: 49.3 us -> none  [the longest x42 17.2 us: apply_inverse(): lax.linalg.triangular_solve(factor, halfway, left_side=True, lower=True,...]
    dot_general x21 -> x0, matrix products: 48.2 us -> none  [product(): jnp.dot(first_term, second_term, precision=lax.Precision.HIGHEST, preferr...]
    another operation x52 -> x0, local copies, waits for them, and re-layouts: 30.1 us -> none  [the longest x40 26.8 us: apply_inverse(): lax.linalg.triangular_solve(factor, halfway, left_side=True, lower=True,...]
    all_gather x7 -> x0, waiting for transfers between devices: 26.1 us -> none  [the longest x1 20.3 us: shards(): lax.all_gather(diag, 'rhs', axis=1, tiled=True)]
    ppermute x9 -> x11, waiting for transfers between devices: 48.3 us -> 29.4 us  [the longest x3 27.8 us: shards(): lax.ppermute(x, 'tm', [(i, (i + 1) % runs) for i in range(runs)])]
    unnamed x96 -> x15, local copies, waits for them, and re-layouts: 18.5 us -> 1.99 us
  transfers between devices with their start and end apart: 16 -> 11, of which waited for: 6 -> 4; matrix products, arithmetic and copies ran while one was open for 57% -> 8% of each run, Pallas kernels for 0% -> 21%
where the time goes in v1:
time: 122 us; the launch traced here: 121 us
  Pallas kernels  55 us (45%)
  waiting for transfers between devices  29.4 us (24%)
  starting transfers between devices  20.3 us (17%)
  other arithmetic  11.2 us (9%)
  local copies, waits for them, and re-layouts  4.86 us (4%)
    pallas_call x3, Pallas kernels, local(): pl.pallas_call(body, out_shape=outs, in_specs=[VMEM] * len(args), out_spe...  43.4 us
    ppermute x3, waiting for transfers between devices, shards(): lax.ppermute(x, 'tm', [(i, (i + 1) % runs) for i in range(runs)])  27.8 us
    ppermute x2, starting transfers between devices, shards(): lax.ppermute(lower[:N], both, back(source))  14.2 us
    pallas_call x2, Pallas kernels, exchange(): pl.pallas_call(functools.partial(exchange_body, windows, len(arrays)), ou...  11.6 us
    ppermute x2, starting transfers between devices, shards(): lax.ppermute(coarse_sol, both, back(source))  3.75 us
    select_n x1, other arithmetic, shards(): b_own = jnp.where(core == 0, lower[2 * N:3 * N], next_left)  2.78 us
  transfers between devices with their start and end apart: 11, of which 4 were waited for; matrix products, arithmetic and copies ran while one was open for 8% of the time, Pallas kernels for 21%

profile of v1, /device:TPU:1, one launch (start us, length us, event | category | flops | bytes accessed | tf_op | source)
XLA Modules:
  0.0 121.4 jit_solution(849277339186932077)
XLA Ops:
  0.6 1.1 slice.21
  1.7 1.3 %collective-permute-start = (f32[512,256]{1,0:T(8,128)S(1)}, f32[512,256]{1,0:T(8,128)S(1)}, u32[]{:S(2)}, u32[]{:S(2)}) collective-permute-start(f32[512,256]{1,0:T(8,128)S(1)} %slice.21), channel_id=1, source_target_pairs={{2,1},{4,3},{6,5},{8,7},{10,9},{12,11},{14,13},{16,15},{18,17},{20... | collective-permute-start | bytes 1572872 | tf_op jit(solution)/shard_map/ppermute | solution.py:282
  3.0 12.9 %collective-permute-start.1 = (f32[512,256]{1,0:T(8,128)S(1)}, f32[512,256]{1,0:T(8,128)}, u32[]{:S(2)}, u32[]{:S(2)}) collective-permute-start(f32[512,256]{1,0:T(8,128)S(1)} %slice.21), channel_id=1, source_target_pairs={{3,1},{5,3},{7,5},{9,7},{11,9},{13,11},{15,13},{17,15},{19,17},{21... | collective-permute-start | bytes 1572872 | tf_op jit(solution)/shard_map/ppermute | solution.py:282
  16.0 2.5 %collective-permute-start.3 = (f32[64,512]{1,0:T(8,128)}, f32[64,512]{1,0:T(8,128)S(1)}, u32[]{:S(2)}, u32[]{:S(2)}) collective-permute-start(f32[64,512]{1,0:T(8,128)} %refs_3_.1), channel_id=1, source_target_pairs={{3,1},{5,3},{7,5},{9,7},{11,9},{13,11},{15,13},{17,15},{19,17},{21... | collective-permute-start | bytes 393224 | tf_op jit(solution)/shard_map/ppermute | solution.py:283
  18.4 1.3 %collective-permute-start.2 = (f32[64,512]{1,0:T(8,128)}, f32[64,512]{1,0:T(8,128)S(1)}, u32[]{:S(2)}, u32[]{:S(2)}) collective-permute-start(f32[64,512]{1,0:T(8,128)} %refs_3_.1), channel_id=1, source_target_pairs={{2,1},{4,3},{6,5},{8,7},{10,9},{12,11},{14,13},{16,15},{18,17},{20... | collective-permute-start | bytes 393224 | tf_op jit(solution)/shard_map/ppermute | solution.py:283
  19.7 1.8 %fusion.1 = (f32[64,512]{1,0:T(8,128)}, f32[64,512]{1,0:T(8,128)}, f32[64,512]{1,0:T(8,128)}) fusion(f32[64,2048]{1,0:T(8,128)} %refs_2_.1, s32[]{:T(128)S(6)} %select_n.40), kind=kLoop, calls=%fused_computation.11 | loop fusion | bytes 786436 | tf_op jit(solution)/shard_map/slice | solution.py:336
  21.5 6.1 %shard_map.75 = (f32[512,256]{1,0:T(8,128)}, f32[512,256]{1,0:T(8,128)}, f32[512,256]{1,0:T(8,128)}, f32[512,256]{1,0:T(8,128)}, f32[64,512]{1,0:T(8,128)}, /*index=5*/f32[64,512]{1,0:T(8,128)}, f32[64,512]{1,0:T(8,128)}) custom-call(f32[2048,256]{1,0:T(8,128)} %refs_0_.1, f32[2048,256]{1,0:T(8,128)} %refs_1_.1, f32[64,2048]{1,0:T(8,128)} %refs_2_.1, ...), custom_call_target="tpu_custom_call" | custom-call | tf_op jit(solution)/shard_map/pallas_call | solution.py:253
  27.7 0.7 broadcast_select_fusion.2.y_own
  28.3 1.6 %collective-permute-done.3 = f32[64,512]{1,0:T(8,128)S(1)} collective-permute-done((f32[64,512]{1,0:T(8,128)}, f32[64,512]{1,0:T(8,128)S(1)}, u32[]{:S(2)}, u32[]{:S(2)}) %collective-permute-start.3) | collective-permute-done | bytes 131104 | tf_op jit(solution)/shard_map/ppermute | solution.py:283
  29.9 0.7 broadcast_select_fusion.1.y_other
  30.6 2.8 %slice_select_fusion = (f32[512,256]{1,0:T(8,128)}, f32[512,256]{1,0:T(8,128)}, f32[512,256]{1,0:T(8,128)}, f32[512,256]{1,0:T(8,128)}, f32[512,256]{1,0:T(8,128)}) fusion(f32[512,256]{1,0:T(8,128)S(1)} %collective-permute-done, f32[2048,256]{1,0:T(8,128)} %refs_1_.1, pred[]{:T(512)S(6)} %eq.2, s32[]{:T(128)S(6)} %select_n.40, f32[2048,256]{1,0:T(8,128)S(1)} %copy-done), kind=kLoop, calls=%fused_computation.1 | loop fusion | flops 131072 | bytes 5767173 | tf_op jit(solution)/shard_map/jit(_where)/select_n | solution.py:304
  33.4 1.9 %broadcast_select_fusion.b_other = f32[512,256]{1,0:T(8,128)} fusion(f32[512,256]{1,0:T(8,128)S(1)} %copy-done.3, f32[512,256]{1,0:T(8,128)} %collective-permute-done.1, pred[]{:T(512)S(6)} %eq.2), kind=kLoop, calls=%fused_computation.2 | loop fusion | flops 131072 | bytes 1572865 | tf_op jit(solution)/shard_map/jit(_where)/select_n | solution.py:305
  35.3 21.4 %shard_map.76 = (f32[512,512]{1,0:T(8,128)}, f32[512,512]{1,0:T(8,128)}, f32[512,256]{1,0:T(8,128)}, f32[512,256]{1,0:T(8,128)}, f32[512,512]{1,0:T(8,128)}, /*i...) custom-call(f32[512,256]{1,0:T(8,128)} %get-tuple-element.68.d_own, ...), custom_call_target="tpu_custom_call" | custom-call | flops 6442450944 | bytes 8912896 | tf_op jit(solution)/shard_map/pallas_call | solution.py:212
  56.7 0.4 collective-permute-start.4
  57.2 0.1 collective-permute-start.5
  57.3 0.4 collective-permute-start.6
  57.7 5.5 %shard_map.77 = (f32[512,512]{1,0:T(8,128)}, f32[256,512]{1,0:T(8,128)}) custom-call(f32[512,512]{1,0:T(8,128)} %get-tuple-element.37.refs_0_.gv_own, f32[256,512]{1,0:T(8,128)} %get-tuple-element.38.refs_1_.gzw_own), custom_call_target="tpu_custom_call" | custom-call | tf_op jit(solution)/shard_map/pallas_call | solution.py:253
  63.2 14.1 %shard_map.78 = (f32[512,512]{1,0:T(8,128)}, f32[256,512]{1,0:T(8,128)}) custom-call(f32[512,256]{1,0:T(8,128)} %get-tuple-element.69.d_own, f32[512,256]{1,0:T(8,128)} %get-tuple-element.31.d_other, f32[512,512]{1,0:T(8,128)} %get-tuple-element.37.refs_0_.gv_own, f32[512,512]{1,0:T(8,128)} %get-tuple-element.39.gv_other, ...), custom_call_target="tpu_custom_call" | custom-call | flops 6442450944 | bytes 6029312 | tf_op jit(solution)/shard_map/pallas_call | solution.py:212
  77.4 0.7 copy-done.6
  78.0 0.2 copy-done.5
  78.2 0.3 copy-done.4
  78.5 7.8 %shard_map.79 = (f32[512,256]{1,0:T(8,128)}, f32[64,512]{1,0:T(8,128)}, f32[512,256]{1,0:T(8,128)}, f32[512,256]{1,0:T(8,128)}, f32[64,512]{1,0:T(8,128)}, /*ind...) custom-call(f32[512,512]{1,0:T(8,128)} %get-tuple-element.42.inverse_ref, ...), custom_call_target="tpu_custom_call" | custom-call | flops 2415919104 | bytes 9568256 | tf_op jit(solution)/shard_map/pallas_call | solution.py:212
  86.5 0.5 collective-permute-start.10
  86.9 0.8 collective-permute-start.8
  87.7 9.6 %collective-permute-done.9 = f32[64,512]{1,0:T(8,128)S(1)} collective-permute-done((f32[64,512]{1,0:T(8,128)}, f32[64,512]{1,0:T(8,128)S(1)}, u32[]{:S(2)}, u32[]{:S(2)}) %collective-permute-start.9) | collective-permute-done | bytes 131104 | tf_op jit(solution)/shard_map/ppermute | solution.py:338
  97.3 1.6 %sub.7 = f32[64,512]{1,0:T(8,128)} subtract(f32[64,512]{1,0:T(8,128)} %get-tuple-element.53, f32[64,512]{1,0:T(8,128)S(1)} %collective-permute-done.9) | non-fusion elementwise | flops 32768 | bytes 393216 | tf_op jit(solution)/shard_map/sub | solution.py:345
  98.9 0.9 dynamic-slice_select_fusion.1
  99.8 1.7 %pad_maximum_fusion = f32[64,2048]{1,0:T(8,128)} fusion(f32[64,512]{1,0:T(8,128)S(1)} %get-tuple-element.67, f32[64,512]{1,0:T(8,128)} %get-tuple-element.57, f32[64,512]{1,0:T(8,128)S(1)} %get-tuple-element.66, f32[64,512]{1,0:T(8,128)S(1)} %copy-done.1), kind=kLoop, calls=%fused_computation | loop fusion | flops 393216 | bytes 1048576 | tf_op jit(solution)/shard_map/concatenate | solution.py:344
  101.6 7.0 %collective-permute-done.8 = f32[512,256]{1,0:T(8,128)S(1)} collective-permute-done((f32[512,256]{1,0:T(8,128)}, f32[512,256]{1,0:T(8,128)S(1)}, u32[]{:S(2)}, u32[]{:S(2)}) %collective-permute-start.8) | collective-permute-done | bytes 524320 | tf_op jit(solution)/shard_map/ppermute | solution.py:338
  108.5 11.2 %collective-permute-done.7 = f32[512,256]{1,0:T(8,128)S(1)} collective-permute-done((f32[512,256]{1,0:T(8,128)}, f32[512,256]{1,0:T(8,128)S(1)}, u32[]{:S(2)}, u32[]{:S(2)}) %collective-permute-start.7) | collective-permute-done | bytes 524320 | tf_op jit(solution)/shard_map/ppermute | solution.py:338
  119.8 0.9 sub.6
  120.6 0.8 copy.9
  (20 shorter events, 0.1 us)
Async XLA Ops:
  1.7 28.9 %collective-permute-start = (f32[512,256]{1,0:T(8,128)S(1)}, f32[512,256]{1,0:T(8,128)S(1)}, u32[]{:S(2)}, u32[]{:S(2)}) collective-permute-start(f32[512,256]{1,0:T(8,128)S(1)} %slice.21), channel_id=1, source_target_pairs={{2,1},{4,3},{6,5},{8,7},{10,9},{12,11},{14,13},{16,15},{18,17},{20... | collective-permute-start | bytes 1572872 | tf_op jit(solution)/shard_map/ppermute | solution.py:282
  3.0 30.4 %collective-permute-start.1 = (f32[512,256]{1,0:T(8,128)S(1)}, f32[512,256]{1,0:T(8,128)}, u32[]{:S(2)}, u32[]{:S(2)}) collective-permute-start(f32[512,256]{1,0:T(8,128)S(1)} %slice.21), channel_id=1, source_target_pairs={{3,1},{5,3},{7,5},{9,7},{11,9},{13,11},{15,13},{17,15},{19,17},{21... | collective-permute-start | bytes 1572872 | tf_op jit(solution)/shard_map/ppermute | solution.py:282
  16.0 13.9 %collective-permute-start.3 = (f32[64,512]{1,0:T(8,128)}, f32[64,512]{1,0:T(8,128)S(1)}, u32[]{:S(2)}, u32[]{:S(2)}) collective-permute-start(f32[64,512]{1,0:T(8,128)} %refs_3_.1), channel_id=1, source_target_pairs={{3,1},{5,3},{7,5},{9,7},{11,9},{13,11},{15,13},{17,15},{19,17},{21... | collective-permute-start | bytes 393224 | tf_op jit(solution)/shard_map/ppermute | solution.py:283
  18.4 9.2 %collective-permute-start.2 = (f32[64,512]{1,0:T(8,128)}, f32[64,512]{1,0:T(8,128)S(1)}, u32[]{:S(2)}, u32[]{:S(2)}) collective-permute-start(f32[64,512]{1,0:T(8,128)} %refs_3_.1), channel_id=1, source_target_pairs={{2,1},{4,3},{6,5},{8,7},{10,9},{12,11},{14,13},{16,15},{18,17},{20... | collective-permute-start | bytes 393224 | tf_op jit(solution)/shard_map/ppermute | solution.py:283
  21.5 6.1 %copy-start.1 = (f32[64,512]{1,0:T(8,128)S(1)}, f32[64,512]{1,0:T(8,128)}, u32[]{:S(2)}) copy-start(f32[64,512]{1,0:T(8,128)} %refs_3_.1) | copy-start | bytes 393220
  21.5 9.0 %copy-start = (f32[2048,256]{1,0:T(8,128)S(1)}, f32[2048,256]{1,0:T(8,128)}, u32[]{:S(2)}) copy-start(f32[2048,256]{1,0:T(8,128)} %refs_0_.1) | copy-start | bytes 6291460
  30.6 2.8 %copy-start.3 = (f32[512,256]{1,0:T(8,128)S(1)}, f32[512,256]{1,0:T(8,128)}, u32[]{:S(2)}) copy-start(f32[512,256]{1,0:T(8,128)} %get-tuple-element.34) | copy-start | bytes 1572868
  56.7 20.6 %collective-permute-start.4 = (f32[512,512]{1,0:T(8,128)}, f32[512,512]{1,0:T(8,128)S(1)}, u32[]{:S(2)}, u32[]{:S(2)}) collective-permute-start(f32[512,512]{1,0:T(8,128)} %get-tuple-element.44.c_own), channel_id=1, source_target_pairs={{0,1},{1,0},{2,3},{3,2},{4,5},{5,4},{6,7},{7,6},{8,9},{9,8},{10,11... | collective-permute-start | bytes 3145736 | tf_op jit(solution)/shard_map/ppermute | solution.py:319
  57.2 20.2 %collective-permute-start.5 = (f32[512,256]{1,0:T(8,128)}, f32[512,256]{1,0:T(8,128)S(1)}, u32[]{:S(2)}, u32[]{:S(2)}) collective-permute-start(f32[512,256]{1,0:T(8,128)} %get-tuple-element.46), channel_id=1, source_target_pairs={{0,1},{1,0},{2,3},{3,2},{4,5},{5,4},{6,7},{7,6},{8,9},{9,8},{10,11... | collective-permute-start | bytes 1572872 | tf_op jit(solution)/shard_map/ppermute | solution.py:319
  57.3 20.1 %collective-permute-start.6 = (f32[128,512]{1,0:T(8,128)}, f32[128,512]{1,0:T(8,128)S(1)}, u32[]{:S(2)}, u32[]{:S(2)}) collective-permute-start(f32[128,512]{1,0:T(8,128)} %get-tuple-element.47.hz_own), channel_id=1, source_target_pairs={{0,1},{1,0},{2,3},{3,2},{4,5},{5,4},{6,7},{7,6},{8,9},{9,8},{10,11... | collective-permute-start | bytes 786440 | tf_op jit(solution)/shard_map/ppermute | solution.py:319
  77.3 0.7 copy-start.6
  77.3 0.9 copy-start.5
  77.4 1.2 copy-start.4
  86.4 33.4 %copy-start.2 = (f32[512,256]{1,0:T(8,128)S(1)}, f32[512,256]{1,0:T(8,128)}, u32[]{:S(2)}) copy-start(f32[512,256]{1,0:T(8,128)} %get-tuple-element.50) | copy-start | bytes 1572868
  86.4 10.9 %collective-permute-start.9 = (f32[64,512]{1,0:T(8,128)}, f32[64,512]{1,0:T(8,128)S(1)}, u32[]{:S(2)}, u32[]{:S(2)}) collective-permute-start(f32[64,512]{1,0:T(8,128)} %get-tuple-element.54), channel_id=1, source_target_pairs={{0,2},{2,4},{4,6},{6,8},{8,10},{10,12},{12,14},{14,16},{16,18},{18... | collective-permute-start | bytes 393224 | tf_op jit(solution)/shard_map/ppermute | solution.py:338
  86.5 12.4 %collective-permute-start.10 = (f32[64,512]{1,0:T(8,128)}, f32[64,512]{1,0:T(8,128)S(1)}, u32[]{:S(2)}, u32[]{:S(2)}) collective-permute-start(f32[64,512]{1,0:T(8,128)} %get-tuple-element.56), channel_id=1, source_target_pairs={{0,1},{1,0},{2,3},{3,2},{4,5},{5,4},{6,7},{7,6},{8,9},{9,8},{10,11... | collective-permute-start | bytes 393224 | tf_op jit(solution)/shard_map/ppermute | solution.py:319
  86.9 21.6 %collective-permute-start.8 = (f32[512,256]{1,0:T(8,128)}, f32[512,256]{1,0:T(8,128)S(1)}, u32[]{:S(2)}, u32[]{:S(2)}) collective-permute-start(f32[512,256]{1,0:T(8,128)} %get-tuple-element.52), channel_id=1, source_target_pairs={{0,2},{2,4},{4,6},{6,8},{8,10},{10,12},{12,14},{14,16},{16,18},{18... | collective-permute-start | bytes 1572872 | tf_op jit(solution)/shard_map/ppermute | solution.py:338
  87.7 32.1 %collective-permute-start.7 = (f32[512,256]{1,0:T(8,128)}, f32[512,256]{1,0:T(8,128)S(1)}, u32[]{:S(2)}, u32[]{:S(2)}) collective-permute-start(f32[512,256]{1,0:T(8,128)} %get-tuple-element.51), channel_id=1, source_target_pairs={{0,2},{2,4},{4,6},{6,8},{8,10},{10,12},{12,14},{14,16},{16,18},{18... | collective-permute-start | bytes 1572872 | tf_op jit(solution)/shard_map/ppermute | solution.py:338

commit v2 on v0

v2 whole, which is shorter than its diff:
```python
import functools

import jax
import jax.numpy as jnp
from jax import lax
from jax.experimental import pallas as pl
from jax.experimental.pallas import tpu as pltpu
from jax.sharding import PartitionSpec as P

f32, bf16 = jnp.float32, jnp.bfloat16
N = 512
HALF = 256
RHS = 128
SHARE = 64
LOWEST = 2.0
TOL = 2e-6
MAX_STEPS = 40
VMEM = pl.BlockSpec(memory_space=pltpu.VMEM)
ANY = pl.BlockSpec(memory_space=pl.ANY)
MESH = pl.DeviceIdType.MESH
NN = (((1,), (0,)), ((), ()))
NT = (((1,), (1,)), ((), ()))


def split(x):
    high = x.astype(bf16)
    return high, (x - high.astype(f32)).astype(bf16)


def mul(a, b, dims=NN):
    one = lambda p, q: lax.dot_general(p, q, dims, preferred_element_type=f32)
    return one(a[0], b[0]) + (one(a[0], b[1]) + one(a[1], b[0]))


def identity(n):
    return (
        lax.broadcasted_iota(jnp.int32, (n, n), 0) == lax.broadcasted_iota(jnp.int32, (n, n), 1)
    ).astype(f32)


def newton(block, x_ref, d_ref):
    n = block.shape[0]
    d_ref[0], d_ref[1] = split(block)
    top = jnp.maximum(jnp.max(jnp.sum(jnp.abs(block), axis=0, keepdims=True)), LOWEST)
    eye = identity(n)
    gap = (top - LOWEST) / (top + LOWEST)
    lead = 2.0 / (top + LOWEST)
    gain = 2.0 / (2.0 - gap * gap)
    x_ref[...] = (gain * lead) * (2.0 * eye - lead * block)
    gap = 0.5 * gain * gap * gap

    def more(state):
        step, gap = state
        return jnp.logical_and(gap > TOL, step < MAX_STEPS)

    def body(state):
        step, gap = state
        x = x_ref[...]
        x_parts = split(x)
        rest = split(eye - mul((d_ref[0], d_ref[1]), x_parts))
        gain = 2.0 / (2.0 - gap * gap)
        x_ref[...] = gain * (x + mul(x_parts, rest))
        return step + 1, 0.5 * gain * gap * gap

    lax.while_loop(more, body, (jnp.int32(0), gap))
    return x_ref[...]


def places():
    core = lax.axis_index("rhs")
    return (
        core,
        pl.ds(pl.multiple_of(core * HALF, HALF), HALF),
        pl.ds(pl.multiple_of(HALF - core * HALF, HALF), HALF),
        pl.ds(pl.multiple_of(core * SHARE, SHARE), SHARE),
        pl.ds(pl.multiple_of(SHARE - core * SHARE, SHARE), SHARE),
    )


def invert(first_block, cross_block, last_block, out_ref, x_ref, d_ref):
    _, mine, other, _, _ = places()
    first = newton(first_block, x_ref, d_ref)
    cross = split(cross_block)
    lift = split(mul(cross, split(first)))
    out_ref[mine, mine] = first
    last = newton(last_block() - mul(lift, cross, NT), x_ref, d_ref)
    low = -mul(split(last), lift)
    up = low.T
    out_ref[other, other] = last
    out_ref[other, mine] = low
    out_ref[mine, other] = up
    out_ref[mine, mine] = out_ref[mine, mine] - mul(split(up), lift)


def loads(sems, *pairs):
    copies = [
        pltpu.make_async_copy(source, target, sems.at[index])
        for index, (source, target) in enumerate(pairs)
    ]
    for copy in copies:
        copy.start()
    return copies


def rows(first, second, count=N):
    core = lax.axis_index("rhs")
    return pl.ds(pl.multiple_of(first + core * (second - first), HALF), count)


def level_one(
    diag, lower, right_side, d_other, g_other, f_other,
    inverse_ref, v_ref, z_ref, send_ref, keep_ref, gz_ref,
    d_own, d_last, g_whole, g_ref, f_ref, x_ref, d_ref, sems,
):
    core, mine, other, share, rest = places()
    section = rows(N, 3 * N)
    copies = loads(
        sems,
        (diag.at[section], d_own),
        (d_other, d_last),
        (lower.at[rows(2 * N, 3 * N)], g_whole.at[:, mine]),
        (g_other, g_whole.at[:, other]),
        (right_side.at[:, section], f_ref.at[share]),
        (f_other, f_ref.at[rest]),
    )
    copies[0].wait()

    def last_block():
        copies[1].wait()
        return d_last[...]

    invert(d_own[mine], d_own[other], last_block, inverse_ref, x_ref, d_ref)
    for copy in copies[2:]:
        copy.wait()

    @pl.when(core == 0)
    def _():
        g_ref[...] = g_whole[...]

    @pl.when(core == 1)
    def _():
        g_ref[...] = g_whole[...].T

    inverse, g = split(inverse_ref[...]), split(g_ref[...])
    v = mul(inverse, g, NT)
    v_ref[...] = v
    g_whole[...] = mul(g, split(v))
    z = mul(split(f_ref[...]), inverse)
    z_ref[...] = z
    gz = mul(split(z), g, NT)
    gz_ref[...] = gz
    send_ref[:N] = g_whole[:, other]
    send_ref[N : N + HALF] = g_whole[mine, mine]
    send_ref[N + HALF : N + HALF + RHS] = gz[:, :HALF]
    send_ref[N + HALF + RHS :] = gz[:, HALF:]
    keep_ref[:N] = g_whole[:, mine]
    keep_ref[N:] = g_whole[other, other]


def outward(
    inverse_ref, v_ref, z_ref, lower, h_other, next_left, next_right,
    w_ref, send_ref, hw_ref, hz_ref,
    h_whole, h_ref, sems,
):
    core, mine, other, share, rest = places()

    @pl.when(core == 0)
    def _():
        copies = loads(
            sems, (lower.at[N : 2 * N], h_whole.at[:, :HALF]), (h_other, h_whole.at[:, HALF:])
        )
        for copy in copies:
            copy.wait()
        h_ref[...] = h_whole[...].T

    @pl.when(core == 1)
    def _():
        copies = loads(sems, (next_left, h_ref.at[:, :HALF]), (next_right, h_ref.at[:, HALF:]))
        for copy in copies:
            copy.wait()

    h = split(h_ref[...])
    c = -mul(h, split(v_ref[...]))
    send_ref[:N] = c[:, :HALF]
    send_ref[N : 2 * N] = c[:, HALF:]
    w = mul(split(inverse_ref[...]), h, NT)
    w_ref[...] = w
    h_whole[...] = mul(h, split(w))
    hw_ref[...] = h_whole[:, mine]
    send_ref[2 * N : 3 * N] = h_whole[:, other]
    h_ref[:RHS] = mul(split(z_ref[...]), h, NT)
    hz_ref[...] = h_ref[share]
    send_ref[3 * N : 3 * N + SHARE] = h_ref[rest, :HALF]
    send_ref[3 * N + SHARE :] = h_ref[rest, HALF:]


def level_two(
    diag, right_side, d_other, f_other, keep_ref, came_ref, gz_ref,
    inverse_ref, z_ref,
    d_own, f_ref, x_ref, d_ref, sems,
):
    core, mine, other, share, rest = places()
    copies = loads(
        sems,
        (diag.at[2 * N : 3 * N], d_own),
        (right_side.at[:, 2 * N : 3 * N], f_ref.at[share]),
    )
    copies[0].wait()
    d_own[...] = d_own[...] - (keep_ref[:N] + came_ref[:N])
    last_block = lambda: d_other[...] - (keep_ref[N:] + came_ref[N : N + HALF])
    invert(d_own[mine], d_own[other], last_block, inverse_ref, x_ref, d_ref)
    copies[1].wait()
    f_ref[rest] = f_other[...]
    start = N + HALF
    f_ref[:, :HALF] = f_ref[:, :HALF] - (gz_ref[:, :HALF] + came_ref[start : start + RHS])
    f_ref[:, HALF:] = f_ref[:, HALF:] - (gz_ref[:, HALF:] + came_ref[start + RHS :])
    z_ref[...] = mul(split(f_ref[...]), split(inverse_ref[...]))


def survivors(
    inverse_ref, z2_ref, own_ref, came_ref, hw_ref, hz_ref,
    diag, right_side, coarse_sol, v_any, w_any, z_any,
    diag_ref, low_out, rhs_ref, solution_ref,
    c_both, hw_both, hz_both, low_send, diag_send, rhs_send, diag_came, rhs_came,
    d0, f0, y_ref, v_ref, w_ref, z_ref, y_next, y_send, ys_ref, x2_ref, x_ref, x_both,
    sems, send_sems, recv_sems,
):
    core, mine, other, share, rest = places()
    me = lax.axis_index("tm")
    runs = lax.axis_size("tm")
    after, before = {"tm": lax.rem(me + 1, runs)}, {"tm": lax.rem(me + runs - 1, runs)}
    partner = {"rhs": 1 - core}
    barrier = pltpu.get_barrier_semaphore()
    for device in (after, before, partner):
        pl.semaphore_signal(barrier, inc=1, device_id=device, device_id_type=MESH)
    copies = loads(
        sems,
        (diag.at[:N], d0),
        (right_side.at[:, :N], f0),
        (coarse_sol, y_ref),
        (v_any, v_ref),
        (w_any, w_ref),
        (z_any, z_ref),
    )
    pl.semaphore_wait(barrier, 3)
    sent = []

    def send(source, target, device):
        copy = pltpu.make_async_remote_copy(
            src_ref=source,
            dst_ref=target,
            send_sem=send_sems.at[len(sent)],
            recv_sem=recv_sems.at[len(sent)],
            device_id=device,
            device_id_type=MESH,
        )
        copy.start()
        sent.append(copy)
        return copy

    later = send(coarse_sol, y_next, before)
    for column in range(2):
        span = slice(column * HALF, (column + 1) * HALF)
        c_both[core, :, span] = own_ref[column * N : (column + 1) * N]
        c_both[1 - core, :, span] = came_ref[column * N : (column + 1) * N]
        hz_both[1 - core, :, span] = came_ref[
            3 * N + column * SHARE : 3 * N + (column + 1) * SHARE
        ]
    hw_both[core] = hw_ref[...]
    hw_both[1 - core] = came_ref[2 * N : 3 * N]
    hz_both[core] = hz_ref[...]

    inverse = split(inverse_ref[...])
    right = split(c_both[1])
    u_right = split(mul(inverse, split(c_both[1, mine]), NT))
    arrivals = []
    for half in range(2):
        span = slice(half * HALF, (half + 1) * HALF)
        diag_send[span] = hw_both[1, span] + mul((right[0][span], right[1][span]), u_right)
        arrivals.append(send(diag_send.at[span], diag_came.at[span], after))
    z2 = split(z2_ref[share])
    rhs_send[...] = hz_both[1] + mul(z2, right, NT)
    arrivals.append(send(rhs_send, rhs_came, after))
    left = split(c_both[0])
    u_left = split(mul(inverse, split(c_both[0, mine]), NT))
    lows = []
    for half in range(2):
        span = slice(half * HALF, (half + 1) * HALF)
        low_send[span] = -mul((right[0][span], right[1][span]), u_left)
        lows.append(send(low_send.at[span], low_out.at[span], after))

    for copy in copies[:3]:
        copy.wait()
    diag_ref[...] = d0[...] - hw_both[0] - mul(left, u_left)
    rhs_ref[...] = f0[...] - hz_both[0] - mul(z2, left, NT)

    later.wait_recv()

    @pl.when(core == 0)
    def _():
        y_send[...] = y_next[...]
        ys_ref[0] = y_ref[...]

    @pl.when(core == 1)
    def _():
        y_send[...] = y_ref[...]
        ys_ref[0] = y_next[...]

    swap_y = send(y_send, ys_ref.at[1], partner)
    known = mul(split(y_ref[...]), left) + mul(split(y_next[...]), right)
    x2_ref[0] = z2_ref[share] - mul(split(known), inverse)
    swap_x2 = send(x2_ref.at[0], x2_ref.at[1], partner)
    for copy in copies[3:]:
        copy.wait()
    swap_y.wait_recv()
    swap_x2.wait_recv()
    v, w = split(v_ref[...]), split(w_ref[...])
    for slot, place in ((1, rest), (0, share)):
        x_ref[slot] = (
            z_ref[place]
            - mul(split(ys_ref[slot]), w, NT)
            - mul(split(x2_ref[slot]), v, NT)
        )
        if slot == 1:
            swap_x = send(x_ref.at[1], x_both.at[core], partner)
    solution_ref[:, :N] = y_ref[...]
    solution_ref[:, 2 * N : 3 * N] = x2_ref[0]
    swap_x.wait_recv()

    @pl.when(core == 0)
    def _():
        solution_ref[:, N : 2 * N] = x_ref[0]
        solution_ref[:, 3 * N :] = x_both[1]

    @pl.when(core == 1)
    def _():
        solution_ref[:, N : 2 * N] = x_both[0]
        solution_ref[:, 3 * N :] = x_ref[0]

    for half in range(2):
        span = slice(half * HALF, (half + 1) * HALF)
        arrivals[half].wait_recv()
        diag_ref[span] = diag_ref[span] - diag_came[span]
    arrivals[2].wait_recv()
    rhs_ref[...] = rhs_ref[...] - rhs_came[...]
    for copy in lows:
        copy.wait_recv()
    for copy in sent:
        copy.wait_send()


def partners_body(
    diag, lower, right_side,
    d_ref, g_ref, f_ref, h_ref, d2_ref, f2_ref,
    send_sems, recv_sems,
):
    core = lax.axis_index("rhs")
    partner = {"rhs": 1 - core}
    barrier = pltpu.get_barrier_semaphore()
    pl.semaphore_signal(barrier, inc=1, device_id=partner, device_id_type=MESH)
    pl.semaphore_wait(barrier, 1)
    section = rows(3 * N, N)
    windows = (
        (diag.at[rows(3 * N, N + HALF, HALF)], d_ref),
        (lower.at[rows(3 * N, 2 * N)], g_ref),
        (right_side.at[:, section], f_ref),
        (diag.at[rows(2 * N, 2 * N + HALF, HALF)], d2_ref),
        (right_side.at[:, 2 * N : 3 * N], f2_ref),
        (lower.at[N : 2 * N], h_ref),
    )
    copies = [
        pltpu.make_async_remote_copy(
            src_ref=source,
            dst_ref=target,
            send_sem=send_sems.at[index],
            recv_sem=recv_sems.at[index],
            device_id=partner,
            device_id_type=MESH,
        )
        for index, (source, target) in enumerate(windows)
    ]
    for copy in copies:
        copy.start()
    for copy in copies:
        copy.wait()


def shape(*dims):
    return jax.ShapeDtypeStruct(dims, f32)


def call(body, in_specs, outs, out_specs, scratch, flops, args, limit, **params):
    size = sum(a.size for a in args) + sum(o.size for o in outs)
    return pl.pallas_call(
        body,
        out_shape=outs,
        in_specs=in_specs,
        out_specs=out_specs,
        scratch_shapes=scratch,
        compiler_params=pltpu.CompilerParams(vmem_limit_bytes=limit << 20, **params),
        cost_estimate=pl.CostEstimate(flops=flops, bytes_accessed=4 * size, transcendentals=0),
    )(*args)


def newton_scratch():
    return [pltpu.VMEM((HALF, HALF), f32), pltpu.VMEM((2, HALF, HALF), bf16)]


def copy_sems(count):
    return pltpu.SemaphoreType.DMA((count,))


def shards(diag, lower, right_side, coarse_sol):
    runs = lax.axis_size("tm")
    next_left, next_right = (
        lax.ppermute(
            lower[:N],
            ("tm", "rhs"),
            [(2 * ((i + 1) % runs) + source, 2 * i + 1) for i in range(runs)],
        )
        for source in (0, 1)
    )
    swap = lambda x: lax.ppermute(x, "rhs", [(0, 1), (1, 0)])
    d_other, g_other, f_other, d2_other, f2_other, h_other = (
        lambda d, g, f, h, d2, f2: (d, g, f, d2, f2, h)
    )(
        *call(
            partners_body,
            [ANY] * 3,
            [shape(HALF, HALF), shape(N, HALF), shape(SHARE, N), shape(N, HALF),
             shape(HALF, HALF), shape(SHARE, N)],
            [ANY] * 6,
            [copy_sems(6), copy_sems(6)],
            0,
            (diag, lower, right_side),
            8,
            collective_id=1,
            has_side_effects=True,
        )
    )
    inverse, v, z, send, keep, gz = call(
        level_one,
        [ANY] * 6,
        [shape(N, N), shape(N, N), shape(RHS, N), shape(2 * N, HALF), shape(N + HALF, HALF),
         shape(RHS, N)],
        [VMEM] * 6,
        [pltpu.VMEM((N, HALF), f32), pltpu.VMEM((HALF, HALF), f32), pltpu.VMEM((N, N), f32),
         pltpu.VMEM((N, N), f32), pltpu.VMEM((RHS, N), f32)] + newton_scratch() + [copy_sems(6)],
        2 * N**3 * 20,
        (diag, lower, right_side, d_other, g_other, f_other),
        28,
    )
    came = swap(send)
    w, pack, hw, hz = call(
        outward,
        [VMEM] * 3 + [ANY] * 4,
        [shape(N, N), shape(3 * N + RHS, HALF), shape(N, HALF), shape(SHARE, N)],
        [VMEM] * 4,
        [pltpu.VMEM((N, N), f32), pltpu.VMEM((N, N), f32), copy_sems(2)],
        2 * N**3 * 10,
        (inverse, v, z, lower, h_other, next_left, next_right),
        28,
    )
    pack_came = swap(pack)
    inverse2, z2 = call(
        level_two,
        [ANY] * 2 + [VMEM] * 5,
        [shape(N, N), shape(RHS, N)],
        [VMEM] * 2,
        [pltpu.VMEM((N, HALF), f32), pltpu.VMEM((RHS, N), f32)]
        + newton_scratch() + [copy_sems(2)],
        2 * N**3 * 20,
        (diag, right_side, d2_other, f2_other, keep, came, gz),
        28,
    )
    small = pltpu.VMEM((SHARE, N), f32)
    small_pair = pltpu.VMEM((2, SHARE, N), f32)
    half = pltpu.VMEM((N, HALF), f32)
    full = pltpu.VMEM((N, N), f32)
    return call(
        survivors,
        [VMEM] * 6 + [ANY] * 6,
        [shape(N, HALF), shape(N, HALF), shape(SHARE, N), shape(SHARE, 4 * N)],
        [VMEM, ANY, VMEM, VMEM],
        [pltpu.VMEM((2, N, N), f32), pltpu.VMEM((2, N, HALF), f32), small_pair,
         half, half, small, half, small,
         half, small, small, full, full, pltpu.VMEM((RHS, N), f32), small, small, small_pair,
         small_pair, small_pair, small_pair,
         copy_sems(6), copy_sems(9), copy_sems(9)],
        2 * N**3 * 9,
        (inverse2, z2, pack, pack_came, hw, hz, diag, right_side, coarse_sol, v, w, z),
        40,
        collective_id=2,
        has_side_effects=True,
    )


def solution(mesh):
    return jax.shard_map(
        shards,
        mesh=mesh,
        in_specs=(P("tm", "rhs"), P("tm", "rhs"), P("rhs", "tm"), P("rhs", "tm")),
        out_specs=(P("tm", "rhs"), P("tm", "rhs"), P("rhs", "tm"), P("rhs", "tm")),
        check_vma=False,
    )
```

time: 688 us -> 97 us (0.14); the launches traced: 676 us -> 96.8 us
  other arithmetic: 393 us -> 0 us
  matrix products: 97.5 us -> 0 us
  waiting for transfers between devices: 74.5 us -> 4.63 us
  Pallas kernels: 0 us -> 68.1 us
  local copies, waits for them, and re-layouts: 71.2 us -> 8.41 us
  between operations: 23.6 us -> 0.77 us
    another operation x53 -> x0, other arithmetic: 385 us -> none  [the longest x43 262 us: eliminate_one(): factor = jnp.linalg.cholesky(diag_block)]
    pallas_call x0 -> x5, Pallas kernels: none -> 68.1 us  [call(): pl.pallas_call(body, out_shape=outs, in_specs=in_specs, out_specs=out_spe...]
    another operation x102 -> x0, matrix products: 49.3 us -> none  [the longest x42 17.2 us: apply_inverse(): lax.linalg.triangular_solve(factor, halfway, left_side=True, lower=True,...]
    dot_general x21 -> x0, matrix products: 48.2 us -> none  [product(): jnp.dot(first_term, second_term, precision=lax.Precision.HIGHEST, preferr...]
    ppermute x9 -> x4, waiting for transfers between devices: 48.3 us -> 4.63 us  [the longest x2 4.63 us: shards(): swap = lambda x: lax.ppermute(x, 'rhs', [(0, 1), (1, 0)])]
    another operation x52 -> x0, local copies, waits for them, and re-layouts: 30.1 us -> none  [the longest x40 26.8 us: apply_inverse(): lax.linalg.triangular_solve(factor, halfway, left_side=True, lower=True,...]
    all_gather x7 -> x0, waiting for transfers between devices: 26.1 us -> none  [the longest x1 20.3 us: shards(): lax.all_gather(diag, 'rhs', axis=1, tiled=True)]
    unnamed x96 -> x18, local copies, waits for them, and re-layouts: 18.5 us -> 7.27 us
  transfers between devices with their start and end apart: 16 -> 4, of which waited for: 6 -> 1; matrix products, arithmetic and copies ran while one was open for 57% -> 0% of each run, Pallas kernels for 0% -> 31%
where the time goes in v2:
time: 97 us; the launch traced here: 96.8 us
  Pallas kernels  68.1 us (70%)
  starting transfers between devices  14.8 us (15%)
  local copies, waits for them, and re-layouts  8.41 us (9%)
  waiting for transfers between devices  4.63 us (5%)
    pallas_call x5, Pallas kernels, call(): pl.pallas_call(body, out_shape=outs, in_specs=in_specs, out_specs=out_spe...  68.1 us
    ppermute x2, starting transfers between devices, shards(): lax.ppermute(lower[:N], ('tm', 'rhs'), [(2 * ((i + 1) % runs) + source, 2...  14.2 us
    unnamed x18, local copies, waits for them, and re-layouts  7.27 us
    ppermute x2, waiting for transfers between devices, shards(): swap = lambda x: lax.ppermute(x, 'rhs', [(0, 1), (1, 0)])  4.63 us
  transfers between devices with their start and end apart: 4, of which 1 were waited for; matrix products, arithmetic and copies ran while one was open for 0% of the time, Pallas kernels for 31%

profile of v2, /device:TPU:1, one launch (start us, length us, event | category | flops | bytes accessed | tf_op | source)
XLA Modules:
  0.0 96.8 jit_solution(11524647261273047607)
XLA Ops:
  0.6 0.0 copy-start.5
  0.6 1.1 %slice.4 = f32[512,256]{1,0:T(8,128)S(1)} slice(f32[2048,256]{1,0:T(8,128)} %lower.5), slice={[0:512], [0:256]} | slice | bytes 1048576 | tf_op jit(solution)/shard_map/slice | solution.py:417
  1.8 12.9 %collective-permute-start.2 = (f32[512,256]{1,0:T(8,128)S(1)}, f32[512,256]{1,0:T(8,128)S(1)}, u32[]{:S(2)}, u32[]{:S(2)}) collective-permute-start(f32[512,256]{1,0:T(8,128)S(1)} %slice.4), channel_id=1, source_target_pairs={{3,1},{5,3},{7,5},{9,7},{11,9},{13,11},{15,13},{17,15},{19,17},{21... | collective-permute-start | bytes 1572872 | tf_op jit(solution)/shard_map/ppermute | solution.py:416
  14.7 1.3 %collective-permute-start.1 = (f32[512,256]{1,0:T(8,128)S(1)}, f32[512,256]{1,0:T(8,128)S(1)}, u32[]{:S(2)}, u32[]{:S(2)}) collective-permute-start(f32[512,256]{1,0:T(8,128)S(1)} %slice.4), channel_id=1, source_target_pairs={{2,1},{4,3},{6,5},{8,7},{10,9},{12,11},{14,13},{16,15},{18,17},{20... | collective-permute-start | bytes 1572872 | tf_op jit(solution)/shard_map/ppermute | solution.py:416
  16.0 0.0 copy-start
  16.0 1.6 %copy-done = f32[2048,256]{1,0:T(8,128)S(1)} copy-done((f32[2048,256]{1,0:T(8,128)S(1)}, f32[2048,256]{1,0:T(8,128)}, u32[]{:S(2)}) %copy-start) | copy-done | bytes 2097176
  17.6 0.0 copy-start.2
  17.6 1.6 %copy-done.2 = f32[2048,256]{1,0:T(8,128)S(1)} copy-done((f32[2048,256]{1,0:T(8,128)S(1)}, f32[2048,256]{1,0:T(8,128)}, u32[]{:S(2)}) %copy-start.2) | copy-done | bytes 2097176
  19.2 0.0 copy-start.4
  19.2 1.0 %copy-done.4 = f32[64,2048]{1,0:T(8,128)S(1)} copy-done((f32[64,2048]{1,0:T(8,128)S(1)}, f32[64,2048]{1,0:T(8,128)}, u32[]{:S(2)}) %copy-start.4) | copy-done | bytes 524312
  20.3 0.0 copy-start.1
  20.3 0.0 copy-start.3
  20.3 5.1 %shard_map.75 = (f32[256,256]{1,0:T(8,128)S(1)}, f32[512,256]{1,0:T(8,128)S(1)}, f32[64,512]{1,0:T(8,128)S(1)}, f32[512,256]{1,0:T(8,128)S(1)}, f32[256,256]{1,0:T(8,128)S(1)}, /*index=5*/f32[64,512]{1,0:T(8,128)S(1)}) custom-call(f32[2048,256]{1,0:T(8,128)S(1)} %copy-done, f32[2048,256]{1,0:T(8,128)S(1)} %copy-done.2, f32[64,2048]{1,0:T(8,128)S(1)} %copy-done.4), custom_call_target="tpu_custom_call" | custom-call | bytes 6553600 | tf_op jit(solution)/shard_map/pallas_call | solution.py:394
  25.4 0.0 copy-done.5
  25.4 0.0 copy-done.1
  25.4 0.0 copy-done.3
  25.4 13.9 %shard_map.76 = (f32[512,512]{1,0:T(8,128)S(1)}, f32[512,512]{1,0:T(8,128)S(1)}, f32[128,512]{1,0:T(8,128)S(1)}, f32[1024,256]{1,0:T(8,128)S(1)}, f32[768,256]{1,0:T(8,128)S(1)}, /*index=5*/f32[128,512]{1,0:T(8,128)S(1)}) custom-call(f32[2048,256]{1,0:T(8,128)S(1)} %copy-done.1, f32[2048,256]{1,0:T(8,128)S(1)} %copy-done.3, f32[64,2048]{1,0:T(8,128)S(1)} %copy-done.5, ...), custom_call_target="tpu_custom_call" | custom-call | flops 5368709120 | bytes 10092544 | tf_op jit(solution)/shard_map/pallas_call | solution.py:394
  39.4 0.0 collective-permute-done.2.next_right
  39.4 0.0 collective-permute-done.1.next_left
  39.4 3.6 %shard_map.78 = (f32[512,512]{1,0:T(8,128)S(1)}, f32[1664,256]{1,0:T(8,128)S(1)}, f32[512,256]{1,0:T(8,128)S(1)}, f32[64,512]{1,0:T(8,128)S(1)}) custom-call(f32[512,512]{1,0:T(8,128)S(1)} %get-tuple-element.32.inverse_ref, f32[512,512]{1,0:T(8,128)S(1)} %get-tuple-element.33.v_ref.v_any, f32[128,512]{1,0:T(8,128)S(1)} %get-tuple-element.34.z_ref.z_any, ...), custom_call_target="tpu_custom_call" | custom-call | flops 2684354560 | bytes 9437184 | tf_op jit(solution)/shard_map/pallas_call | solution.py:394
  42.9 0.5 collective-permute-start.3
  43.4 0.1 collective-permute-start
  43.5 4.6 %collective-permute-done.came_ref = f32[1024,256]{1,0:T(8,128)S(1)} collective-permute-done((f32[1024,256]{1,0:T(8,128)S(1)}, f32[1024,256]{1,0:T(8,128)S(1)}, u32[]{:S(2)}, u32[]{:S(2)}) %collective-permute-start) | collective-permute-done | bytes 1048608 | tf_op jit(solution)/shard_map/ppermute | solution.py:423
  48.2 0.0 copy-start.6
  48.2 10.9 %shard_map.77 = (f32[512,512]{1,0:T(8,128)S(1)}, f32[128,512]{1,0:T(8,128)S(1)}) custom-call(f32[2048,256]{1,0:T(8,128)S(1)} %copy-done.1, f32[64,2048]{1,0:T(8,128)S(1)} %copy-done.5, f32[256,256]{1,0:T(8,128)S(1)} %get-tuple-element.22.d_other, f32[64,512]{1,0:T(8,128)S(1)} %get-tuple-element.23.f_other, f32[768,256]{1,0:T(8,128)S(1)} %get-tuple-element.27.keep_ref, ...), custom_call_target="tpu_custom_call" | custom-call | flops 5368709120 | bytes 6422528 | tf_op jit(solution)/shard_map/pallas_call | solution.py:394
  59.1 0.0 collective-permute-done.3.came_ref
  59.1 0.0 copy-done.6
  59.1 34.7 %shard_map.79 = (f32[512,256]{1,0:T(8,128)S(1)}, f32[512,256]{1,0:T(8,128)S(1)}, f32[64,512]{1,0:T(8,128)S(1)}, f32[64,2048]{1,0:T(8,128)S(1)}) custom-call(f32[512,512]{1,0:T(8,128)S(1)} %get-tuple-element.30.inverse_ref, f32[128,512]{1,0:T(8,128)S(1)} %get-tuple-element.31.z2_ref, f32[1664,256]{1,0:T(8,128)S(1)} %get-tuple-element.36.own_ref, ...), custom_call_target="tpu_custom_call" | custom-call | flops 2415919104 | bytes 12189696 | tf_op jit(solution)/shard_map/pallas_call | solution.py:394
  93.8 0.8 copy.12
  94.6 0.8 copy.13
  95.3 0.7 copy.14
  96.0 0.8 copy.15
Async XLA Ops:
  0.6 24.8 %copy-start.5 = (f32[64,2048]{1,0:T(8,128)S(1)}, f32[64,2048]{1,0:T(8,128)}, u32[]{:S(2)}) copy-start(f32[64,2048]{1,0:T(8,128)} %right_side.7) | copy-start | bytes 1572868
  1.8 37.6 %collective-permute-start.2 = (f32[512,256]{1,0:T(8,128)S(1)}, f32[512,256]{1,0:T(8,128)S(1)}, u32[]{:S(2)}, u32[]{:S(2)}) collective-permute-start(f32[512,256]{1,0:T(8,128)S(1)} %slice.4), channel_id=1, source_target_pairs={{3,1},{5,3},{7,5},{9,7},{11,9},{13,11},{15,13},{17,15},{19,17},{21... | collective-permute-start | bytes 1572872 | tf_op jit(solution)/shard_map/ppermute | solution.py:416
  14.7 24.6 %collective-permute-start.1 = (f32[512,256]{1,0:T(8,128)S(1)}, f32[512,256]{1,0:T(8,128)S(1)}, u32[]{:S(2)}, u32[]{:S(2)}) collective-permute-start(f32[512,256]{1,0:T(8,128)S(1)} %slice.4), channel_id=1, source_target_pairs={{2,1},{4,3},{6,5},{8,7},{10,9},{12,11},{14,13},{16,15},{18,17},{20... | collective-permute-start | bytes 1572872 | tf_op jit(solution)/shard_map/ppermute | solution.py:416
  16.0 1.6 %copy-start = (f32[2048,256]{1,0:T(8,128)S(1)}, f32[2048,256]{1,0:T(8,128)}, u32[]{:S(2)}) copy-start(f32[2048,256]{1,0:T(8,128)} %diag.7) | copy-start | bytes 6291460
  17.6 1.6 %copy-start.2 = (f32[2048,256]{1,0:T(8,128)S(1)}, f32[2048,256]{1,0:T(8,128)}, u32[]{:S(2)}) copy-start(f32[2048,256]{1,0:T(8,128)} %lower.5) | copy-start | bytes 6291460
  19.2 1.0 %copy-start.4 = (f32[64,2048]{1,0:T(8,128)S(1)}, f32[64,2048]{1,0:T(8,128)}, u32[]{:S(2)}) copy-start(f32[64,2048]{1,0:T(8,128)} %right_side.7) | copy-start | bytes 1572868
  20.3 5.1 %copy-start.1 = (f32[2048,256]{1,0:T(8,128)S(1)}, f32[2048,256]{1,0:T(8,128)}, u32[]{:S(2)}) copy-start(f32[2048,256]{1,0:T(8,128)} %diag.7) | copy-start | bytes 6291460
  20.3 5.1 %copy-start.3 = (f32[2048,256]{1,0:T(8,128)S(1)}, f32[2048,256]{1,0:T(8,128)}, u32[]{:S(2)}) copy-start(f32[2048,256]{1,0:T(8,128)} %lower.5) | copy-start | bytes 6291460
  42.9 16.1 %collective-permute-start.3 = (f32[1664,256]{1,0:T(8,128)S(1)}, f32[1664,256]{1,0:T(8,128)S(1)}, u32[]{:S(2)}, u32[]{:S(2)}) collective-permute-start(f32[1664,256]{1,0:T(8,128)S(1)} %get-tuple-element.36.own_ref), channel_id=1, source_target_pairs={{0,1},{1,0},{2,3},{3,2},{4,5},{5,4},{6,7},{7,6},{8,9},{9,8},{10,11... | collective-permute-start | bytes 5111816 | tf_op jit(solution)/shard_map/ppermute | solution.py:423
  43.4 4.7 %collective-permute-start = (f32[1024,256]{1,0:T(8,128)S(1)}, f32[1024,256]{1,0:T(8,128)S(1)}, u32[]{:S(2)}, u32[]{:S(2)}) collective-permute-start(f32[1024,256]{1,0:T(8,128)S(1)} %get-tuple-element.28), channel_id=1, source_target_pairs={{0,1},{1,0},{2,3},{3,2},{4,5},{5,4},{6,7},{7,6},{8,9},{9,8},{10,11... | collective-permute-start | bytes 3145736 | tf_op jit(solution)/shard_map/ppermute | solution.py:423
  48.2 10.9 %copy-start.6 = (f32[64,512]{1,0:T(8,128)S(1)}, f32[64,512]{1,0:T(8,128)}, u32[]{:S(2)}) copy-start(f32[64,512]{1,0:T(8,128)} %coarse_sol.1) | copy-start | bytes 393220

commit v3 on v2

v3 whole, which is shorter than its diff:
```python
import functools

import jax
import jax.numpy as jnp
from jax import lax
from jax.experimental import pallas as pl
from jax.experimental.pallas import tpu as pltpu
from jax.sharding import PartitionSpec as P

f32, bf16 = jnp.float32, jnp.bfloat16
N = 512
HALF = 256
RHS = 128
SHARE = 64
LOWEST = 2.0
TOL = 4e-6
COARSE_TOL = 1.6e-3
NOISE = 2e-6
FIXED_STEPS = 4
MAX_STEPS = 40
VMEM = pl.BlockSpec(memory_space=pltpu.VMEM)
ANY = pl.BlockSpec(memory_space=pl.ANY)
HBM = pl.BlockSpec(memory_space=pltpu.HBM)
MESH = pl.DeviceIdType.MESH
NN = (((1,), (0,)), ((), ()))
NT = (((1,), (1,)), ((), ()))


def split(x):
    high = x.astype(bf16)
    return high, (x - high.astype(f32)).astype(bf16)


def mul(a, b, dims=NN):
    one = lambda p, q: lax.dot_general(p, q, dims, preferred_element_type=f32)
    return one(a[0], b[0]) + (one(a[0], b[1]) + one(a[1], b[0]))


def identity(n):
    return (
        lax.broadcasted_iota(jnp.int32, (n, n), 0) == lax.broadcasted_iota(jnp.int32, (n, n), 1)
    ).astype(f32)


def norm_steps(gap):
    gain = 2.0 / (2.0 - gap * gap)
    return gain, 0.5 * gain * gap * gap


def newton_start(block, x_ref, t_ref, d_ref):
    d_ref[0], d_ref[1] = split(block)
    top = jnp.maximum(jnp.max(jnp.sum(jnp.abs(block), axis=0, keepdims=True)), LOWEST)
    lead = 2.0 / (top + LOWEST)
    gain, gap = norm_steps((top - LOWEST) / (top + LOWEST))
    rest = 2.0 * identity(block.shape[0]) - lead * block
    x_ref[...] = (gain * lead) * rest
    t_ref[...] = (gain * lead) * mul((d_ref[0], d_ref[1]), split(rest))
    return gap


def newton_step(gap, x_ref, t_ref):
    gain, gap = norm_steps(gap)
    n = x_ref.shape[0]
    rest = split(2.0 * identity(n) - t_ref[...])
    both = mul(split(jnp.concatenate([t_ref[...], x_ref[...]], axis=0)), rest)
    t_ref[...] = gain * both[:n]
    x_ref[...] = gain * both[n:]
    return gap


def newton_finish(gap, x_ref, t_ref, d_ref, noise):
    def more(limit):
        return lambda state: jnp.logical_and(state[1] > limit, state[0] < MAX_STEPS)

    step = lambda state: (state[0] + 1, newton_step(state[1], x_ref, t_ref))
    _, gap = lax.while_loop(more(COARSE_TOL), step, (jnp.int32(0), gap))

    def correct(state):
        x = x_ref[...]
        x_parts = split(x)
        residual = split(identity(x.shape[0]) - mul((d_ref[0], d_ref[1]), x_parts))
        x_ref[...] = x + mul(x_parts, residual)
        return state[0] + 1, state[1] * state[1]

    lax.while_loop(more(TOL), correct, (jnp.int32(0), gap + noise))
    return x_ref[...]


def noise_of(block):
    return jnp.max(jnp.sum(jnp.abs(block), axis=0, keepdims=True)) * NOISE


def newton(block, x_ref, t_ref, d_ref):
    gap = newton_start(block, x_ref, t_ref, d_ref)
    return newton_finish(gap, x_ref, t_ref, d_ref, noise_of(block))


def places():
    core = lax.axis_index("rhs")
    return (
        core,
        pl.ds(pl.multiple_of(core * HALF, HALF), HALF),
        pl.ds(pl.multiple_of(HALF - core * HALF, HALF), HALF),
        pl.ds(pl.multiple_of(core * SHARE, SHARE), SHARE),
        pl.ds(pl.multiple_of(SHARE - core * SHARE, SHARE), SHARE),
    )


def invert(first, cross_block, last_block, out_ref, x_ref, t_ref, d_ref):
    _, mine, other, _, _ = places()
    cross = split(cross_block)
    lift = split(mul(cross, split(first)))
    out_ref[mine, mine] = first
    last = newton(last_block() - mul(lift, cross, NT), x_ref, t_ref, d_ref)
    low = -mul(split(last), lift)
    up = low.T
    out_ref[other, other] = last
    out_ref[other, mine] = low
    out_ref[mine, other] = up
    out_ref[mine, mine] = out_ref[mine, mine] - mul(split(up), lift)


def loads(sems, *pairs):
    copies = [
        pltpu.make_async_copy(source, target, sems.at[index])
        for index, (source, target) in enumerate(pairs)
    ]
    for copy in copies:
        copy.start()
    return copies


def rows(first, second, count=N):
    core = lax.axis_index("rhs")
    return pl.ds(pl.multiple_of(first + core * (second - first), HALF), count)


def remote(source, target, sems, index, device):
    copy = pltpu.make_async_remote_copy(
        src_ref=source,
        dst_ref=target,
        send_sem=sems[0].at[index],
        recv_sem=sems[1].at[index],
        device_id=device,
        device_id_type=MESH,
    )
    copy.start()
    return copy


def greet(*devices):
    barrier = pltpu.get_barrier_semaphore()
    for device in devices:
        pl.semaphore_signal(barrier, inc=1, device_id=device, device_id_type=MESH)
    return lambda: pl.semaphore_wait(barrier, len(devices))


def partners(
    diag, lower, right_side,
    d_other, g_other, f_other, h_other, d2_other, x_ref, t_ref, gap_ref,
    block_ref, d_ref, sems, send_sems, recv_sems,
):
    core = lax.axis_index("rhs")
    partner = {"rhs": 1 - core}
    arrived = greet(partner)
    mine = loads(sems, (diag.at[rows(N, 3 * N + HALF, HALF)], block_ref))
    arrived()
    pair = (send_sems, recv_sems)
    copies = [
        remote(source, target, pair, index, partner)
        for index, (source, target) in enumerate(
            (
                (diag.at[rows(3 * N, N + HALF, HALF)], d_other),
                (lower.at[rows(3 * N, 2 * N)], g_other),
                (right_side.at[:, rows(3 * N, N)], f_other),
                (diag.at[rows(2 * N, 2 * N + HALF, HALF)], d2_other),
                (lower.at[N : 2 * N], h_other),
            )
        )
    ]
    mine[0].wait()
    gap = newton_start(block_ref[...], x_ref, t_ref, d_ref)
    gap = lax.fori_loop(0, FIXED_STEPS, lambda _, gap: newton_step(gap, x_ref, t_ref), gap)
    gap_ref[...] = jnp.full(gap_ref.shape, gap, f32)
    for copy in copies:
        copy.wait()


def level_one(
    diag, lower, d_other, g_other, first_x, first_t, gap_in,
    inverse_ref, v_ref, send_ref, keep_ref,
    d_own, d_last, g_whole, g_ref, x_ref, t_ref, d_ref, sems,
):
    core, mine, other, share, rest = places()
    copies = loads(
        sems,
        (diag.at[rows(N, 3 * N)], d_own),
        (d_other, d_last),
        (lower.at[rows(2 * N, 3 * N)], g_whole.at[:, mine]),
        (g_other, g_whole.at[:, other]),
    )
    x_ref[...] = first_x[...]
    t_ref[...] = first_t[...]
    copies[0].wait()
    block = d_own[mine]
    d_ref[0], d_ref[1] = split(block)
    first = newton_finish(jnp.max(gap_in[...]), x_ref, t_ref, d_ref, noise_of(block))

    def last_block():
        copies[1].wait()
        return d_last[...]

    invert(first, d_own[other], last_block, inverse_ref, x_ref, t_ref, d_ref)
    for copy in copies[2:]:
        copy.wait()

    @pl.when(core == 0)
    def _():
        g_ref[...] = g_whole[...]

    @pl.when(core == 1)
    def _():
        g_ref[...] = g_whole[...].T

    g = split(g_ref[...])
    v = mul(split(inverse_ref[...]), g, NT)
    v_ref[...] = v
    g_whole[...] = mul(g, split(v))
    send_ref[:N] = g_whole[:, other]
    send_ref[N:] = g_whole[mine, mine]
    keep_ref[:N] = g_whole[:, mine]
    keep_ref[N:] = g_whole[other, other]


def outward(
    inverse_ref, v_ref, send_ref, lower, right_side, f_other, h_other, next_left, next_right,
    came_ref, w_ref, z_ref, pack_ref, hw_ref, small_ref,
    h_whole, h_ref, f_ref, sems, send_sems, recv_sems,
):
    core, mine, other, share, rest = places()
    partner = {"rhs": 1 - core}
    arrived = greet(partner)
    wanted = loads(
        sems, (right_side.at[:, rows(N, 3 * N)], f_ref.at[share]), (f_other, f_ref.at[rest])
    )
    arrived()
    swapped = remote(send_ref, came_ref, (send_sems, recv_sems), 0, partner)

    @pl.when(core == 0)
    def _():
        copies = [
            pltpu.make_async_copy(lower.at[N : 2 * N], h_whole.at[:, :HALF], sems.at[2]),
            pltpu.make_async_copy(h_other, h_whole.at[:, HALF:], sems.at[3]),
        ]
        for copy in copies:
            copy.start()
        for copy in copies:
            copy.wait()
        h_ref[...] = h_whole[...].T

    @pl.when(core == 1)
    def _():
        copies = [
            pltpu.make_async_copy(next_left, h_ref.at[:, :HALF], sems.at[2]),
            pltpu.make_async_copy(next_right, h_ref.at[:, HALF:], sems.at[3]),
        ]
        for copy in copies:
            copy.start()
        for copy in copies:
            copy.wait()

    h, v = split(h_ref[...]), split(v_ref[...])
    c = -mul(h, v)
    pack_ref[:N] = c[:, :HALF]
    pack_ref[N : 2 * N] = c[:, HALF:]
    inverse = split(inverse_ref[...])
    w = mul(inverse, h, NT)
    w_ref[...] = w
    w = split(w)
    h_whole[...] = mul(h, w)
    hw_ref[...] = h_whole[:, mine]
    pack_ref[2 * N : 3 * N] = h_whole[:, other]
    for copy in wanted:
        copy.wait()
    f = split(f_ref[...])
    z_ref[...] = mul(f, inverse)
    for index, term in enumerate((w, v)):
        first = 3 * N + index * RHS
        f_ref[...] = mul(f, term)
        small_ref[index] = f_ref[share]
        pack_ref[first : first + SHARE] = f_ref[rest, :HALF]
        pack_ref[first + SHARE : first + RHS] = f_ref[rest, HALF:]
    swapped.wait()


def level_two(
    diag, d_other, keep_ref, came_ref, inverse_ref,
    d_own, x_ref, t_ref, d_ref, sems,
):
    core, mine, other, share, rest = places()
    loads(sems, (diag.at[2 * N : 3 * N], d_own))[0].wait()
    d_own[...] = d_own[...] - (keep_ref[:N] + came_ref[:N])
    last_block = lambda: d_other[...] - (keep_ref[N:] + came_ref[N:])
    first = newton(d_own[mine], x_ref, t_ref, d_ref)
    invert(first, d_own[other], last_block, inverse_ref, x_ref, t_ref, d_ref)


def survivors(
    inverse_ref, own_ref, came_ref, hw_ref, small_ref,
    diag, right_side, coarse_sol, v_any, w_any, z_any,
    diag_ref, low_out, rhs_ref, solution_ref,
    c_both, hw_both, hz_both, low_send, diag_send, rhs_send, diag_came, cross_came, rhs_came,
    d0, f0, f2, y_ref, v_ref, w_ref, z_ref, y_next, y_send, ys_ref, x2_ref, x_ref, x_both,
    sems, send_sems, recv_sems,
):
    core, mine, other, share, rest = places()
    me = lax.axis_index("tm")
    runs = lax.axis_size("tm")
    after, before = {"tm": lax.rem(me + 1, runs)}, {"tm": lax.rem(me + runs - 1, runs)}
    partner = {"rhs": 1 - core}
    arrived = greet(after, before, partner)
    copies = loads(
        sems,
        (right_side.at[:, 2 * N : 3 * N], f2),
        (diag.at[:N], d0),
        (right_side.at[:, :N], f0),
        (coarse_sol, y_ref),
        (v_any, v_ref),
        (w_any, w_ref),
        (z_any, z_ref),
    )
    pair = (send_sems, recv_sems)
    inverse = split(inverse_ref[...])
    for column in range(2):
        span = slice(column * HALF, (column + 1) * HALF)
        c_both[core, :, span] = own_ref[column * N : (column + 1) * N]
        c_both[1 - core, :, span] = came_ref[column * N : (column + 1) * N]
        first = 3 * N + column * SHARE
        hz_both[1 - core, :, span] = came_ref[first : first + SHARE]
        hz_both[2, :, span] = came_ref[first + RHS : first + RHS + SHARE]
    hw_both[core] = hw_ref[...]
    hw_both[1 - core] = came_ref[2 * N : 3 * N]
    hz_both[core] = small_ref[0]
    right = split(c_both[1])
    u_right = split(mul(inverse, split(c_both[1, mine]), NT))
    arrived()
    later = remote(coarse_sol, y_next, pair, 0, before)

    def diag_block(place):
        c_rows = split(c_both[1, place])
        return hw_both[1, place] + mul(c_rows, u_right)

    corner = pl.ds(pl.multiple_of(core * HALF, HALF), HALF)

    @pl.when(core == 0)
    def _():
        diag_send[HALF:] = diag_block(slice(HALF, N))
        remote(diag_send.at[HALF:], diag_came.at[HALF:], pair, 1, after)

    diag_send[:HALF] = diag_block(corner)
    square = remote(diag_send.at[:HALF], diag_came.at[:HALF], pair, 2, after)
    left = split(c_both[0])
    u_left = split(mul(inverse, split(c_both[0, mine]), NT))
    lows = []
    for half in range(2):
        span = slice(half * HALF, (half + 1) * HALF)
        low_send[span] = -mul((right[0][span], right[1][span]), u_left)
        lows.append(remote(low_send.at[span], low_out.at[span], pair, 3 + half, after))
    copies[0].wait()
    z2 = mul(split(f2[...] - (small_ref[1] + hz_both[2])), inverse)
    z2_parts = split(z2)
    rhs_send[...] = hz_both[1] + mul(z2_parts, right, NT)
    rhs_sent = remote(rhs_send, rhs_came, pair, 5, after)

    for copy in copies[1:4]:
        copy.wait()
    diag_ref[...] = d0[...] - hw_both[0] - mul(left, u_left)
    rhs_ref[...] = f0[...] - hz_both[0] - mul(z2_parts, left, NT)

    later.wait_recv()

    @pl.when(core == 0)
    def _():
        y_send[...] = y_next[...]
        ys_ref[0] = y_ref[...]

    @pl.when(core == 1)
    def _():
        y_send[...] = y_ref[...]
        ys_ref[0] = y_next[...]

    swap_y = remote(y_send, ys_ref.at[1], pair, 6, partner)
    known = mul(split(y_ref[...]), left) + mul(split(y_next[...]), right)
    x2_ref[0] = z2 - mul(split(known), inverse)
    swap_x2 = remote(x2_ref.at[0], x2_ref.at[1], pair, 7, partner)
    for copy in copies[4:]:
        copy.wait()
    swap_y.wait_recv()
    swap_x2.wait_recv()
    v, w = split(v_ref[...]), split(w_ref[...])
    for slot, place in ((1, rest), (0, share)):
        x_ref[slot] = (
            z_ref[place]
            - mul(split(ys_ref[slot]), w, NT)
            - mul(split(x2_ref[slot]), v, NT)
        )
        if slot == 1:
            swap_x = remote(x_ref.at[1], x_both, pair, 8, partner)
    solution_ref[:, :N] = y_ref[...]
    solution_ref[:, 2 * N : 3 * N] = x2_ref[0]
    swap_x.wait_recv()

    @pl.when(core == 0)
    def _():
        solution_ref[:, N : 2 * N] = x_ref[0]
        solution_ref[:, 3 * N :] = x_both[...]

    @pl.when(core == 1)
    def _():
        solution_ref[:, N : 2 * N] = x_both[...]
        solution_ref[:, 3 * N :] = x_ref[0]

    def crossing(device):
        return pltpu.make_async_remote_copy(
            src_ref=diag_send.at[HALF:],
            dst_ref=diag_came.at[HALF:],
            send_sem=send_sems.at[1],
            recv_sem=recv_sems.at[1],
            device_id=device,
            device_id_type=MESH,
        )

    def handing():
        return pltpu.make_async_remote_copy(
            src_ref=diag_came.at[HALF:],
            dst_ref=cross_came,
            send_sem=send_sems.at[9],
            recv_sem=recv_sems.at[9],
            device_id=partner,
            device_id_type=MESH,
        )

    @pl.when(core == 0)
    def _():
        crossing(after).wait_recv()
        handing().start()
        diag_ref[HALF:] = diag_ref[HALF:] - diag_came[HALF:]

    square.wait_recv()
    diag_ref[corner] = diag_ref[corner] - diag_came[:HALF]

    @pl.when(core == 1)
    def _():
        handing().wait_recv()
        diag_ref[:HALF] = diag_ref[:HALF] - cross_came[...].T

    rhs_sent.wait_recv()
    rhs_ref[...] = rhs_ref[...] - rhs_came[...]
    for copy in lows:
        copy.wait_recv()
    for copy in (later, square, *lows, rhs_sent, swap_y, swap_x2, swap_x):
        copy.wait_send()

    @pl.when(core == 0)
    def _():
        crossing(after).wait_send()
        handing().wait_send()


def shape(*dims):
    return jax.ShapeDtypeStruct(dims, f32)


def call(body, in_specs, outs, out_specs, scratch, flops, args, limit, **params):
    size = sum(a.size for a in args) + sum(o.size for o in outs)
    return pl.pallas_call(
        body,
        out_shape=outs,
        in_specs=in_specs,
        out_specs=out_specs,
        scratch_shapes=scratch,
        compiler_params=pltpu.CompilerParams(vmem_limit_bytes=limit << 20, **params),
        cost_estimate=pl.CostEstimate(flops=flops, bytes_accessed=4 * size, transcendentals=0),
    )(*args)


def newton_scratch():
    return [pltpu.VMEM((HALF, HALF), f32)] * 2 + [pltpu.VMEM((2, HALF, HALF), bf16)]


def copy_sems(count):
    return pltpu.SemaphoreType.DMA((count,))


def shards(diag, lower, right_side, coarse_sol):
    runs = lax.axis_size("tm")
    sent_first = lower[:N]
    diag, lower, right_side, coarse_sol = (
        pltpu.with_memory_space_constraint(array, pltpu.HBM)
        for array in (diag, lower, right_side, coarse_sol)
    )
    next_left, next_right = (
        lax.ppermute(
            sent_first,
            ("tm", "rhs"),
            [(2 * ((i + 1) % runs) + source, 2 * i + 1) for i in range(runs)],
        )
        for source in (0, 1)
    )
    swap = lambda x: lax.ppermute(x, "rhs", [(0, 1), (1, 0)])
    full, half, quarter = (N, N), (N, HALF), (HALF, HALF)
    small, scratch = (SHARE, N), lambda *dims: pltpu.VMEM(dims, f32)
    d_other, g_other, f_other, h_other, d2_other, first_x, first_t, gap = call(
        partners,
        [HBM] * 3,
        [shape(*quarter), shape(*half), shape(*small), shape(*half), shape(*quarter),
         shape(*quarter), shape(*quarter), shape(8, 128)],
        [ANY] * 5 + [VMEM] * 3,
        [scratch(*quarter), pltpu.VMEM((2, HALF, HALF), bf16),
         copy_sems(1), copy_sems(5), copy_sems(5)],
        2 * HALF**3 * 30,
        (diag, lower, right_side),
        16,
        collective_id=1,
        has_side_effects=True,
    )
    inverse, v, send, keep = call(
        level_one,
        [HBM] * 2 + [ANY] * 2 + [VMEM] * 3,
        [shape(*full), shape(*full), shape(N + HALF, HALF), shape(N + HALF, HALF)],
        [VMEM] * 4,
        [scratch(*half), scratch(*quarter), scratch(*full), scratch(*full)]
        + newton_scratch() + [copy_sems(4)],
        2 * N**3 * 20,
        (diag, lower, d_other, g_other, first_x, first_t, gap),
        28,
    )
    came, w, z, pack, hw, tails = call(
        outward,
        [VMEM] * 2 + [ANY] + [HBM] * 2 + [ANY] * 4,
        [shape(N + HALF, HALF), shape(*full), shape(RHS, N), shape(3 * N + 2 * RHS, HALF),
         shape(*half), shape(2, *small)],
        [ANY] + [VMEM] * 5,
        [scratch(*full), scratch(*full), scratch(RHS, N), copy_sems(4), copy_sems(1), copy_sems(1)],
        2 * N**3 * 10,
        (inverse, v, send, lower, right_side, f_other, h_other, next_left, next_right),
        28,
        collective_id=3,
        has_side_effects=True,
    )
    pack_came = swap(pack)
    inverse2 = call(
        level_two,
        [HBM] + [VMEM] * 3,
        [shape(*full)],
        [VMEM],
        [scratch(*half)] + newton_scratch() + [copy_sems(1)],
        2 * N**3 * 20,
        (diag, d2_other, keep, came),
        28,
    )[0]
    return call(
        survivors,
        [VMEM] * 5 + [HBM] * 3 + [ANY] * 3,
        [shape(*half), shape(*half), shape(*small), shape(SHARE, 4 * N)],
        [VMEM, ANY, VMEM, VMEM],
        [scratch(2, *full), scratch(2, *half), scratch(3, *small),
         scratch(*half), scratch(*half), scratch(*small),
         scratch(*half), scratch(*quarter), scratch(*small),
         scratch(*half), scratch(*small), scratch(*small), scratch(*small),
         scratch(*full), scratch(*full), scratch(RHS, N),
         scratch(*small), scratch(*small), scratch(2, *small),
         scratch(2, *small), scratch(2, *small), scratch(*small),
         copy_sems(7), copy_sems(10), copy_sems(10)],
        2 * N**3 * 9,
        (inverse2, pack, pack_came, hw, tails, diag, right_side, coarse_sol, v, w, z),
        40,
        collective_id=2,
        has_side_effects=True,
    )


def solution(mesh):
    return jax.shard_map(
        shards,
        mesh=mesh,
        in_specs=(P("tm", "rhs"), P("tm", "rhs"), P("rhs", "tm"), P("rhs", "tm")),
        out_specs=(P("tm", "rhs"), P("tm", "rhs"), P("rhs", "tm"), P("rhs", "tm")),
        check_vma=False,
    )
```

time: 97 us -> 77.2 us (0.80)
  Pallas kernels: 68.1 us -> 55.8 us
  waiting for transfers between devices: 4.63 us -> 0.01 us
  local copies, waits for them, and re-layouts: 8.41 us -> 4.11 us
  starting transfers between devices: 14.8 us -> 15.9 us
    pallas_call x5, Pallas kernels: 68.1 us -> 55.8 us  [call(): pl.pallas_call(body, out_shape=outs, in_specs=in_specs, out_specs=out_spe...]
    ppermute x2 -> x1, waiting for transfers between devices: 4.63 us -> 0.01 us  [shards(): swap = lambda x: lax.ppermute(x, 'rhs', [(0, 1), (1, 0)])]
    unnamed x18 -> x4, local copies, waits for them, and re-layouts: 7.27 us -> 3.04 us
    ppermute x2 -> x1, starting transfers between devices: 0.6 us -> 1.61 us  [shards(): swap = lambda x: lax.ppermute(x, 'rhs', [(0, 1), (1, 0)])]
  transfers between devices with their start and end apart: 4 -> 3, of which waited for: 1 -> 0; matrix products, arithmetic and copies ran while one was open for 0% -> 0% of each run, Pallas kernels for 31% -> 31%
where the time goes in v3:
time: 77.2 us; the launch traced here: 76.5 us
  Pallas kernels  55.8 us (72%)
  starting transfers between devices  15.9 us (21%)
  local copies, waits for them, and re-layouts  4.11 us (5%)
    pallas_call x5, Pallas kernels, call(): pl.pallas_call(body, out_shape=outs, in_specs=in_specs, out_specs=out_spe...  55.8 us
    ppermute x2, starting transfers between devices, shards(): lax.ppermute(sent_first, ('tm', 'rhs'), [(2 * ((i + 1) % runs) + source,...  14.2 us
    unnamed x4, local copies, waits for them, and re-layouts  3.04 us
    ppermute x1, starting transfers between devices, shards(): swap = lambda x: lax.ppermute(x, 'rhs', [(0, 1), (1, 0)])  1.61 us
  transfers between devices with their start and end apart: 3, of which 0 were waited for; matrix products, arithmetic and copies ran while one was open for 0% of the time, Pallas kernels for 31%

profile of v3, /device:TPU:1, one launch (start us, length us, event | category | flops | bytes accessed | tf_op | source)
XLA Modules:
  0.0 76.5 jit_solution(12207257402734935488)
XLA Ops:
  0.6 1.1 %slice.3 = f32[512,256]{1,0:T(8,128)S(1)} slice(f32[2048,256]{1,0:T(8,128)} %lower.5), slice={[0:512], [0:256]} | slice | bytes 1048576 | tf_op jit(solution)/shard_map/slice | solution.py:497
  1.7 12.9 %collective-permute-start.1 = (f32[512,256]{1,0:T(8,128)S(1)}, f32[512,256]{1,0:T(8,128)S(1)}, u32[]{:S(2)}, u32[]{:S(2)}) collective-permute-start(f32[512,256]{1,0:T(8,128)S(1)} %slice.3), channel_id=1, source_target_pairs={{3,1},{5,3},{7,5},{9,7},{11,9},{13,11},{15,13},{17,15},{19,17},{21... | collective-permute-start | bytes 1572872 | tf_op jit(solution)/shard_map/ppermute | solution.py:503
  14.7 1.3 %collective-permute-start = (f32[512,256]{1,0:T(8,128)S(1)}, f32[512,256]{1,0:T(8,128)S(1)}, u32[]{:S(2)}, u32[]{:S(2)}) collective-permute-start(f32[512,256]{1,0:T(8,128)S(1)} %slice.3), channel_id=1, source_target_pairs={{2,1},{4,3},{6,5},{8,7},{10,9},{12,11},{14,13},{16,15},{18,17},{20... | collective-permute-start | bytes 1572872 | tf_op jit(solution)/shard_map/ppermute | solution.py:503
  16.0 5.1 %shard_map.75 = (f32[256,256]{1,0:T(8,128)S(1)}, f32[512,256]{1,0:T(8,128)S(1)}, f32[64,512]{1,0:T(8,128)S(1)}, f32[512,256]{1,0:T(8,128)S(1)}, f32[256,256]{1,0...) custom-call(f32[2048,256]{1,0:T(8,128)} %diag.7, f32[2048,256]{1,0:T(8,128)} %lower.5, ...), custom_call_target="tpu_custom_call" | custom-call | flops 1006632960 | bytes 6950912 | tf_op jit(solution)/shard_map/pallas_call | solution.py:476
  21.1 9.4 %shard_map.76 = (f32[512,512]{1,0:T(8,128)S(1)}, f32[512,512]{1,0:T(8,128)S(1)}, f32[768,256]{1,0:T(8,128)S(1)}, f32[768,256]{1,0:T(8,128)S(1)}) custom-call(f32[2048,256]{1,0:T(8,128)} %diag.7, f32[2048,256]{1,0:T(8,128)} %lower.5, f32[256,256]{1,0:T(8,128)S(1)} %get-tuple-element.23.d_other, f32[512,256]{1,0:T(8,128)S(1)} %get-tuple-element.24.g_other, ...), custom_call_target="tpu_custom_call" | custom-call | flops 5368709120 | bytes 9179136 | tf_op jit(solution)/shard_map/pallas_call | solution.py:476
  30.5 0.0 collective-permute-done.1.next_right
  30.5 0.0 collective-permute-done.next_left
  30.6 4.1 %shard_map.77 = (f32[768,256]{1,0:T(8,128)S(1)}, f32[512,512]{1,0:T(8,128)S(1)}, f32[128,512]{1,0:T(8,128)S(1)}, f32[1792,256]{1,0:T(8,128)S(1)}, f32[512,256]{1,0:T(8,128)S(1)}, /*index=5*/f32[2,64,512]{2,1,0:T(8,128)S(1)}) custom-call(f32[512,512]{1,0:T(8,128)S(1)} %get-tuple-element.29.inverse_ref, f32[512,512]{1,0:T(8,128)S(1)} %get-tuple-element.30.v_ref.v_any, ...), custom_call_target="tpu_custom_call" | custom-call | flops 2684354560 | bytes 11927552 | tf_op jit(solution)/shard_map/pallas_call | solution.py:476
  34.6 1.6 %collective-permute-start.2 = (f32[1792,256]{1,0:T(8,128)S(1)}, f32[1792,256]{1,0:T(8,128)S(1)}, u32[]{:S(2)}, u32[]{:S(2)}) collective-permute-start(f32[1792,256]{1,0:T(8,128)S(1)} %get-tuple-element.35.own_ref), channel_id=1, source_target_pairs={{0,1},{1,0},{2,3},{3,2},{4,5},{5,4},{6,7},{7,6},{8,9},{9,8},{10,11... | collective-permute-start | bytes 5505032 | tf_op jit(solution)/shard_map/ppermute | solution.py:510
  36.3 9.0 %shard_map.78.inverse_ref = f32[512,512]{1,0:T(8,128)S(1)} custom-call(f32[2048,256]{1,0:T(8,128)} %diag.7, f32[256,256]{1,0:T(8,128)S(1)} %get-tuple-element.22.d_other, f32[768,256]{1,0:T(8,128)S(1)} %get-tuple-element.28.keep_ref, f32[768,256]{1,0:T(8,128)S(1)} %get-tuple-element.34.came_ref), custom_call_target="tpu_custom_call" | custom-call | flops 5368709120 | bytes 4980736 | tf_op jit(solution)/shard_map/pallas_call | solution.py:476
  45.2 0.0 collective-permute-done.2.came_ref
  45.2 28.2 %shard_map.79 = (f32[512,256]{1,0:T(8,128)S(1)}, f32[512,256]{1,0:T(8,128)S(1)}, f32[64,512]{1,0:T(8,128)S(1)}, f32[64,2048]{1,0:T(8,128)S(1)}) custom-call(f32[512,512]{1,0:T(8,128)S(1)} %shard_map.78.inverse_ref, f32[1792,256]{1,0:T(8,128)S(1)} %get-tuple-element.35.own_ref, f32[1792,256]{1,0:T(8,128)S(1)} %collective-permute-done.2.came_ref, ...), custom_call_target="tpu_custom_call" | custom-call | flops 2415919104 | bytes 12320768 | tf_op jit(solution)/shard_map/pallas_call | solution.py:476
  73.5 0.8 %copy.12 = f32[512,256]{1,0:T(8,128)} copy(f32[512,256]{1,0:T(8,128)S(1)} %get-tuple-element.44) | data formatting | bytes 1048576
  74.3 0.8 %copy.13 = f32[512,256]{1,0:T(8,128)} copy(f32[512,256]{1,0:T(8,128)S(1)} %get-tuple-element.45) | data formatting | bytes 1048576
  75.1 0.7 copy.14
  75.7 0.8 %copy.15 = f32[64,2048]{1,0:T(8,128)} copy(f32[64,2048]{1,0:T(8,128)S(1)} %get-tuple-element.47) | data formatting | bytes 1048576
Async XLA Ops:
  1.7 28.8 %collective-permute-start.1 = (f32[512,256]{1,0:T(8,128)S(1)}, f32[512,256]{1,0:T(8,128)S(1)}, u32[]{:S(2)}, u32[]{:S(2)}) collective-permute-start(f32[512,256]{1,0:T(8,128)S(1)} %slice.3), channel_id=1, source_target_pairs={{3,1},{5,3},{7,5},{9,7},{11,9},{13,11},{15,13},{17,15},{19,17},{21... | collective-permute-start | bytes 1572872 | tf_op jit(solution)/shard_map/ppermute | solution.py:503
  14.7 15.9 %collective-permute-start = (f32[512,256]{1,0:T(8,128)S(1)}, f32[512,256]{1,0:T(8,128)S(1)}, u32[]{:S(2)}, u32[]{:S(2)}) collective-permute-start(f32[512,256]{1,0:T(8,128)S(1)} %slice.3), channel_id=1, source_target_pairs={{2,1},{4,3},{6,5},{8,7},{10,9},{12,11},{14,13},{16,15},{18,17},{20... | collective-permute-start | bytes 1572872 | tf_op jit(solution)/shard_map/ppermute | solution.py:503
  34.6 10.6 %collective-permute-start.2 = (f32[1792,256]{1,0:T(8,128)S(1)}, f32[1792,256]{1,0:T(8,128)S(1)}, u32[]{:S(2)}, u32[]{:S(2)}) collective-permute-start(f32[1792,256]{1,0:T(8,128)S(1)} %get-tuple-element.35.own_ref), channel_id=1, source_target_pairs={{0,1},{1,0},{2,3},{3,2},{4,5},{5,4},{6,7},{7,6},{8,9},{9,8},{10,11... | collective-permute-start | bytes 5505032 | tf_op jit(solution)/shard_map/ppermute | solution.py:510

commit v4 on v3

--- a/solution.py
+++ b/solution.py
@@ -12,6 +12,10 @@
 HALF = 256
 RHS = 128
 SHARE = 64
+QUARTER = 128
+ROW = 4
+DIRECT = 320
+CHUNK = 96
 LOWEST = 2.0
 TOL = 4e-6
 COARSE_TOL = 1.6e-3
@@ -157,62 +161,78 @@
 
 def partners(
     diag, lower, right_side,
-    d_other, g_other, f_other, h_other, d2_other, x_ref, t_ref, gap_ref,
-    block_ref, d_ref, sems, send_sems, recv_sems,
+    d_own, d_other, g_ref, h_ref, f_ref, d2_own, x_ref, t_ref, gap_ref,
+    d_ref, sems, send_sems, recv_sems,
 ):
-    core = lax.axis_index("rhs")
+    core, mine, other, share, rest = places()
     partner = {"rhs": 1 - core}
     arrived = greet(partner)
-    mine = loads(sems, (diag.at[rows(N, 3 * N + HALF, HALF)], block_ref))
+    section = rows(N, 3 * N)
+    copies = loads(
+        sems,
+        (diag.at[section], d_own),
+        (lower.at[rows(2 * N, 3 * N)], g_ref.at[:, mine]),
+        (lower.at[N : 2 * N], h_ref.at[:, mine]),
+        (right_side.at[:, section], f_ref.at[share]),
+        (diag.at[2 * N : 3 * N], d2_own),
+    )
     arrived()
     pair = (send_sems, recv_sems)
-    copies = [
+    swaps = [
         remote(source, target, pair, index, partner)
         for index, (source, target) in enumerate(
             (
                 (diag.at[rows(3 * N, N + HALF, HALF)], d_other),
-                (lower.at[rows(3 * N, 2 * N)], g_other),
-                (right_side.at[:, rows(3 * N, N)], f_other),
-                (diag.at[rows(2 * N, 2 * N + HALF, HALF)], d2_other),
-                (lower.at[N : 2 * N], h_other),
+                (lower.at[rows(3 * N, 2 * N)], g_ref.at[:, mine]),
+                (right_side.at[:, rows(3 * N, N)], f_ref.at[share]),
             )
         )
     ]
-    mine[0].wait()
-    gap = newton_start(block_ref[...], x_ref, t_ref, d_ref)
+
+    def outer():
+        return pltpu.make_async_remote_copy(
+            src_ref=lower.at[N : 2 * N],
+            dst_ref=h_ref.at[:, mine],
+            send_sem=send_sems.at[3],
+            recv_sem=recv_sems.at[3],
+            device_id=partner,
+            device_id_type=MESH,
+        )
+
+    @pl.when(core == 1)
+    def _():
+        outer().start()
+
+    copies[0].wait()
+    gap = newton_start(d_own[mine], x_ref, t_ref, d_ref)
     gap = lax.fori_loop(0, FIXED_STEPS, lambda _, gap: newton_step(gap, x_ref, t_ref), gap)
     gap_ref[...] = jnp.full(gap_ref.shape, gap, f32)
-    for copy in copies:
+    for copy in copies[1:]:
         copy.wait()
+    for copy in swaps:
+        copy.wait()
+
+    @pl.when(core == 0)
+    def _():
+        outer().wait_recv()
+
+    @pl.when(core == 1)
+    def _():
+        outer().wait_send()
 
 
 def level_one(
-    diag, lower, d_other, g_other, first_x, first_t, gap_in,
+    d_own, d_other, g_whole, d2_own, first_x, first_t, gap_in,
     inverse_ref, v_ref, send_ref, keep_ref,
-    d_own, d_last, g_whole, g_ref, x_ref, t_ref, d_ref, sems,
+    gv_ref, g_ref, x_ref, t_ref, d_ref,
 ):
     core, mine, other, share, rest = places()
-    copies = loads(
-        sems,
-        (diag.at[rows(N, 3 * N)], d_own),
-        (d_other, d_last),
-        (lower.at[rows(2 * N, 3 * N)], g_whole.at[:, mine]),
-        (g_other, g_whole.at[:, other]),
-    )
     x_ref[...] = first_x[...]
     t_ref[...] = first_t[...]
-    copies[0].wait()
     block = d_own[mine]
     d_ref[0], d_ref[1] = split(block)
     first = newton_finish(jnp.max(gap_in[...]), x_ref, t_ref, d_ref, noise_of(block))
-
-    def last_block():
-        copies[1].wait()
-        return d_last[...]
-
-    invert(first, d_own[other], last_block, inverse_ref, x_ref, t_ref, d_ref)
-    for copy in copies[2:]:
-        copy.wait()
+    invert(first, d_own[other], lambda: d_other[...], inverse_ref, x_ref, t_ref, d_ref)
 
     @pl.when(core == 0)
     def _():
@@ -225,49 +245,31 @@
     g = split(g_ref[...])
     v = mul(split(inverse_ref[...]), g, NT)
     v_ref[...] = v
-    g_whole[...] = mul(g, split(v))
-    send_ref[:N] = g_whole[:, other]
-    send_ref[N:] = g_whole[mine, mine]
-    keep_ref[:N] = g_whole[:, mine]
-    keep_ref[N:] = g_whole[other, other]
+    gv_ref[...] = mul(g, split(v))
+    send_ref[:N] = gv_ref[:, other]
+    send_ref[N:] = gv_ref[mine, mine] - d2_own[mine]
+    keep_ref[:N] = gv_ref[:, mine]
+    keep_ref[N:] = gv_ref[other, other]
 
 
 def outward(
-    inverse_ref, v_ref, send_ref, lower, right_side, f_other, h_other, next_left, next_right,
+    inverse_ref, v_ref, send_ref, h_own, f_own, next_left, next_right,
     came_ref, w_ref, z_ref, pack_ref, hw_ref, small_ref,
-    h_whole, h_ref, f_ref, sems, send_sems, recv_sems,
+    h_whole, h_ref, f_ref, send_sems, recv_sems,
 ):
     core, mine, other, share, rest = places()
     partner = {"rhs": 1 - core}
-    arrived = greet(partner)
-    wanted = loads(
-        sems, (right_side.at[:, rows(N, 3 * N)], f_ref.at[share]), (f_other, f_ref.at[rest])
-    )
-    arrived()
+    greet(partner)()
     swapped = remote(send_ref, came_ref, (send_sems, recv_sems), 0, partner)
 
     @pl.when(core == 0)
     def _():
-        copies = [
-            pltpu.make_async_copy(lower.at[N : 2 * N], h_whole.at[:, :HALF], sems.at[2]),
-            pltpu.make_async_copy(h_other, h_whole.at[:, HALF:], sems.at[3]),
-        ]
-        for copy in copies:
-            copy.start()
-        for copy in copies:
-            copy.wait()
-        h_ref[...] = h_whole[...].T
+        h_ref[...] = h_own[...].T
 
     @pl.when(core == 1)
     def _():
-        copies = [
-            pltpu.make_async_copy(next_left, h_ref.at[:, :HALF], sems.at[2]),
-            pltpu.make_async_copy(next_right, h_ref.at[:, HALF:], sems.at[3]),
-        ]
-        for copy in copies:
-            copy.start()
-        for copy in copies:
-            copy.wait()
+        h_ref[:, :HALF] = next_left[...]
+        h_ref[:, HALF:] = next_right[...]
 
     h, v = split(h_ref[...]), split(v_ref[...])
     c = -mul(h, v)
@@ -280,9 +282,7 @@
     h_whole[...] = mul(h, w)
     hw_ref[...] = h_whole[:, mine]
     pack_ref[2 * N : 3 * N] = h_whole[:, other]
-    for copy in wanted:
-        copy.wait()
-    f = split(f_ref[...])
+    f = split(f_own[...])
     z_ref[...] = mul(f, inverse)
     for index, term in enumerate((w, v)):
         first = 3 * N + index * RHS
@@ -293,14 +293,10 @@
     swapped.wait()
 
 
-def level_two(
-    diag, d_other, keep_ref, came_ref, inverse_ref,
-    d_own, x_ref, t_ref, d_ref, sems,
-):
+def level_two(d2_own, keep_ref, came_ref, inverse_ref, d_own, x_ref, t_ref, d_ref):
     core, mine, other, share, rest = places()
-    loads(sems, (diag.at[2 * N : 3 * N], d_own))[0].wait()
-    d_own[...] = d_own[...] - (keep_ref[:N] + came_ref[:N])
-    last_block = lambda: d_other[...] - (keep_ref[N:] + came_ref[N:])
+    d_own[...] = d2_own[...] - (keep_ref[:N] + came_ref[:N])
+    last_block = lambda: -(keep_ref[N:] + came_ref[N:])
     first = newton(d_own[mine], x_ref, t_ref, d_ref)
     invert(first, d_own[other], last_block, inverse_ref, x_ref, t_ref, d_ref)
 
@@ -309,7 +305,7 @@
     inverse_ref, own_ref, came_ref, hw_ref, small_ref,
     diag, right_side, coarse_sol, v_any, w_any, z_any,
     diag_ref, low_out, rhs_ref, solution_ref,
-    c_both, hw_both, hz_both, low_send, diag_send, rhs_send, diag_came, cross_came, rhs_came,
+    c_both, hw_both, hz_both, low_send, hops, diag_send, rhs_send, diag_came, cross_came, rhs_came,
     d0, f0, f2, y_ref, v_ref, w_ref, z_ref, y_next, y_send, ys_ref, x2_ref, x_ref, x_both,
     sems, send_sems, recv_sems,
 ):
@@ -318,7 +314,13 @@
     runs = lax.axis_size("tm")
     after, before = {"tm": lax.rem(me + 1, runs)}, {"tm": lax.rem(me + runs - 1, runs)}
     partner = {"rhs": 1 - core}
-    arrived = greet(after, before, partner)
+    place_x = lax.rem(me, ROW)
+    first_x = me - place_x
+    left_chip = {"tm": first_x + lax.rem(place_x + ROW - 1, ROW)}
+    right_chip = {"tm": first_x + lax.rem(place_x + 1, ROW)}
+    row_after = {"tm": lax.rem(me + ROW, runs)}
+    row_before = {"tm": lax.rem(me + runs - ROW, runs)}
+    arrived = greet(after, before, partner, left_chip, right_chip, row_after, row_before)
     copies = loads(
         sems,
         (right_side.at[:, 2 * N : 3 * N], f2),
@@ -342,15 +344,28 @@
     hw_both[1 - core] = came_ref[2 * N : 3 * N]
     hz_both[core] = small_ref[0]
     right = split(c_both[1])
-    u_right = split(mul(inverse, split(c_both[1, mine]), NT))
+    left = split(c_both[0])
+    u_left = split(mul(inverse, split(c_both[0, mine]), NT))
     arrived()
     later = remote(coarse_sol, y_next, pair, 0, before)
+
+    def low_rows(first, count):
+        span = slice(first, first + count)
+        low_send[span] = -mul((right[0][span], right[1][span]), u_left)
+
+    low_rows(DIRECT, N - DIRECT)
+    steps = []
+    for chunk in range(2):
+        span = pl.ds(DIRECT + chunk * CHUNK, CHUNK)
+        steps.append(remote(low_send.at[span], hops.at[0, chunk], pair, 10 + chunk, left_chip))
+
+    u_right = split(mul(inverse, split(c_both[1, mine]), NT))
 
     def diag_block(place):
         c_rows = split(c_both[1, place])
         return hw_both[1, place] + mul(c_rows, u_right)
 
-    corner = pl.ds(pl.multiple_of(core * HALF, HALF), HALF)
+    corner = mine
 
     @pl.when(core == 0)
     def _():
@@ -358,13 +373,17 @@
         remote(diag_send.at[HALF:], diag_came.at[HALF:], pair, 1, after)
 
     diag_send[:HALF] = diag_block(corner)
-    square = remote(diag_send.at[:HALF], diag_came.at[:HALF], pair, 2, after)
-    left = split(c_both[0])
-    u_left = split(mul(inverse, split(c_both[0, mine]), NT))
+    square = [
+        remote(diag_send.at[span, width], diag_came.at[span, width], pair, index, after)
+        for index, span, width in (
+            (2, slice(QUARTER, HALF), slice(0, HALF)),
+            (9, slice(0, QUARTER), slice(0, QUARTER)),
+        )
+    ]
     lows = []
     for half in range(2):
-        span = slice(half * HALF, (half + 1) * HALF)
-        low_send[span] = -mul((right[0][span], right[1][span]), u_left)
+        span = pl.ds(half * (DIRECT // 2), DIRECT // 2)
+        low_rows(half * (DIRECT // 2), DIRECT // 2)
         lows.append(remote(low_send.at[span], low_out.at[span], pair, 3 + half, after))
     copies[0].wait()
     z2 = mul(split(f2[...] - (small_ref[1] + hz_both[2])), inverse)
@@ -377,6 +396,17 @@
     diag_ref[...] = d0[...] - hw_both[0] - mul(left, u_left)
     rhs_ref[...] = f0[...] - hz_both[0] - mul(z2_parts, left, NT)
 
+    def forward(hop):
+        for chunk in range(2):
+            steps[2 * hop + chunk].wait_recv()
+            steps.append(
+                remote(
+                    hops.at[hop, chunk], hops.at[hop + 1, chunk], pair,
+                    12 + 2 * hop + chunk, left_chip,
+                )
+            )
+
+    forward(0)
     later.wait_recv()
 
     @pl.when(core == 0)
@@ -395,6 +425,7 @@
     swap_x2 = remote(x2_ref.at[0], x2_ref.at[1], pair, 7, partner)
     for copy in copies[4:]:
         copy.wait()
+    forward(1)
     swap_y.wait_recv()
     swap_x2.wait_recv()
     v, w = split(v_ref[...]), split(w_ref[...])
@@ -434,8 +465,8 @@
         return pltpu.make_async_remote_copy(
             src_ref=diag_came.at[HALF:],
             dst_ref=cross_came,
-            send_sem=send_sems.at[9],
-            recv_sem=recv_sems.at[9],
+            send_sem=send_sems.at[18],
+            recv_sem=recv_sems.at[18],
             device_id=partner,
             device_id_type=MESH,
         )
@@ -446,25 +477,67 @@
         handing().start()
         diag_ref[HALF:] = diag_ref[HALF:] - diag_came[HALF:]
 
-    square.wait_recv()
+    def turn(chunk):
+        return pltpu.make_async_remote_copy(
+            src_ref=hops.at[2, chunk],
+            dst_ref=hops.at[3, chunk],
+            send_sem=send_sems.at[16 + chunk],
+            recv_sem=recv_sems.at[16 + chunk],
+            device_id=row_after,
+            device_id_type=MESH,
+        )
+
+    for chunk in range(2):
+        steps[4 + chunk].wait_recv()
+
+        @pl.when(place_x == 0)
+        def _():
+            turn(chunk).start()
+
+    for copy in square:
+        copy.wait_recv()
+    diag_came[:QUARTER, QUARTER:] = diag_came[QUARTER:HALF, :QUARTER].T
     diag_ref[corner] = diag_ref[corner] - diag_came[:HALF]
 
     @pl.when(core == 1)
     def _():
         handing().wait_recv()
         diag_ref[:HALF] = diag_ref[:HALF] - cross_came[...].T
+
+    for chunk in range(2):
+        span = pl.ds(DIRECT + chunk * CHUNK, CHUNK)
+
+        @pl.when(place_x == 0)
+        def _():
+            turn(chunk).wait_recv()
+            low_out[span] = hops[3, chunk]
+
+        @pl.when(place_x != 0)
+        def _():
+            low_out[span] = hops[2, chunk]
 
     rhs_sent.wait_recv()
     rhs_ref[...] = rhs_ref[...] - rhs_came[...]
     for copy in lows:
         copy.wait_recv()
-    for copy in (later, square, *lows, rhs_sent, swap_y, swap_x2, swap_x):
+    for copy in (later, *square, *lows, rhs_sent, swap_y, swap_x2, swap_x, *steps):
         copy.wait_send()
+
+    @pl.when(place_x == 0)
+    def _():
+        for chunk in range(2):
+            turn(chunk).wait_send()
 
     @pl.when(core == 0)
     def _():
         crossing(after).wait_send()
         handing().wait_send()
+
+
+def deliver(*refs):
+    count = (len(refs) - 1) // 2
+    for copy in loads(refs[-1], *zip(refs[:count], refs[count : 2 * count])):
+        copy.wait()
 
 
 def shape(*dims):
@@ -510,14 +583,13 @@
     swap = lambda x: lax.ppermute(x, "rhs", [(0, 1), (1, 0)])
     full, half, quarter = (N, N), (N, HALF), (HALF, HALF)
     small, scratch = (SHARE, N), lambda *dims: pltpu.VMEM(dims, f32)
-    d_other, g_other, f_other, h_other, d2_other, first_x, first_t, gap = call(
+    d_own, d_other, g, h, f, d2_own, first_x, first_t, gap = call(
         partners,
         [HBM] * 3,
-        [shape(*quarter), shape(*half), shape(*small), shape(*half), shape(*quarter),
+        [shape(*half), shape(*quarter), shape(*full), shape(*full), shape(RHS, N), shape(*half),
          shape(*quarter), shape(*quarter), shape(8, 128)],
-        [ANY] * 5 + [VMEM] * 3,
-        [scratch(*quarter), pltpu.VMEM((2, HALF, HALF), bf16),
-         copy_sems(1), copy_sems(5), copy_sems(5)],
+        [VMEM] * 9,
+        [pltpu.VMEM((2, HALF, HALF), bf16), copy_sems(5), copy_sems(4), copy_sems(4)],
         2 * HALF**3 * 30,
         (diag, lower, right_side),
         16,
@@ -526,24 +598,23 @@
     )
     inverse, v, send, keep = call(
         level_one,
-        [HBM] * 2 + [ANY] * 2 + [VMEM] * 3,
+        [VMEM] * 7,
         [shape(*full), shape(*full), shape(N + HALF, HALF), shape(N + HALF, HALF)],
         [VMEM] * 4,
-        [scratch(*half), scratch(*quarter), scratch(*full), scratch(*full)]
-        + newton_scratch() + [copy_sems(4)],
+        [scratch(*full), scratch(*full)] + newton_scratch(),
         2 * N**3 * 20,
-        (diag, lower, d_other, g_other, first_x, first_t, gap),
+        (d_own, d_other, g, d2_own, first_x, first_t, gap),
         28,
     )
     came, w, z, pack, hw, tails = call(
         outward,
-        [VMEM] * 2 + [ANY] + [HBM] * 2 + [ANY] * 4,
+        [VMEM] * 2 + [ANY] + [VMEM] * 4,
         [shape(N + HALF, HALF), shape(*full), shape(RHS, N), shape(3 * N + 2 * RHS, HALF),
          shape(*half), shape(2, *small)],
         [ANY] + [VMEM] * 5,
-        [scratch(*full), scratch(*full), scratch(RHS, N), copy_sems(4), copy_sems(1), copy_sems(1)],
+        [scratch(*full), scratch(*full), scratch(RHS, N), copy_sems(1), copy_sems(1)],
         2 * N**3 * 10,
-        (inverse, v, send, lower, right_side, f_other, h_other, next_left, next_right),
+        (inverse, v, send, h, f, next_left, next_right),
         28,
         collective_id=3,
         has_side_effects=True,
@@ -551,32 +622,36 @@
     pack_came = swap(pack)
     inverse2 = call(
         level_two,
-        [HBM] + [VMEM] * 3,
+        [VMEM] * 3,
         [shape(*full)],
         [VMEM],
-        [scratch(*half)] + newton_scratch() + [copy_sems(1)],
+        [scratch(*half)] + newton_scratch(),
         2 * N**3 * 20,
-        (diag, d2_other, keep, came),
+        (d2_own, keep, came),
         28,
     )[0]
-    return call(
+    finals = [shape(*half), shape(*half), shape(*small), shape(SHARE, 4 * N)]
+    results = call(
         survivors,
         [VMEM] * 5 + [HBM] * 3 + [ANY] * 3,
-        [shape(*half), shape(*half), shape(*small), shape(SHARE, 4 * N)],
-        [VMEM, ANY, VMEM, VMEM],
+        finals,
+        [VMEM] * 4,
         [scratch(2, *full), scratch(2, *half), scratch(3, *small),
-         scratch(*half), scratch(*half), scratch(*small),
+         scratch(*half), scratch(4, 2, CHUNK, HALF), scratch(*half), scratch(*small),
          scratch(*half), scratch(*quarter), scratch(*small),
          scratch(*half), scratch(*small), scratch(*small), scratch(*small),
          scratch(*full), scratch(*full), scratch(RHS, N),
          scratch(*small), scratch(*small), scratch(2, *small),
          scratch(2, *small), scratch(2, *small), scratch(*small),
-         copy_sems(7), copy_sems(10), copy_sems(10)],
+         copy_sems(7), copy_sems(19), copy_sems(19)],
         2 * N**3 * 9,
         (inverse2, pack, pack_came, hw, tails, diag, right_side, coarse_sol, v, w, z),
         40,
         collective_id=2,
         has_side_effects=True,
+    )
+    return call(
+        deliver, [ANY] * 4, finals, [HBM] * 4, [copy_sems(4)], 0, tuple(results), 8
     )
 
 

time: 77.2 us -> 71.8 us (0.930)
  local copies, waits for them, and re-layouts: 4.11 us -> 1.08 us
  Pallas kernels: 55.8 us -> 54.5 us
  starting transfers between devices: 15.9 us -> 15 us
    unnamed x4 -> x0, local copies, waits for them, and re-layouts: 3.04 us -> none
    pallas_call x5 -> x6, Pallas kernels: 55.8 us -> 54.5 us  [call(): pl.pallas_call(body, out_shape=outs, in_specs=in_specs, out_specs=out_spe...]
    ppermute x1, starting transfers between devices: 1.61 us -> 0.8 us  [shards(): swap = lambda x: lax.ppermute(x, 'rhs', [(0, 1), (1, 0)])]
  transfers between devices with their start and end apart: 3 -> 3, of which waited for: 0 -> 0; matrix products, arithmetic and copies ran while one was open for 0% -> 0% of each run, Pallas kernels for 31% -> 29%
where the time goes in v4:
time: 71.8 us; the launch traced here: 71.5 us
  Pallas kernels  54.5 us (76%)
  starting transfers between devices  15 us (21%)
  local copies, waits for them, and re-layouts  1.08 us (2%)
  between operations  0.87 us (1%)
    pallas_call x6, Pallas kernels, call(): pl.pallas_call(body, out_shape=outs, in_specs=in_specs, out_specs=out_spe...  54.5 us
    ppermute x2, starting transfers between devices, shards(): lax.ppermute(sent_first, ('tm', 'rhs'), [(2 * ((i + 1) % runs) + source,...  14.2 us
  transfers between devices with their start and end apart: 3, of which 0 were waited for; matrix products, arithmetic and copies ran while one was open for 0% of the time, Pallas kernels for 29%

profile of v4, /device:TPU:1, one launch (start us, length us, event | category | flops | bytes accessed | tf_op | source)
XLA Modules:
  0.0 71.5 jit_solution(4473749720120616430)
XLA Ops:
  0.6 1.1 %slice.3 = f32[512,256]{1,0:T(8,128)S(1)} slice(f32[2048,256]{1,0:T(8,128)} %lower.1), slice={[0:512], [0:256]} | slice | bytes 1048576 | tf_op jit(solution)/shard_map/slice | solution.py:570
  1.7 12.9 %collective-permute-start.1 = (f32[512,256]{1,0:T(8,128)S(1)}, f32[512,256]{1,0:T(8,128)S(1)}, u32[]{:S(2)}, u32[]{:S(2)}) collective-permute-start(f32[512,256]{1,0:T(8,128)S(1)} %slice.3), channel_id=1, source_target_pairs={{3,1},{5,3},{7,5},{9,7},{11,9},{13,11},{15,13},{17,15},{19,17},{21... | collective-permute-start | bytes 1572872 | tf_op jit(solution)/shard_map/ppermute | solution.py:576
  14.7 1.3 %collective-permute-start = (f32[512,256]{1,0:T(8,128)S(1)}, f32[512,256]{1,0:T(8,128)S(1)}, u32[]{:S(2)}, u32[]{:S(2)}) collective-permute-start(f32[512,256]{1,0:T(8,128)S(1)} %slice.3), channel_id=1, source_target_pairs={{2,1},{4,3},{6,5},{8,7},{10,9},{12,11},{14,13},{16,15},{18,17},{20... | collective-permute-start | bytes 1572872 | tf_op jit(solution)/shard_map/ppermute | solution.py:576
  16.0 4.8 %shard_map.75 = (f32[512,256]{1,0:T(8,128)S(1)}, f32[256,256]{1,0:T(8,128)S(1)}, f32[512,512]{1,0:T(8,128)S(1)}, f32[512,512]{1,0:T(8,128)S(1)}, f32[128,512]{1,...) custom-call(f32[2048,256]{1,0:T(8,128)} %diag.3, ...), custom_call_target="tpu_custom_call" | custom-call | flops 1006632960 | bytes 8916992 | tf_op jit(solution)/shard_map/pallas_call | solution.py:549
  20.8 8.2 %shard_map.76 = (f32[512,512]{1,0:T(8,128)S(1)}, f32[512,512]{1,0:T(8,128)S(1)}, f32[768,256]{1,0:T(8,128)S(1)}, f32[768,256]{1,0:T(8,128)S(1)}) custom-call(f32[512,256]{1,0:T(8,128)S(1)} %get-tuple-element.28.d_own, f32[256,256]{1,0:T(8,128)S(1)} %get-tuple-element.29.d_other, f32[512,512]{1,0:T(8,128)S(1)} %get-tuple-element.30.g_whole, ...), custom_call_target="tpu_custom_call" | custom-call | flops 5368709120 | bytes 6557696 | tf_op jit(solution)/shard_map/pallas_call | solution.py:549
  28.9 0.0 collective-permute-done.1.next_right
  29.0 0.0 collective-permute-done.next_left
  29.0 3.8 %shard_map.77 = (f32[768,256]{1,0:T(8,128)S(1)}, f32[512,512]{1,0:T(8,128)S(1)}, f32[128,512]{1,0:T(8,128)S(1)}, f32[1792,256]{1,0:T(8,128)S(1)}, f32[512,256]{1,0:T(8,128)S(1)}, /*index=5*/f32[2,64,512]{2,1,0:T(8,128)S(1)}) custom-call(f32[512,512]{1,0:T(8,128)S(1)} %get-tuple-element.35.inverse_ref, f32[512,512]{1,0:T(8,128)S(1)} %get-tuple-element.36.v_ref.v_any, ...), custom_call_target="tpu_custom_call" | custom-call | flops 2684354560 | bytes 9961472 | tf_op jit(solution)/shard_map/pallas_call | solution.py:549
  32.7 0.8 %collective-permute-start.2 = (f32[1792,256]{1,0:T(8,128)S(1)}, f32[1792,256]{1,0:T(8,128)S(1)}, u32[]{:S(2)}, u32[]{:S(2)}) collective-permute-start(f32[1792,256]{1,0:T(8,128)S(1)} %get-tuple-element.41.own_ref), channel_id=1, source_target_pairs={{0,1},{1,0},{2,3},{3,2},{4,5},{5,4},{6,7},{7,6},{8,9},{9,8},{10,11... | collective-permute-start | bytes 5505032 | tf_op jit(solution)/shard_map/ppermute | solution.py:583
  33.5 7.9 %shard_map.78.inverse_ref = f32[512,512]{1,0:T(8,128)S(1)} custom-call(f32[512,256]{1,0:T(8,128)S(1)} %get-tuple-element.27.d2_own, f32[768,256]{1,0:T(8,128)S(1)} %get-tuple-element.34.keep_ref, f32[768,256]{1,0:T(8,128)S(1)} %get-tuple-element.40.came_ref), custom_call_target="tpu_custom_call" | custom-call | flops 5368709120 | bytes 3145728 | tf_op jit(solution)/shard_map/pallas_call | solution.py:549
  41.5 0.0 collective-permute-done.2.came_ref
  41.5 28.6 %shard_map.79 = (f32[512,256]{1,0:T(8,128)S(1)}, f32[512,256]{1,0:T(8,128)S(1)}, f32[64,512]{1,0:T(8,128)S(1)}, f32[64,2048]{1,0:T(8,128)S(1)}) custom-call(f32[512,512]{1,0:T(8,128)S(1)} %shard_map.78.inverse_ref, f32[1792,256]{1,0:T(8,128)S(1)} %get-tuple-element.41.own_ref, f32[1792,256]{1,0:T(8,128)S(1)} %collective-permute-done.2.came_ref, ...), custom_call_target="tpu_custom_call" | custom-call | flops 2415919104 | bytes 12320768 | tf_op jit(solution)/shard_map/pallas_call | solution.py:549
  70.1 1.2 %shard_map.80 = (f32[512,256]{1,0:T(8,128)}, f32[512,256]{1,0:T(8,128)}, f32[64,512]{1,0:T(8,128)}, f32[64,2048]{1,0:T(8,128)}) custom-call(f32[512,256]{1,0:T(8,128)S(1)} %get-tuple-element.46.refs_0_, f32[512,256]{1,0:T(8,128)S(1)} %get-tuple-element.47.refs_1_, f32[64,512]{1,0:T(8,128)S(1)} %get-tuple-element.48.refs_2_, ...), custom_call_target="tpu_custom_call" | custom-call | bytes 3407872 | tf_op jit(solution)/shard_map/pallas_call | solution.py:549
Async XLA Ops:
  1.7 27.2 %collective-permute-start.1 = (f32[512,256]{1,0:T(8,128)S(1)}, f32[512,256]{1,0:T(8,128)S(1)}, u32[]{:S(2)}, u32[]{:S(2)}) collective-permute-start(f32[512,256]{1,0:T(8,128)S(1)} %slice.3), channel_id=1, source_target_pairs={{3,1},{5,3},{7,5},{9,7},{11,9},{13,11},{15,13},{17,15},{19,17},{21... | collective-permute-start | bytes 1572872 | tf_op jit(solution)/shard_map/ppermute | solution.py:576
  14.7 14.3 %collective-permute-start = (f32[512,256]{1,0:T(8,128)S(1)}, f32[512,256]{1,0:T(8,128)S(1)}, u32[]{:S(2)}, u32[]{:S(2)}) collective-permute-start(f32[512,256]{1,0:T(8,128)S(1)} %slice.3), channel_id=1, source_target_pairs={{2,1},{4,3},{6,5},{8,7},{10,9},{12,11},{14,13},{16,15},{18,17},{20... | collective-permute-start | bytes 1572872 | tf_op jit(solution)/shard_map/ppermute | solution.py:576
  32.7 8.7 %collective-permute-start.2 = (f32[1792,256]{1,0:T(8,128)S(1)}, f32[1792,256]{1,0:T(8,128)S(1)}, u32[]{:S(2)}, u32[]{:S(2)}) collective-permute-start(f32[1792,256]{1,0:T(8,128)S(1)} %get-tuple-element.41.own_ref), channel_id=1, source_target_pairs={{0,1},{1,0},{2,3},{3,2},{4,5},{5,4},{6,7},{7,6},{8,9},{9,8},{10,11... | collective-permute-start | bytes 5505032 | tf_op jit(solution)/shard_map/ppermute | solution.py:583

commit v5 on v4

--- a/solution.py
+++ b/solution.py
@@ -253,43 +253,41 @@
 
 
 def outward(
-    inverse_ref, v_ref, send_ref, h_own, f_own, next_left, next_right,
-    came_ref, w_ref, z_ref, pack_ref, hw_ref, small_ref,
-    h_whole, h_ref, f_ref, send_sems, recv_sems,
+    inverse_ref, v_ref, send_ref, h_ref, f_own,
+    came_ref, ht_ref, z_ref, pack_ref, corner_ref, small_ref,
+    c_ref, f_ref, send_sems, recv_sems,
 ):
     core, mine, other, share, rest = places()
     partner = {"rhs": 1 - core}
     greet(partner)()
     swapped = remote(send_ref, came_ref, (send_sems, recv_sems), 0, partner)
-
-    @pl.when(core == 0)
-    def _():
-        h_ref[...] = h_own[...].T
-
-    @pl.when(core == 1)
-    def _():
-        h_ref[:, :HALF] = next_left[...]
-        h_ref[:, HALF:] = next_right[...]
-
-    h, v = split(h_ref[...]), split(v_ref[...])
-    c = -mul(h, v)
-    pack_ref[:N] = c[:, :HALF]
-    pack_ref[N : 2 * N] = c[:, HALF:]
-    inverse = split(inverse_ref[...])
-    w = mul(inverse, h, NT)
-    w_ref[...] = w
-    w = split(w)
-    h_whole[...] = mul(h, w)
-    hw_ref[...] = h_whole[:, mine]
-    pack_ref[2 * N : 3 * N] = h_whole[:, other]
-    f = split(f_own[...])
-    z_ref[...] = mul(f, inverse)
-    for index, term in enumerate((w, v)):
-        first = 3 * N + index * RHS
-        f_ref[...] = mul(f, term)
-        small_ref[index] = f_ref[share]
+    v, inverse = split(v_ref[...]), split(inverse_ref[...])
+    z = mul(split(f_own[...]), inverse)
+    z_ref[...] = z
+
+    def stack(place, first):
+        small_ref[place] = f_ref[share]
         pack_ref[first : first + SHARE] = f_ref[rest, :HALF]
         pack_ref[first + SHARE : first + RHS] = f_ref[rest, HALF:]
+
+    @pl.when(core == 0)
+    def _():
+        ht_ref[...] = h_ref[...].T
+        c_ref[...] = -mul(split(ht_ref[...]), v)
+        f_ref[...] = mul(split(z), split(h_ref[...]))
+
+    @pl.when(core == 1)
+    def _():
+        c_ref[...] = -v_ref[...]
+        corner_ref[...] = inverse_ref[:, mine]
+        pack_ref[2 * N : 3 * N] = inverse_ref[:, other]
+        f_ref[...] = z
+
+    pack_ref[:N] = c_ref[:, :HALF]
+    pack_ref[N : 2 * N] = c_ref[:, HALF:]
+    stack(0, 3 * N)
+    f_ref[...] = mul(split(f_own[...]), v)
+    stack(1, 3 * N + RHS)
     swapped.wait()
 
 
@@ -302,11 +300,12 @@
 
 
 def survivors(
-    inverse_ref, own_ref, came_ref, hw_ref, small_ref,
-    diag, right_side, coarse_sol, v_any, w_any, z_any,
+    inverse_ref, own_ref, came_ref, hw_ref, small_ref, first_inverse, v_ref, z_ref, h_ref, ht_ref,
+    diag, lower, right_side, coarse_sol,
     diag_ref, low_out, rhs_ref, solution_ref,
-    c_both, hw_both, hz_both, low_send, hops, diag_send, rhs_send, diag_came, cross_came, rhs_came,
-    d0, f0, f2, y_ref, v_ref, w_ref, z_ref, y_next, y_send, ys_ref, x2_ref, x_ref, x_both,
+    c_both, hw_next, hz_both, low_send, low_came, hops, diag_send, rhs_send, diag_came, cross_came,
+    corner_came, m_ref, n_ref, hw_own, hw_came, rhs_came,
+    d0, f0, f2, y_ref, y_next, y_back, y_send, ys_ref, x2_ref, x_ref, x_both,
     sems, send_sems, recv_sems,
 ):
     core, mine, other, share, rest = places()
@@ -324,12 +323,10 @@
     copies = loads(
         sems,
         (right_side.at[:, 2 * N : 3 * N], f2),
+        (lower.at[:N], n_ref.at[:, mine]),
+        (coarse_sol, y_ref),
         (diag.at[:N], d0),
         (right_side.at[:, :N], f0),
-        (coarse_sol, y_ref),
-        (v_any, v_ref),
-        (w_any, w_ref),
-        (z_any, z_ref),
     )
     pair = (send_sems, recv_sems)
     inverse = split(inverse_ref[...])
@@ -340,14 +337,20 @@
         first = 3 * N + column * SHARE
         hz_both[1 - core, :, span] = came_ref[first : first + SHARE]
         hz_both[2, :, span] = came_ref[first + RHS : first + RHS + SHARE]
-    hw_both[core] = hw_ref[...]
-    hw_both[1 - core] = came_ref[2 * N : 3 * N]
+
+    @pl.when(core == 0)
+    def _():
+        hw_next[...] = came_ref[2 * N : 3 * N]
+
+    @pl.when(core == 1)
+    def _():
+        hw_next[...] = hw_ref[...]
+
     hz_both[core] = small_ref[0]
     right = split(c_both[1])
     left = split(c_both[0])
     u_left = split(mul(inverse, split(c_both[0, mine]), NT))
     arrived()
-    later = remote(coarse_sol, y_next, pair, 0, before)
 
     def low_rows(first, count):
         span = slice(first, first + count)
@@ -363,7 +366,7 @@
 
     def diag_block(place):
         c_rows = split(c_both[1, place])
-        return hw_both[1, place] + mul(c_rows, u_right)
+        return hw_next[place] + mul(c_rows, u_right)
 
     corner = mine
 
@@ -381,20 +384,24 @@
         )
     ]
     lows = []
-    for half in range(2):
-        span = pl.ds(half * (DIRECT // 2), DIRECT // 2)
-        low_rows(half * (DIRECT // 2), DIRECT // 2)
-        lows.append(remote(low_send.at[span], low_out.at[span], pair, 3 + half, after))
+    for index, (first, count) in enumerate(((0, HALF), (HALF, DIRECT - HALF))):
+        span = pl.ds(first, count)
+        low_rows(first, count)
+        lows.append(remote(low_send.at[span], low_came.at[span], pair, 3 + index, after))
+    swap_n = remote(lower.at[:N], n_ref.at[:, mine], pair, 19, partner)
     copies[0].wait()
     z2 = mul(split(f2[...] - (small_ref[1] + hz_both[2])), inverse)
     z2_parts = split(z2)
     rhs_send[...] = hz_both[1] + mul(z2_parts, right, NT)
     rhs_sent = remote(rhs_send, rhs_came, pair, 5, after)
 
-    for copy in copies[1:4]:
-        copy.wait()
-    diag_ref[...] = d0[...] - hw_both[0] - mul(left, u_left)
-    rhs_ref[...] = f0[...] - hz_both[0] - mul(z2_parts, left, NT)
+    copies[1].wait()
+    copies[2].wait()
+    swap_n.wait_recv()
+    n = split(n_ref[...])
+    y = split(y_ref[...])
+    y_back[...] = mul(y, n)
+    later = remote(y_back, y_next, pair, 0, before)
 
     def forward(hop):
         for chunk in range(2):
@@ -407,6 +414,25 @@
             )
 
     forward(0)
+
+    def half_of_own():
+        return pltpu.make_async_remote_copy(
+            src_ref=hw_own.at[:, HALF:],
+            dst_ref=hw_came,
+            send_sem=send_sems.at[20],
+            recv_sem=recv_sems.at[20],
+            device_id=partner,
+            device_id_type=MESH,
+        )
+
+    @pl.when(core == 0)
+    def _():
+        w = split(mul(split(first_inverse[...]), split(h_ref[...])))
+        hw_own[...] = mul(split(ht_ref[...]), w)
+        half_of_own().start()
+        hw_came[...] = hw_own[:, :HALF]
+
+    forward(1)
     later.wait_recv()
 
     @pl.when(core == 0)
@@ -420,36 +446,36 @@
         ys_ref[0] = y_next[...]
 
     swap_y = remote(y_send, ys_ref.at[1], pair, 6, partner)
-    known = mul(split(y_ref[...]), left) + mul(split(y_next[...]), right)
+    known = mul(y, left) + mul(split(y_next[...]), right)
     x2_ref[0] = z2 - mul(split(known), inverse)
     swap_x2 = remote(x2_ref.at[0], x2_ref.at[1], pair, 7, partner)
-    for copy in copies[4:]:
+
+    for copy in copies[3:]:
         copy.wait()
-    forward(1)
-    swap_y.wait_recv()
-    swap_x2.wait_recv()
-    v, w = split(v_ref[...]), split(w_ref[...])
-    for slot, place in ((1, rest), (0, share)):
-        x_ref[slot] = (
-            z_ref[place]
-            - mul(split(ys_ref[slot]), w, NT)
-            - mul(split(x2_ref[slot]), v, NT)
+
+    @pl.when(core == 1)
+    def _():
+        half_of_own().wait_recv()
+
+    diag_ref[...] = d0[...] - hw_came[...] - mul(left, u_left)
+    rhs_ref[...] = f0[...] - hz_both[0] - mul(z2_parts, left, NT)
+
+    def turn(chunk):
+        return pltpu.make_async_remote_copy(
+            src_ref=hops.at[2, chunk],
+            dst_ref=hops.at[3, chunk],
+            send_sem=send_sems.at[16 + chunk],
+            recv_sem=recv_sems.at[16 + chunk],
+            device_id=row_after,
+            device_id_type=MESH,
         )
-        if slot == 1:
-            swap_x = remote(x_ref.at[1], x_both, pair, 8, partner)
-    solution_ref[:, :N] = y_ref[...]
-    solution_ref[:, 2 * N : 3 * N] = x2_ref[0]
-    swap_x.wait_recv()
-
-    @pl.when(core == 0)
-    def _():
-        solution_ref[:, N : 2 * N] = x_ref[0]
-        solution_ref[:, 3 * N :] = x_both[...]
-
-    @pl.when(core == 1)
-    def _():
-        solution_ref[:, N : 2 * N] = x_both[...]
-        solution_ref[:, 3 * N :] = x_ref[0]
+
+    for chunk in range(2):
+        steps[4 + chunk].wait_recv()
+
+        @pl.when(place_x == 0)
+        def _():
+            turn(chunk).start()
 
     def crossing(device):
         return pltpu.make_async_remote_copy(
@@ -475,52 +501,79 @@
     def _():
         crossing(after).wait_recv()
         handing().start()
-        diag_ref[HALF:] = diag_ref[HALF:] - diag_came[HALF:]
-
-    def turn(chunk):
-        return pltpu.make_async_remote_copy(
-            src_ref=hops.at[2, chunk],
-            dst_ref=hops.at[3, chunk],
-            send_sem=send_sems.at[16 + chunk],
-            recv_sem=recv_sems.at[16 + chunk],
-            device_id=row_after,
-            device_id_type=MESH,
-        )
-
-    for chunk in range(2):
-        steps[4 + chunk].wait_recv()
-
-        @pl.when(place_x == 0)
-        def _():
-            turn(chunk).start()
 
     for copy in square:
         copy.wait_recv()
-    diag_came[:QUARTER, QUARTER:] = diag_came[QUARTER:HALF, :QUARTER].T
-    diag_ref[corner] = diag_ref[corner] - diag_came[:HALF]
+    diag_came[:QUARTER, QUARTER:HALF] = diag_came[QUARTER:HALF, :QUARTER].T
+    swap_corner = remote(diag_came.at[:HALF], corner_came, pair, 21, partner)
+
+    swap_y.wait_recv()
+    swap_x2.wait_recv()
+
+    @pl.when(core == 0)
+    def _():
+        for slot in range(2):
+            ys_ref[slot] = mul(split(ys_ref[slot]), split(h_ref[...]), NT)
+
+    v, w = split(v_ref[...]), split(first_inverse[...])
+    for slot, place in ((1, rest), (0, share)):
+        x_ref[slot] = (
+            z_ref[place] - mul(split(ys_ref[slot]), w) - mul(split(x2_ref[slot]), v, NT)
+        )
+        if slot == 1:
+            swap_x = remote(x_ref.at[1], x_both, pair, 8, partner)
+    solution_ref[:, :N] = y_ref[...]
+    solution_ref[:, 2 * N : 3 * N] = x2_ref[0]
+
+    m_ref[mine, mine] = diag_came[:HALF]
+    swap_corner.wait_recv()
+    m_ref[other, other] = corner_came[...]
+
+    @pl.when(core == 0)
+    def _():
+        m_ref[HALF:, :HALF] = diag_came[HALF:]
 
     @pl.when(core == 1)
     def _():
         handing().wait_recv()
-        diag_ref[:HALF] = diag_ref[:HALF] - cross_came[...].T
-
+        m_ref[HALF:, :HALF] = cross_came[...]
+
+    m_ref[:HALF, HALF:] = m_ref[HALF:, :HALF].T
+    applied = split(mul(split(m_ref[...]), split(n_ref[mine]), NT))
+    diag_ref[...] = diag_ref[...] - mul(n, applied)
+    swap_x.wait_recv()
+
+    @pl.when(core == 0)
+    def _():
+        solution_ref[:, N : 2 * N] = x_ref[0]
+        solution_ref[:, 3 * N :] = x_both[...]
+
+    @pl.when(core == 1)
+    def _():
+        solution_ref[:, N : 2 * N] = x_both[...]
+        solution_ref[:, 3 * N :] = x_ref[0]
+
+    lows[0].wait_recv()
+    low_out[...] = mul(split(n_ref[:, :HALF]), split(low_came[:HALF]))
+    rhs_sent.wait_recv()
+    rhs_ref[...] = rhs_ref[...] - mul(split(rhs_came[...]), n, NT)
+    lows[1].wait_recv()
     for chunk in range(2):
         span = pl.ds(DIRECT + chunk * CHUNK, CHUNK)
 
         @pl.when(place_x == 0)
         def _():
             turn(chunk).wait_recv()
-            low_out[span] = hops[3, chunk]
+            low_came[span] = hops[3, chunk]
 
         @pl.when(place_x != 0)
         def _():
-            low_out[span] = hops[2, chunk]
-
-    rhs_sent.wait_recv()
-    rhs_ref[...] = rhs_ref[...] - rhs_came[...]
-    for copy in lows:
-        copy.wait_recv()
-    for copy in (later, *square, *lows, rhs_sent, swap_y, swap_x2, swap_x, *steps):
+            low_came[span] = hops[2, chunk]
+
+    low_out[...] = low_out[...] + mul(split(n_ref[:, HALF:]), split(low_came[HALF:]))
+    for copy in (
+        later, *square, *lows, rhs_sent, swap_y, swap_x2, swap_x, swap_n, swap_corner, *steps
+    ):
         copy.wait_send()
 
     @pl.when(place_x == 0)
@@ -532,6 +585,7 @@
     def _():
         crossing(after).wait_send()
         handing().wait_send()
+        half_of_own().wait_send()
 
 
 def deliver(*refs):
@@ -566,19 +620,9 @@
 
 
 def shards(diag, lower, right_side, coarse_sol):
-    runs = lax.axis_size("tm")
-    sent_first = lower[:N]
     diag, lower, right_side, coarse_sol = (
         pltpu.with_memory_space_constraint(array, pltpu.HBM)
         for array in (diag, lower, right_side, coarse_sol)
-    )
-    next_left, next_right = (
-        lax.ppermute(
-            sent_first,
-            ("tm", "rhs"),
-            [(2 * ((i + 1) % runs) + source, 2 * i + 1) for i in range(runs)],
-        )
-        for source in (0, 1)
     )
     swap = lambda x: lax.ppermute(x, "rhs", [(0, 1), (1, 0)])
     full, half, quarter = (N, N), (N, HALF), (HALF, HALF)
@@ -606,15 +650,15 @@
         (d_own, d_other, g, d2_own, first_x, first_t, gap),
         28,
     )
-    came, w, z, pack, hw, tails = call(
+    came, ht, z, pack, hw, tails = call(
         outward,
-        [VMEM] * 2 + [ANY] + [VMEM] * 4,
+        [VMEM] * 2 + [ANY] + [VMEM] * 2,
         [shape(N + HALF, HALF), shape(*full), shape(RHS, N), shape(3 * N + 2 * RHS, HALF),
          shape(*half), shape(2, *small)],
         [ANY] + [VMEM] * 5,
-        [scratch(*full), scratch(*full), scratch(RHS, N), copy_sems(1), copy_sems(1)],
-        2 * N**3 * 10,
-        (inverse, v, send, h, f, next_left, next_right),
+        [scratch(*full), scratch(RHS, N), copy_sems(1), copy_sems(1)],
+        2 * N**3 * 6,
+        (inverse, v, send, h, f),
         28,
         collective_id=3,
         has_side_effects=True,
@@ -633,19 +677,21 @@
     finals = [shape(*half), shape(*half), shape(*small), shape(SHARE, 4 * N)]
     results = call(
         survivors,
-        [VMEM] * 5 + [HBM] * 3 + [ANY] * 3,
+        [VMEM] * 10 + [HBM] * 4,
         finals,
         [VMEM] * 4,
-        [scratch(2, *full), scratch(2, *half), scratch(3, *small),
-         scratch(*half), scratch(4, 2, CHUNK, HALF), scratch(*half), scratch(*small),
-         scratch(*half), scratch(*quarter), scratch(*small),
-         scratch(*half), scratch(*small), scratch(*small), scratch(*small),
-         scratch(*full), scratch(*full), scratch(RHS, N),
-         scratch(*small), scratch(*small), scratch(2, *small),
-         scratch(2, *small), scratch(2, *small), scratch(*small),
-         copy_sems(7), copy_sems(19), copy_sems(19)],
+        [scratch(2, *full), scratch(*half), scratch(3, *small), scratch(*half), scratch(*half),
+         scratch(4, 2, CHUNK, HALF), scratch(*half), scratch(*small), scratch(*half),
+         scratch(*quarter),
+         scratch(*quarter), scratch(*full), scratch(*full), scratch(*full), scratch(*half),
+         scratch(*small),
+         scratch(*half), scratch(*small), scratch(*small), scratch(*small), scratch(*small),
+         scratch(*small), scratch(*small), scratch(2, *small), scratch(2, *small),
+         scratch(2, *small), scratch(*small),
+         copy_sems(5), copy_sems(22), copy_sems(22)],
         2 * N**3 * 9,
-        (inverse2, pack, pack_came, hw, tails, diag, right_side, coarse_sol, v, w, z),
+        (inverse2, pack, pack_came, hw, tails, inverse, v, z, h, ht,
+         diag, lower, right_side, coarse_sol),
         40,
         collective_id=2,
         has_side_effects=True,

time: 71.8 us -> 61.5 us (0.86)
  starting transfers between devices: 15 us -> 0.71 us
  Pallas kernels: 54.5 us -> 59.9 us
  local copies, waits for them, and re-layouts: 1.08 us -> 0 us
    ppermute x2 -> x0, starting transfers between devices: 14.2 us -> none  [shards(): lax.ppermute(sent_first, ('tm', 'rhs'), [(2 * ((i + 1) % runs) + source,...]
    pallas_call x6, Pallas kernels: 54.5 us -> 59.9 us  [call(): pl.pallas_call(body, out_shape=outs, in_specs=in_specs, out_specs=out_spe...]
    slice x1 -> x0, local copies, waits for them, and re-layouts: 1.08 us -> none  [shards(): sent_first = lower[:N]]
  transfers between devices with their start and end apart: 3 -> 1, of which waited for: 0 -> 0; matrix products, arithmetic and copies ran while one was open for 0% -> 0% of each run, Pallas kernels for 29% -> 13%
where the time goes in v5:
time: 61.5 us; the launch traced here: 61.4 us
  Pallas kernels  59.9 us (97%)
  between operations  0.84 us (1%)
  starting transfers between devices  0.71 us (1%)
    pallas_call x6, Pallas kernels, call(): pl.pallas_call(body, out_shape=outs, in_specs=in_specs, out_specs=out_spe...  59.9 us
  transfers between devices with their start and end apart: 1, of which 0 were waited for; matrix products, arithmetic and copies ran while one was open for 0% of the time, Pallas kernels for 13%

profile of v5, /device:TPU:1, one launch (start us, length us, event | category | flops | bytes accessed | tf_op | source)
XLA Modules:
  0.0 61.4 jit_solution(11304674251431655956)
XLA Ops:
  0.6 6.4 %shard_map.75 = (f32[512,256]{1,0:T(8,128)S(1)}, f32[256,256]{1,0:T(8,128)S(1)}, f32[512,512]{1,0:T(8,128)S(1)}, f32[512,512]{1,0:T(8,128)S(1)}, f32[128,512]{1,...) custom-call(f32[2048,256]{1,0:T(8,128)} %diag.3, ...), custom_call_target="tpu_custom_call" | custom-call | flops 1006632960 | bytes 8916992 | tf_op jit(solution)/shard_map/pallas_call | solution.py:603
  7.0 8.2 %shard_map.76 = (f32[512,512]{1,0:T(8,128)S(1)}, f32[512,512]{1,0:T(8,128)S(1)}, f32[768,256]{1,0:T(8,128)S(1)}, f32[768,256]{1,0:T(8,128)S(1)}) custom-call(f32[512,256]{1,0:T(8,128)S(1)} %get-tuple-element.28.d_own, f32[256,256]{1,0:T(8,128)S(1)} %get-tuple-element.29.d_other, f32[512,512]{1,0:T(8,128)S(1)} %get-tuple-element.30.g_whole, ...), custom_call_target="tpu_custom_call" | custom-call | flops 5368709120 | bytes 6557696 | tf_op jit(solution)/shard_map/pallas_call | solution.py:603
  15.2 2.3 %shard_map.77 = (f32[768,256]{1,0:T(8,128)S(1)}, f32[512,512]{1,0:T(8,128)S(1)}, f32[128,512]{1,0:T(8,128)S(1)}, f32[1792,256]{1,0:T(8,128)S(1)}, f32[512,256]{1,0:T(8,128)S(1)}, /*index=5*/f32[2,64,512]{2,1,0:T(8,128)S(1)}) custom-call(f32[512,512]{1,0:T(8,128)S(1)} %get-tuple-element.35.inverse_ref.first_inverse, f32[512,512]{1,0:T(8,128)S(1)} %get-tuple-element.36.v_ref, ...), custom_call_target="tpu_custom_call" | custom-call | flops 1610612736 | bytes 8912896 | tf_op jit(solution)/shard_map/pallas_call | solution.py:603
  17.6 0.7 %collective-permute-start = (f32[1792,256]{1,0:T(8,128)S(1)}, f32[1792,256]{1,0:T(8,128)S(1)}, u32[]{:S(2)}, u32[]{:S(2)}) collective-permute-start(f32[1792,256]{1,0:T(8,128)S(1)} %get-tuple-element.41.own_ref), channel_id=1, source_target_pairs={{0,1},{1,0},{2,3},{3,2},{4,5},{5,4},{6,7},{7,6},{8,9},{9,8},{10,11... | collective-permute-start | bytes 5505032 | tf_op jit(solution)/shard_map/ppermute | solution.py:627
  18.3 7.7 %shard_map.78.inverse_ref = f32[512,512]{1,0:T(8,128)S(1)} custom-call(f32[512,256]{1,0:T(8,128)S(1)} %get-tuple-element.27.d2_own, f32[768,256]{1,0:T(8,128)S(1)} %get-tuple-element.34.keep_ref, f32[768,256]{1,0:T(8,128)S(1)} %get-tuple-element.40.came_ref), custom_call_target="tpu_custom_call" | custom-call | flops 5368709120 | bytes 3145728 | tf_op jit(solution)/shard_map/pallas_call | solution.py:603
  26.0 0.0 collective-permute-done.came_ref
  26.0 34.0 %shard_map.79 = (f32[512,256]{1,0:T(8,128)S(1)}, f32[512,256]{1,0:T(8,128)S(1)}, f32[64,512]{1,0:T(8,128)S(1)}, f32[64,2048]{1,0:T(8,128)S(1)}) custom-call(f32[512,512]{1,0:T(8,128)S(1)} %shard_map.78.inverse_ref, f32[1792,256]{1,0:T(8,128)S(1)} %get-tuple-element.41.own_ref, f32[1792,256]{1,0:T(8,128)S(1)} %collective-permute-done.came_ref, ...), custom_call_target="tpu_custom_call" | custom-call | flops 2415919104 | bytes 16515072 | tf_op jit(solution)/shard_map/pallas_call | solution.py:603
  60.0 1.2 %shard_map.80 = (f32[512,256]{1,0:T(8,128)}, f32[512,256]{1,0:T(8,128)}, f32[64,512]{1,0:T(8,128)}, f32[64,2048]{1,0:T(8,128)}) custom-call(f32[512,256]{1,0:T(8,128)S(1)} %get-tuple-element.46.refs_0_, f32[512,256]{1,0:T(8,128)S(1)} %get-tuple-element.47.refs_1_, f32[64,512]{1,0:T(8,128)S(1)} %get-tuple-element.48.refs_2_, ...), custom_call_target="tpu_custom_call" | custom-call | bytes 3407872 | tf_op jit(solution)/shard_map/pallas_call | solution.py:603
Async XLA Ops:
  17.6 8.5 %collective-permute-start = (f32[1792,256]{1,0:T(8,128)S(1)}, f32[1792,256]{1,0:T(8,128)S(1)}, u32[]{:S(2)}, u32[]{:S(2)}) collective-permute-start(f32[1792,256]{1,0:T(8,128)S(1)} %get-tuple-element.41.own_ref), channel_id=1, source_target_pairs={{0,1},{1,0},{2,3},{3,2},{4,5},{5,4},{6,7},{7,6},{8,9},{9,8},{10,11... | collective-permute-start | bytes 5505032 | tf_op jit(solution)/shard_map/ppermute | solution.py:627

commit v6 on v5

--- a/solution.py
+++ b/solution.py
@@ -15,10 +15,11 @@
 QUARTER = 128
 ROW = 4
 DIRECT = 320
-CHUNK = 96
+CHUNKS = 3
+CHUNK = 64
 LOWEST = 2.0
-TOL = 4e-6
-COARSE_TOL = 1.6e-3
+TOL = 2e-5
+COARSE_TOL = 4e-3
 NOISE = 2e-6
 FIXED_STEPS = 4
 MAX_STEPS = 40
@@ -82,8 +83,8 @@
     def correct(state):
         x = x_ref[...]
         x_parts = split(x)
-        residual = split(identity(x.shape[0]) - mul((d_ref[0], d_ref[1]), x_parts))
-        x_ref[...] = x + mul(x_parts, residual)
+        residual = identity(x.shape[0]) - mul((d_ref[0], d_ref[1]), x_parts)
+        x_ref[...] = x + jnp.dot(x_parts[0], residual.astype(bf16), preferred_element_type=f32)
         return state[0] + 1, state[1] * state[1]
 
     lax.while_loop(more(TOL), correct, (jnp.int32(0), gap + noise))
@@ -348,34 +349,35 @@
 
     hz_both[core] = small_ref[0]
     right = split(c_both[1])
-    left = split(c_both[0])
-    u_left = split(mul(inverse, split(c_both[0, mine]), NT))
+    u_right = split(mul(inverse, split(c_both[1, mine]), NT))
     arrived()
-
-    def low_rows(first, count):
-        span = slice(first, first + count)
-        low_send[span] = -mul((right[0][span], right[1][span]), u_left)
-
-    low_rows(DIRECT, N - DIRECT)
-    steps = []
-    for chunk in range(2):
-        span = pl.ds(DIRECT + chunk * CHUNK, CHUNK)
-        steps.append(remote(low_send.at[span], hops.at[0, chunk], pair, 10 + chunk, left_chip))
-
-    u_right = split(mul(inverse, split(c_both[1, mine]), NT))
+    swap_n = remote(lower.at[:N], n_ref.at[:, mine], pair, 23, partner)
 
     def diag_block(place):
         c_rows = split(c_both[1, place])
         return hw_next[place] + mul(c_rows, u_right)
 
-    corner = mine
+    def described(source, target, index, device):
+        return pltpu.make_async_remote_copy(
+            src_ref=source,
+            dst_ref=target,
+            send_sem=send_sems.at[index],
+            recv_sem=recv_sems.at[index],
+            device_id=device,
+            device_id_type=MESH,
+        )
+
+    crossing = lambda: described(diag_send.at[HALF:], diag_came.at[HALF:], 1, after)
+    handing = lambda: described(diag_came.at[HALF:], cross_came, 22, partner)
+    half_of_own = lambda: described(hw_own.at[:, HALF:], hw_came, 24, partner)
+    turn = lambda chunk: described(hops.at[2, chunk], hops.at[3, chunk], 19 + chunk, row_after)
 
     @pl.when(core == 0)
     def _():
         diag_send[HALF:] = diag_block(slice(HALF, N))
-        remote(diag_send.at[HALF:], diag_came.at[HALF:], pair, 1, after)
-
-    diag_send[:HALF] = diag_block(corner)
+        crossing().start()
+
+    diag_send[:HALF] = diag_block(mine)
     square = [
         remote(diag_send.at[span, width], diag_came.at[span, width], pair, index, after)
         for index, span, width in (
@@ -383,12 +385,25 @@
             (9, slice(0, QUARTER), slice(0, QUARTER)),
         )
     ]
+    left = split(c_both[0])
+    u_left = split(mul(inverse, split(c_both[0, mine]), NT))
+
+    def low_rows(first, count):
+        span = slice(first, first + count)
+        low_send[span] = -mul((right[0][span], right[1][span]), u_left)
+
+    low_rows(DIRECT, N - DIRECT)
+    steps = {}
+    for chunk in range(CHUNKS):
+        span = pl.ds(DIRECT + chunk * CHUNK, CHUNK)
+        steps[0, chunk] = remote(
+            low_send.at[span], hops.at[0, chunk], pair, 10 + chunk, left_chip
+        )
     lows = []
     for index, (first, count) in enumerate(((0, HALF), (HALF, DIRECT - HALF))):
         span = pl.ds(first, count)
         low_rows(first, count)
         lows.append(remote(low_send.at[span], low_came.at[span], pair, 3 + index, after))
-    swap_n = remote(lower.at[:N], n_ref.at[:, mine], pair, 19, partner)
     copies[0].wait()
     z2 = mul(split(f2[...] - (small_ref[1] + hz_both[2])), inverse)
     z2_parts = split(z2)
@@ -403,36 +418,30 @@
     y_back[...] = mul(y, n)
     later = remote(y_back, y_next, pair, 0, before)
 
-    def forward(hop):
-        for chunk in range(2):
-            steps[2 * hop + chunk].wait_recv()
-            steps.append(
-                remote(
-                    hops.at[hop, chunk], hops.at[hop + 1, chunk], pair,
-                    12 + 2 * hop + chunk, left_chip,
-                )
-            )
-
-    forward(0)
-
-    def half_of_own():
-        return pltpu.make_async_remote_copy(
-            src_ref=hw_own.at[:, HALF:],
-            dst_ref=hw_came,
-            send_sem=send_sems.at[20],
-            recv_sem=recv_sems.at[20],
-            device_id=partner,
-            device_id_type=MESH,
+    def forward(hop, chunk):
+        steps[hop, chunk].wait_recv()
+        steps[hop + 1, chunk] = remote(
+            hops.at[hop, chunk], hops.at[hop + 1, chunk], pair,
+            10 + CHUNKS * (hop + 1) + chunk, left_chip,
         )
 
-    @pl.when(core == 0)
-    def _():
-        w = split(mul(split(first_inverse[...]), split(h_ref[...])))
-        hw_own[...] = mul(split(ht_ref[...]), w)
+    forward(0, 0)
+    copies[3].wait()
+    diag_ref[...] = d0[...] - mul(left, u_left)
+
+    @pl.when(core == 0)
+    def _():
+        hw_own[...] = mul(split(first_inverse[...]), split(h_ref[...]))
+
+    forward(0, 1)
+
+    @pl.when(core == 0)
+    def _():
+        hw_own[...] = mul(split(ht_ref[...]), split(hw_own[...]))
         half_of_own().start()
         hw_came[...] = hw_own[:, :HALF]
 
-    forward(1)
+    forward(0, 2)
     later.wait_recv()
 
     @pl.when(core == 0)
@@ -449,64 +458,15 @@
     known = mul(y, left) + mul(split(y_next[...]), right)
     x2_ref[0] = z2 - mul(split(known), inverse)
     swap_x2 = remote(x2_ref.at[0], x2_ref.at[1], pair, 7, partner)
-
-    for copy in copies[3:]:
-        copy.wait()
+    copies[4].wait()
+    rhs_ref[...] = f0[...] - hz_both[0] - mul(z2_parts, left, NT)
+    forward(1, 0)
 
     @pl.when(core == 1)
     def _():
         half_of_own().wait_recv()
 
-    diag_ref[...] = d0[...] - hw_came[...] - mul(left, u_left)
-    rhs_ref[...] = f0[...] - hz_both[0] - mul(z2_parts, left, NT)
-
-    def turn(chunk):
-        return pltpu.make_async_remote_copy(
-            src_ref=hops.at[2, chunk],
-            dst_ref=hops.at[3, chunk],
-            send_sem=send_sems.at[16 + chunk],
-            recv_sem=recv_sems.at[16 + chunk],
-            device_id=row_after,
-            device_id_type=MESH,
-        )
-
-    for chunk in range(2):
-        steps[4 + chunk].wait_recv()
-
-        @pl.when(place_x == 0)
-        def _():
-            turn(chunk).start()
-
-    def crossing(device):
-        return pltpu.make_async_remote_copy(
-            src_ref=diag_send.at[HALF:],
-            dst_ref=diag_came.at[HALF:],
-            send_sem=send_sems.at[1],
-            recv_sem=recv_sems.at[1],
-            device_id=device,
-            device_id_type=MESH,
-        )
-
-    def handing():
-        return pltpu.make_async_remote_copy(
-            src_ref=diag_came.at[HALF:],
-            dst_ref=cross_came,
-            send_sem=send_sems.at[18],
-            recv_sem=recv_sems.at[18],
-            device_id=partner,
-            device_id_type=MESH,
-        )
-
-    @pl.when(core == 0)
-    def _():
-        crossing(after).wait_recv()
-        handing().start()
-
-    for copy in square:
-        copy.wait_recv()
-    diag_came[:QUARTER, QUARTER:HALF] = diag_came[QUARTER:HALF, :QUARTER].T
-    swap_corner = remote(diag_came.at[:HALF], corner_came, pair, 21, partner)
-
+    diag_ref[...] = diag_ref[...] - hw_came[...]
     swap_y.wait_recv()
     swap_x2.wait_recv()
 
@@ -515,6 +475,7 @@
         for slot in range(2):
             ys_ref[slot] = mul(split(ys_ref[slot]), split(h_ref[...]), NT)
 
+    forward(1, 1)
     v, w = split(v_ref[...]), split(first_inverse[...])
     for slot, place in ((1, rest), (0, share)):
         x_ref[slot] = (
@@ -524,6 +485,37 @@
             swap_x = remote(x_ref.at[1], x_both, pair, 8, partner)
     solution_ref[:, :N] = y_ref[...]
     solution_ref[:, 2 * N : 3 * N] = x2_ref[0]
+    forward(1, 2)
+
+    @pl.when(core == 0)
+    def _():
+        crossing().wait_recv()
+        handing().start()
+
+    for copy in square:
+        copy.wait_recv()
+    diag_came[:QUARTER, QUARTER:HALF] = diag_came[QUARTER:HALF, :QUARTER].T
+    swap_corner = remote(diag_came.at[:HALF], corner_came, pair, 25, partner)
+
+    def last_hop(chunk):
+        steps[2, chunk].wait_recv()
+
+        @pl.when(place_x == 0)
+        def _():
+            turn(chunk).start()
+
+    last_hop(0)
+    swap_x.wait_recv()
+
+    @pl.when(core == 0)
+    def _():
+        solution_ref[:, N : 2 * N] = x_ref[0]
+        solution_ref[:, 3 * N :] = x_both[...]
+
+    @pl.when(core == 1)
+    def _():
+        solution_ref[:, N : 2 * N] = x_both[...]
+        solution_ref[:, 3 * N :] = x_ref[0]
 
     m_ref[mine, mine] = diag_came[:HALF]
     swap_corner.wait_recv()
@@ -541,24 +533,14 @@
     m_ref[:HALF, HALF:] = m_ref[HALF:, :HALF].T
     applied = split(mul(split(m_ref[...]), split(n_ref[mine]), NT))
     diag_ref[...] = diag_ref[...] - mul(n, applied)
-    swap_x.wait_recv()
-
-    @pl.when(core == 0)
-    def _():
-        solution_ref[:, N : 2 * N] = x_ref[0]
-        solution_ref[:, 3 * N :] = x_both[...]
-
-    @pl.when(core == 1)
-    def _():
-        solution_ref[:, N : 2 * N] = x_both[...]
-        solution_ref[:, 3 * N :] = x_ref[0]
-
+    last_hop(1)
     lows[0].wait_recv()
     low_out[...] = mul(split(n_ref[:, :HALF]), split(low_came[:HALF]))
+    last_hop(2)
     rhs_sent.wait_recv()
     rhs_ref[...] = rhs_ref[...] - mul(split(rhs_came[...]), n, NT)
     lows[1].wait_recv()
-    for chunk in range(2):
+    for chunk in range(CHUNKS):
         span = pl.ds(DIRECT + chunk * CHUNK, CHUNK)
 
         @pl.when(place_x == 0)
@@ -572,18 +554,19 @@
 
     low_out[...] = low_out[...] + mul(split(n_ref[:, HALF:]), split(low_came[HALF:]))
     for copy in (
-        later, *square, *lows, rhs_sent, swap_y, swap_x2, swap_x, swap_n, swap_corner, *steps
+        later, *square, *lows, rhs_sent, swap_y, swap_x2, swap_x, swap_n, swap_corner,
+        *steps.values(),
     ):
         copy.wait_send()
 
     @pl.when(place_x == 0)
     def _():
-        for chunk in range(2):
+        for chunk in range(CHUNKS):
             turn(chunk).wait_send()
 
     @pl.when(core == 0)
     def _():
-        crossing(after).wait_send()
+        crossing().wait_send()
         handing().wait_send()
         half_of_own().wait_send()
 
@@ -681,14 +664,14 @@
         finals,
         [VMEM] * 4,
         [scratch(2, *full), scratch(*half), scratch(3, *small), scratch(*half), scratch(*half),
-         scratch(4, 2, CHUNK, HALF), scratch(*half), scratch(*small), scratch(*half),
+         scratch(4, CHUNKS, CHUNK, HALF), scratch(*half), scratch(*small), scratch(*half),
          scratch(*quarter),
          scratch(*quarter), scratch(*full), scratch(*full), scratch(*full), scratch(*half),
          scratch(*small),
          scratch(*half), scratch(*small), scratch(*small), scratch(*small), scratch(*small),
          scratch(*small), scratch(*small), scratch(2, *small), scratch(2, *small),
          scratch(2, *small), scratch(*small),
-         copy_sems(5), copy_sems(22), copy_sems(22)],
+         copy_sems(5), copy_sems(26), copy_sems(26)],
         2 * N**3 * 9,
         (inverse2, pack, pack_came, hw, tails, inverse, v, z, h, ht,
          diag, lower, right_side, coarse_sol),

time: 61.5 us -> 60.4 us (0.982)
  Pallas kernels: 59.9 us -> 58.8 us
    pallas_call x6, Pallas kernels: 59.9 us -> 58.8 us  [call(): pl.pallas_call(body, out_shape=outs, in_specs=in_specs, out_specs=out_spe...]
  transfers between devices with their start and end apart: 1 -> 1, of which waited for: 0 -> 0; matrix products, arithmetic and copies ran while one was open for 0% -> 0% of each run, Pallas kernels for 13% -> 12%
where the time goes in v6:
time: 60.4 us; the launch traced here: 60.3 us
  Pallas kernels  58.8 us (97%)
  between operations  0.84 us (1%)
  starting transfers between devices  0.71 us (1%)
    pallas_call x6, Pallas kernels, call(): pl.pallas_call(body, out_shape=outs, in_specs=in_specs, out_specs=out_spe...  58.8 us
  transfers between devices with their start and end apart: 1, of which 0 were waited for; matrix products, arithmetic and copies ran while one was open for 0% of the time, Pallas kernels for 12%

profile of v6, /device:TPU:1, one launch (start us, length us, event | category | flops | bytes accessed | tf_op | source)
XLA Modules:
  0.0 60.3 jit_solution(6345914312565417854)
XLA Ops:
  0.6 6.4 %shard_map.75 = (f32[512,256]{1,0:T(8,128)S(1)}, f32[256,256]{1,0:T(8,128)S(1)}, f32[512,512]{1,0:T(8,128)S(1)}, f32[512,512]{1,0:T(8,128)S(1)}, f32[128,512]{1,...) custom-call(f32[2048,256]{1,0:T(8,128)} %diag.3, ...), custom_call_target="tpu_custom_call" | custom-call | flops 1006632960 | bytes 8916992 | tf_op jit(solution)/shard_map/pallas_call | solution.py:586
  7.0 7.8 %shard_map.76 = (f32[512,512]{1,0:T(8,128)S(1)}, f32[512,512]{1,0:T(8,128)S(1)}, f32[768,256]{1,0:T(8,128)S(1)}, f32[768,256]{1,0:T(8,128)S(1)}) custom-call(f32[512,256]{1,0:T(8,128)S(1)} %get-tuple-element.28.d_own, f32[256,256]{1,0:T(8,128)S(1)} %get-tuple-element.29.d_other, f32[512,512]{1,0:T(8,128)S(1)} %get-tuple-element.30.g_whole, ...), custom_call_target="tpu_custom_call" | custom-call | flops 5368709120 | bytes 6557696 | tf_op jit(solution)/shard_map/pallas_call | solution.py:586
  14.8 2.3 %shard_map.77 = (f32[768,256]{1,0:T(8,128)S(1)}, f32[512,512]{1,0:T(8,128)S(1)}, f32[128,512]{1,0:T(8,128)S(1)}, f32[1792,256]{1,0:T(8,128)S(1)}, f32[512,256]{1,0:T(8,128)S(1)}, /*index=5*/f32[2,64,512]{2,1,0:T(8,128)S(1)}) custom-call(f32[512,512]{1,0:T(8,128)S(1)} %get-tuple-element.35.inverse_ref.first_inverse, f32[512,512]{1,0:T(8,128)S(1)} %get-tuple-element.36.v_ref, ...), custom_call_target="tpu_custom_call" | custom-call | flops 1610612736 | bytes 8912896 | tf_op jit(solution)/shard_map/pallas_call | solution.py:586
  17.2 0.7 %collective-permute-start = (f32[1792,256]{1,0:T(8,128)S(1)}, f32[1792,256]{1,0:T(8,128)S(1)}, u32[]{:S(2)}, u32[]{:S(2)}) collective-permute-start(f32[1792,256]{1,0:T(8,128)S(1)} %get-tuple-element.41.own_ref), channel_id=1, source_target_pairs={{0,1},{1,0},{2,3},{3,2},{4,5},{5,4},{6,7},{7,6},{8,9},{9,8},{10,11... | collective-permute-start | bytes 5505032 | tf_op jit(solution)/shard_map/ppermute | solution.py:610
  17.9 7.4 %shard_map.78.inverse_ref = f32[512,512]{1,0:T(8,128)S(1)} custom-call(f32[512,256]{1,0:T(8,128)S(1)} %get-tuple-element.27.d2_own, f32[768,256]{1,0:T(8,128)S(1)} %get-tuple-element.34.keep_ref, f32[768,256]{1,0:T(8,128)S(1)} %get-tuple-element.40.came_ref), custom_call_target="tpu_custom_call" | custom-call | flops 5368709120 | bytes 3145728 | tf_op jit(solution)/shard_map/pallas_call | solution.py:586
  25.2 0.0 collective-permute-done.came_ref
  25.3 33.7 %shard_map.79 = (f32[512,256]{1,0:T(8,128)S(1)}, f32[512,256]{1,0:T(8,128)S(1)}, f32[64,512]{1,0:T(8,128)S(1)}, f32[64,2048]{1,0:T(8,128)S(1)}) custom-call(f32[512,512]{1,0:T(8,128)S(1)} %shard_map.78.inverse_ref, f32[1792,256]{1,0:T(8,128)S(1)} %get-tuple-element.41.own_ref, f32[1792,256]{1,0:T(8,128)S(1)} %collective-permute-done.came_ref, ...), custom_call_target="tpu_custom_call" | custom-call | flops 2415919104 | bytes 16515072 | tf_op jit(solution)/shard_map/pallas_call | solution.py:586
  58.9 1.2 %shard_map.80 = (f32[512,256]{1,0:T(8,128)}, f32[512,256]{1,0:T(8,128)}, f32[64,512]{1,0:T(8,128)}, f32[64,2048]{1,0:T(8,128)}) custom-call(f32[512,256]{1,0:T(8,128)S(1)} %get-tuple-element.46.refs_0_, f32[512,256]{1,0:T(8,128)S(1)} %get-tuple-element.47.refs_1_, f32[64,512]{1,0:T(8,128)S(1)} %get-tuple-element.48.refs_2_, ...), custom_call_target="tpu_custom_call" | custom-call | bytes 3407872 | tf_op jit(solution)/shard_map/pallas_call | solution.py:586
Async XLA Ops:
  17.2 8.1 %collective-permute-start = (f32[1792,256]{1,0:T(8,128)S(1)}, f32[1792,256]{1,0:T(8,128)S(1)}, u32[]{:S(2)}, u32[]{:S(2)}) collective-permute-start(f32[1792,256]{1,0:T(8,128)S(1)} %get-tuple-element.41.own_ref), channel_id=1, source_target_pairs={{0,1},{1,0},{2,3},{3,2},{4,5},{5,4},{6,7},{7,6},{8,9},{9,8},{10,11... | collective-permute-start | bytes 5505032 | tf_op jit(solution)/shard_map/ppermute | solution.py:610

commit v7 on v6

--- a/solution.py
+++ b/solution.py
@@ -14,9 +14,9 @@
 SHARE = 64
 QUARTER = 128
 ROW = 4
-DIRECT = 320
-CHUNKS = 3
-CHUNK = 64
+DIRECT = 352
+CHUNKS = 2
+CHUNK = 80
 LOWEST = 2.0
 TOL = 2e-5
 COARSE_TOL = 4e-3
@@ -52,42 +52,55 @@
     return gain, 0.5 * gain * gap * gap
 
 
-def newton_start(block, x_ref, t_ref, d_ref):
+def keep_state(t, x, tx_ref, z_ref):
+    n = t.shape[0]
+    tx_ref[0, :n], tx_ref[1, :n] = split(t)
+    tx_ref[0, n:], tx_ref[1, n:] = split(x)
+    z_ref[0], z_ref[1] = split(2.0 * identity(n) - t)
+
+
+def newton_start(block, tx_ref, z_ref, d_ref):
     d_ref[0], d_ref[1] = split(block)
     top = jnp.maximum(jnp.max(jnp.sum(jnp.abs(block), axis=0, keepdims=True)), LOWEST)
     lead = 2.0 / (top + LOWEST)
     gain, gap = norm_steps((top - LOWEST) / (top + LOWEST))
     rest = 2.0 * identity(block.shape[0]) - lead * block
-    x_ref[...] = (gain * lead) * rest
-    t_ref[...] = (gain * lead) * mul((d_ref[0], d_ref[1]), split(rest))
+    t = (gain * lead) * mul((d_ref[0], d_ref[1]), split(rest))
+    keep_state(t, (gain * lead) * rest, tx_ref, z_ref)
     return gap
 
 
-def newton_step(gap, x_ref, t_ref):
+def newton_step(gap, tx_ref, z_ref):
     gain, gap = norm_steps(gap)
-    n = x_ref.shape[0]
-    rest = split(2.0 * identity(n) - t_ref[...])
-    both = mul(split(jnp.concatenate([t_ref[...], x_ref[...]], axis=0)), rest)
-    t_ref[...] = gain * both[:n]
-    x_ref[...] = gain * both[n:]
+    n = z_ref.shape[1]
+    both = gain * mul((tx_ref[0], tx_ref[1]), (z_ref[0], z_ref[1]))
+    keep_state(both[:n], both[n:], tx_ref, z_ref)
     return gap
 
 
-def newton_finish(gap, x_ref, t_ref, d_ref, noise):
+def newton_finish(gap, x_ref, tx_ref, z_ref, d_ref, noise):
+    n = z_ref.shape[1]
+
     def more(limit):
         return lambda state: jnp.logical_and(state[1] > limit, state[0] < MAX_STEPS)
 
-    step = lambda state: (state[0] + 1, newton_step(state[1], x_ref, t_ref))
+    step = lambda state: (state[0] + 1, newton_step(state[1], tx_ref, z_ref))
     _, gap = lax.while_loop(more(COARSE_TOL), step, (jnp.int32(0), gap))
 
-    def correct(state):
+    def correct(x, x_parts):
+        residual = identity(n) - mul((d_ref[0], d_ref[1]), x_parts)
+        x_ref[...] = x + jnp.dot(x_parts[0], residual.astype(bf16), preferred_element_type=f32)
+
+    high, low = tx_ref[0, n:], tx_ref[1, n:]
+    correct(high.astype(f32) + low.astype(f32), (high, low))
+
+    def again(state):
         x = x_ref[...]
-        x_parts = split(x)
-        residual = identity(x.shape[0]) - mul((d_ref[0], d_ref[1]), x_parts)
-        x_ref[...] = x + jnp.dot(x_parts[0], residual.astype(bf16), preferred_element_type=f32)
+        correct(x, split(x))
         return state[0] + 1, state[1] * state[1]
 
-    lax.while_loop(more(TOL), correct, (jnp.int32(0), gap + noise))
+    left = gap + noise
+    lax.while_loop(more(TOL), again, (jnp.int32(0), left * left))
     return x_ref[...]
 
 
@@ -95,9 +108,9 @@
     return jnp.max(jnp.sum(jnp.abs(block), axis=0, keepdims=True)) * NOISE
 
 
-def newton(block, x_ref, t_ref, d_ref):
-    gap = newton_start(block, x_ref, t_ref, d_ref)
-    return newton_finish(gap, x_ref, t_ref, d_ref, noise_of(block))
+def newton(block, x_ref, tx_ref, z_ref, d_ref):
+    gap = newton_start(block, tx_ref, z_ref, d_ref)
+    return newton_finish(gap, x_ref, tx_ref, z_ref, d_ref, noise_of(block))
 
 
 def places():
@@ -111,12 +124,12 @@
     )
 
 
-def invert(first, cross_block, last_block, out_ref, x_ref, t_ref, d_ref):
+def invert(first, cross_block, last_block, out_ref, *state):
     _, mine, other, _, _ = places()
     cross = split(cross_block)
     lift = split(mul(cross, split(first)))
     out_ref[mine, mine] = first
-    last = newton(last_block() - mul(lift, cross, NT), x_ref, t_ref, d_ref)
+    last = newton(last_block() - mul(lift, cross, NT), *state)
     low = -mul(split(last), lift)
     up = low.T
     out_ref[other, other] = last
@@ -162,7 +175,7 @@
 
 def partners(
     diag, lower, right_side,
-    d_own, d_other, g_ref, h_ref, f_ref, d2_own, x_ref, t_ref, gap_ref,
+    d_own, d_other, g_ref, h_ref, f_ref, d2_own, tx_ref, z_ref, gap_ref,
     d_ref, sems, send_sems, recv_sems,
 ):
     core, mine, other, share, rest = places()
@@ -205,8 +218,8 @@
         outer().start()
 
     copies[0].wait()
-    gap = newton_start(d_own[mine], x_ref, t_ref, d_ref)
-    gap = lax.fori_loop(0, FIXED_STEPS, lambda _, gap: newton_step(gap, x_ref, t_ref), gap)
+    gap = newton_start(d_own[mine], tx_ref, z_ref, d_ref)
+    gap = lax.fori_loop(0, FIXED_STEPS, lambda _, gap: newton_step(gap, tx_ref, z_ref), gap)
     gap_ref[...] = jnp.full(gap_ref.shape, gap, f32)
     for copy in copies[1:]:
         copy.wait()
@@ -223,17 +236,18 @@
 
 
 def level_one(
-    d_own, d_other, g_whole, d2_own, first_x, first_t, gap_in,
+    d_own, d_other, g_whole, d2_own, first_tx, first_z, gap_in,
     inverse_ref, v_ref, send_ref, keep_ref,
-    gv_ref, g_ref, x_ref, t_ref, d_ref,
+    gv_ref, g_ref, x_ref, tx_ref, z_ref, d_ref,
 ):
     core, mine, other, share, rest = places()
-    x_ref[...] = first_x[...]
-    t_ref[...] = first_t[...]
+    tx_ref[...] = first_tx[...]
+    z_ref[...] = first_z[...]
     block = d_own[mine]
     d_ref[0], d_ref[1] = split(block)
-    first = newton_finish(jnp.max(gap_in[...]), x_ref, t_ref, d_ref, noise_of(block))
-    invert(first, d_own[other], lambda: d_other[...], inverse_ref, x_ref, t_ref, d_ref)
+    state = (x_ref, tx_ref, z_ref, d_ref)
+    first = newton_finish(jnp.max(gap_in[...]), *state, noise_of(block))
+    invert(first, d_own[other], lambda: d_other[...], inverse_ref, *state)
 
     @pl.when(core == 0)
     def _():
@@ -292,12 +306,12 @@
     swapped.wait()
 
 
-def level_two(d2_own, keep_ref, came_ref, inverse_ref, d_own, x_ref, t_ref, d_ref):
+def level_two(d2_own, keep_ref, came_ref, inverse_ref, d_own, *state):
     core, mine, other, share, rest = places()
     d_own[...] = d2_own[...] - (keep_ref[:N] + came_ref[:N])
     last_block = lambda: -(keep_ref[N:] + came_ref[N:])
-    first = newton(d_own[mine], x_ref, t_ref, d_ref)
-    invert(first, d_own[other], last_block, inverse_ref, x_ref, t_ref, d_ref)
+    first = newton(d_own[mine], *state)
+    invert(first, d_own[other], last_block, inverse_ref, *state)
 
 
 def survivors(
@@ -349,9 +363,30 @@
 
     hz_both[core] = small_ref[0]
     right = split(c_both[1])
+    u_left = split(mul(inverse, split(c_both[0, mine]), NT))
+    arrived()
+
+    def low_rows(first, count):
+        span = slice(first, first + count)
+        low_send[span] = -mul((right[0][span], right[1][span]), u_left)
+
+    low_rows(DIRECT, N - DIRECT)
+    steps = {}
+    for chunk in range(CHUNKS):
+        span = pl.ds(DIRECT + chunk * CHUNK, CHUNK)
+        steps[0, chunk] = remote(
+            low_send.at[span], hops.at[0, chunk], pair, 10 + chunk, left_chip
+        )
+    lows = []
+
+    def straight(index, first, count):
+        span = pl.ds(first, count)
+        low_rows(first, count)
+        lows.append(remote(low_send.at[span], low_came.at[span], pair, 3 + index, after))
+
+    straight(0, 0, HALF)
+    swap_n = remote(lower.at[:N], n_ref.at[:, mine], pair, 23, partner)
     u_right = split(mul(inverse, split(c_both[1, mine]), NT))
-    arrived()
-    swap_n = remote(lower.at[:N], n_ref.at[:, mine], pair, 23, partner)
 
     def diag_block(place):
         c_rows = split(c_both[1, place])
@@ -385,25 +420,7 @@
             (9, slice(0, QUARTER), slice(0, QUARTER)),
         )
     ]
-    left = split(c_both[0])
-    u_left = split(mul(inverse, split(c_both[0, mine]), NT))
-
-    def low_rows(first, count):
-        span = slice(first, first + count)
-        low_send[span] = -mul((right[0][span], right[1][span]), u_left)
-
-    low_rows(DIRECT, N - DIRECT)
-    steps = {}
-    for chunk in range(CHUNKS):
-        span = pl.ds(DIRECT + chunk * CHUNK, CHUNK)
-        steps[0, chunk] = remote(
-            low_send.at[span], hops.at[0, chunk], pair, 10 + chunk, left_chip
-        )
-    lows = []
-    for index, (first, count) in enumerate(((0, HALF), (HALF, DIRECT - HALF))):
-        span = pl.ds(first, count)
-        low_rows(first, count)
-        lows.append(remote(low_send.at[span], low_came.at[span], pair, 3 + index, after))
+    straight(1, HALF, DIRECT - HALF)
     copies[0].wait()
     z2 = mul(split(f2[...] - (small_ref[1] + hz_both[2])), inverse)
     z2_parts = split(z2)
@@ -427,6 +444,7 @@
 
     forward(0, 0)
     copies[3].wait()
+    left = split(c_both[0])
     diag_ref[...] = d0[...] - mul(left, u_left)
 
     @pl.when(core == 0)
@@ -441,7 +459,6 @@
         half_of_own().start()
         hw_came[...] = hw_own[:, :HALF]
 
-    forward(0, 2)
     later.wait_recv()
 
     @pl.when(core == 0)
@@ -485,7 +502,6 @@
             swap_x = remote(x_ref.at[1], x_both, pair, 8, partner)
     solution_ref[:, :N] = y_ref[...]
     solution_ref[:, 2 * N : 3 * N] = x2_ref[0]
-    forward(1, 2)
 
     @pl.when(core == 0)
     def _():
@@ -536,7 +552,6 @@
     last_hop(1)
     lows[0].wait_recv()
     low_out[...] = mul(split(n_ref[:, :HALF]), split(low_came[:HALF]))
-    last_hop(2)
     rhs_sent.wait_recv()
     rhs_ref[...] = rhs_ref[...] - mul(split(rhs_came[...]), n, NT)
     lows[1].wait_recv()
@@ -595,7 +610,8 @@
 
 
 def newton_scratch():
-    return [pltpu.VMEM((HALF, HALF), f32)] * 2 + [pltpu.VMEM((2, HALF, HALF), bf16)]
+    pair = pltpu.VMEM((2, HALF, HALF), bf16)
+    return [pltpu.VMEM((HALF, HALF), f32), pltpu.VMEM((2, N, HALF), bf16), pair, pair]
 
 
 def copy_sems(count):
@@ -610,11 +626,12 @@
     swap = lambda x: lax.ppermute(x, "rhs", [(0, 1), (1, 0)])
     full, half, quarter = (N, N), (N, HALF), (HALF, HALF)
     small, scratch = (SHARE, N), lambda *dims: pltpu.VMEM(dims, f32)
-    d_own, d_other, g, h, f, d2_own, first_x, first_t, gap = call(
+    d_own, d_other, g, h, f, d2_own, first_tx, first_z, gap = call(
         partners,
         [HBM] * 3,
         [shape(*half), shape(*quarter), shape(*full), shape(*full), shape(RHS, N), shape(*half),
-         shape(*quarter), shape(*quarter), shape(8, 128)],
+         jax.ShapeDtypeStruct((2, N, HALF), bf16), jax.ShapeDtypeStruct((2, HALF, HALF), bf16),
+         shape(8, 128)],
         [VMEM] * 9,
         [pltpu.VMEM((2, HALF, HALF), bf16), copy_sems(5), copy_sems(4), copy_sems(4)],
         2 * HALF**3 * 30,
@@ -630,7 +647,7 @@
         [VMEM] * 4,
         [scratch(*full), scratch(*full)] + newton_scratch(),
         2 * N**3 * 20,
-        (d_own, d_other, g, d2_own, first_x, first_t, gap),
+        (d_own, d_other, g, d2_own, first_tx, first_z, gap),
         28,
     )
     came, ht, z, pack, hw, tails = call(

time: 60.4 us -> 61.3 us (1.015)
  Pallas kernels: 58.8 us -> 59.7 us
    pallas_call x6, Pallas kernels: 58.8 us -> 59.7 us  [call(): pl.pallas_call(body, out_shape=outs, in_specs=in_specs, out_specs=out_spe...]
where the time goes in v7:
time: 61.3 us; the launch traced here: 61.2 us
  Pallas kernels  59.7 us (97%)
  between operations  0.84 us (1%)
  starting transfers between devices  0.69 us (1%)
    pallas_call x6, Pallas kernels, call(): pl.pallas_call(body, out_shape=outs, in_specs=in_specs, out_specs=out_spe...  59.7 us
  transfers between devices with their start and end apart: 1, of which 0 were waited for; matrix products, arithmetic and copies ran while one was open for 0% of the time, Pallas kernels for 12%

profile of v7, /device:TPU:1, one launch (start us, length us, event | category | flops | bytes accessed | tf_op | source)
XLA Modules:
  0.0 61.2 jit_solution(17494115107919243418)
XLA Ops:
  0.6 6.4 %shard_map.75 = (f32[512,256]{1,0:T(8,128)S(1)}, f32[256,256]{1,0:T(8,128)S(1)}, f32[512,512]{1,0:T(8,128)S(1)}, f32[512,512]{1,0:T(8,128)S(1)}, f32[128,512]{1,...) custom-call(f32[2048,256]{1,0:T(8,128)} %diag.3, ...), custom_call_target="tpu_custom_call" | custom-call | flops 1006632960 | bytes 9965568 | tf_op jit(solution)/shard_map/pallas_call | solution.py:601
  7.0 7.8 %shard_map.76 = (f32[512,512]{1,0:T(8,128)S(1)}, f32[512,512]{1,0:T(8,128)S(1)}, f32[768,256]{1,0:T(8,128)S(1)}, f32[768,256]{1,0:T(8,128)S(1)}) custom-call(f32[512,256]{1,0:T(8,128)S(1)} %get-tuple-element.28.d_own, f32[256,256]{1,0:T(8,128)S(1)} %get-tuple-element.29.d_other, f32[512,512]{1,0:T(8,128)S(1)} %get-tuple-element.30.g_whole, ...), custom_call_target="tpu_custom_call" | custom-call | flops 5368709120 | bytes 7606272 | tf_op jit(solution)/shard_map/pallas_call | solution.py:601
  14.9 2.3 %shard_map.77 = (f32[768,256]{1,0:T(8,128)S(1)}, f32[512,512]{1,0:T(8,128)S(1)}, f32[128,512]{1,0:T(8,128)S(1)}, f32[1792,256]{1,0:T(8,128)S(1)}, f32[512,256]{1,0:T(8,128)S(1)}, /*index=5*/f32[2,64,512]{2,1,0:T(8,128)S(1)}) custom-call(f32[512,512]{1,0:T(8,128)S(1)} %get-tuple-element.35.inverse_ref.first_inverse, f32[512,512]{1,0:T(8,128)S(1)} %get-tuple-element.36.v_ref, ...), custom_call_target="tpu_custom_call" | custom-call | flops 1610612736 | bytes 8912896 | tf_op jit(solution)/shard_map/pallas_call | solution.py:601
  17.2 0.7 %collective-permute-start = (f32[1792,256]{1,0:T(8,128)S(1)}, f32[1792,256]{1,0:T(8,128)S(1)}, u32[]{:S(2)}, u32[]{:S(2)}) collective-permute-start(f32[1792,256]{1,0:T(8,128)S(1)} %get-tuple-element.41.own_ref), channel_id=1, source_target_pairs={{0,1},{1,0},{2,3},{3,2},{4,5},{5,4},{6,7},{7,6},{8,9},{9,8},{10,11... | collective-permute-start | bytes 5505032 | tf_op jit(solution)/shard_map/ppermute | solution.py:626
  17.9 7.5 %shard_map.78.inverse_ref = f32[512,512]{1,0:T(8,128)S(1)} custom-call(f32[512,256]{1,0:T(8,128)S(1)} %get-tuple-element.27.d2_own, f32[768,256]{1,0:T(8,128)S(1)} %get-tuple-element.34.keep_ref, f32[768,256]{1,0:T(8,128)S(1)} %get-tuple-element.40.came_ref), custom_call_target="tpu_custom_call" | custom-call | flops 5368709120 | bytes 3145728 | tf_op jit(solution)/shard_map/pallas_call | solution.py:601
  25.3 0.0 collective-permute-done.came_ref
  25.4 34.5 %shard_map.79 = (f32[512,256]{1,0:T(8,128)S(1)}, f32[512,256]{1,0:T(8,128)S(1)}, f32[64,512]{1,0:T(8,128)S(1)}, f32[64,2048]{1,0:T(8,128)S(1)}) custom-call(f32[512,512]{1,0:T(8,128)S(1)} %shard_map.78.inverse_ref, f32[1792,256]{1,0:T(8,128)S(1)} %get-tuple-element.41.own_ref, f32[1792,256]{1,0:T(8,128)S(1)} %collective-permute-done.came_ref, ...), custom_call_target="tpu_custom_call" | custom-call | flops 2415919104 | bytes 16515072 | tf_op jit(solution)/shard_map/pallas_call | solution.py:601
  59.8 1.2 %shard_map.80 = (f32[512,256]{1,0:T(8,128)}, f32[512,256]{1,0:T(8,128)}, f32[64,512]{1,0:T(8,128)}, f32[64,2048]{1,0:T(8,128)}) custom-call(f32[512,256]{1,0:T(8,128)S(1)} %get-tuple-element.46.refs_0_, f32[512,256]{1,0:T(8,128)S(1)} %get-tuple-element.47.refs_1_, f32[64,512]{1,0:T(8,128)S(1)} %get-tuple-element.48.refs_2_, ...), custom_call_target="tpu_custom_call" | custom-call | bytes 3407872 | tf_op jit(solution)/shard_map/pallas_call | solution.py:601
Async XLA Ops:
  17.2 8.1 %collective-permute-start = (f32[1792,256]{1,0:T(8,128)S(1)}, f32[1792,256]{1,0:T(8,128)S(1)}, u32[]{:S(2)}, u32[]{:S(2)}) collective-permute-start(f32[1792,256]{1,0:T(8,128)S(1)} %get-tuple-element.41.own_ref), channel_id=1, source_target_pairs={{0,1},{1,0},{2,3},{3,2},{4,5},{5,4},{6,7},{7,6},{8,9},{9,8},{10,11... | collective-permute-start | bytes 5505032 | tf_op jit(solution)/shard_map/ppermute | solution.py:626

commit v8 on v6

--- a/solution.py
+++ b/solution.py
@@ -349,13 +349,12 @@
 
     hz_both[core] = small_ref[0]
     right = split(c_both[1])
-    u_right = split(mul(inverse, split(c_both[1, mine]), NT))
+    u_left = split(mul(inverse, split(c_both[0, mine]), NT))
     arrived()
-    swap_n = remote(lower.at[:N], n_ref.at[:, mine], pair, 23, partner)
-
-    def diag_block(place):
-        c_rows = split(c_both[1, place])
-        return hw_next[place] + mul(c_rows, u_right)
+
+    def low_rows(first, count):
+        span = slice(first, first + count)
+        low_send[span] = -mul((right[0][span], right[1][span]), u_left)
 
     def described(source, target, index, device):
         return pltpu.make_async_remote_copy(
@@ -367,10 +366,39 @@
             device_id_type=MESH,
         )
 
+    low_rows(DIRECT, N - DIRECT)
+    around = lambda chunk: low_send.at[pl.ds(DIRECT + chunk * CHUNK, CHUNK)]
+    first_hop = lambda chunk, source: described(source, hops.at[0, chunk], 10 + chunk, left_chip)
+    turn = lambda chunk: described(around(chunk), hops.at[3, chunk], 19 + chunk, row_after)
+
+    @pl.when(place_x == ROW - 1)
+    def _():
+        for chunk in range(CHUNKS):
+            turn(chunk).start()
+
+    @pl.when(place_x != ROW - 1)
+    def _():
+        for chunk in range(CHUNKS):
+            first_hop(chunk, around(chunk)).start()
+
+    lows = []
+
+    def straight(index, first, count):
+        span = pl.ds(first, count)
+        low_rows(first, count)
+        lows.append(remote(low_send.at[span], low_came.at[span], pair, 3 + index, after))
+
+    straight(0, 0, HALF)
+    swap_n = remote(lower.at[:N], n_ref.at[:, mine], pair, 23, partner)
+    u_right = split(mul(inverse, split(c_both[1, mine]), NT))
+
+    def diag_block(place):
+        c_rows = split(c_both[1, place])
+        return hw_next[place] + mul(c_rows, u_right)
+
     crossing = lambda: described(diag_send.at[HALF:], diag_came.at[HALF:], 1, after)
     handing = lambda: described(diag_came.at[HALF:], cross_came, 22, partner)
     half_of_own = lambda: described(hw_own.at[:, HALF:], hw_came, 24, partner)
-    turn = lambda chunk: described(hops.at[2, chunk], hops.at[3, chunk], 19 + chunk, row_after)
 
     @pl.when(core == 0)
     def _():
@@ -385,25 +413,14 @@
             (9, slice(0, QUARTER), slice(0, QUARTER)),
         )
     ]
-    left = split(c_both[0])
-    u_left = split(mul(inverse, split(c_both[0, mine]), NT))
-
-    def low_rows(first, count):
-        span = slice(first, first + count)
-        low_send[span] = -mul((right[0][span], right[1][span]), u_left)
-
-    low_rows(DIRECT, N - DIRECT)
-    steps = {}
-    for chunk in range(CHUNKS):
-        span = pl.ds(DIRECT + chunk * CHUNK, CHUNK)
-        steps[0, chunk] = remote(
-            low_send.at[span], hops.at[0, chunk], pair, 10 + chunk, left_chip
-        )
-    lows = []
-    for index, (first, count) in enumerate(((0, HALF), (HALF, DIRECT - HALF))):
-        span = pl.ds(first, count)
-        low_rows(first, count)
-        lows.append(remote(low_send.at[span], low_came.at[span], pair, 3 + index, after))
+    straight(1, HALF, DIRECT - HALF)
+
+    @pl.when(place_x == ROW - 1)
+    def _():
+        for chunk in range(CHUNKS):
+            turn(chunk).wait_recv()
+            first_hop(chunk, hops.at[3, chunk]).start()
+
     copies[0].wait()
     z2 = mul(split(f2[...] - (small_ref[1] + hz_both[2])), inverse)
     z2_parts = split(z2)
@@ -418,6 +435,8 @@
     y_back[...] = mul(y, n)
     later = remote(y_back, y_next, pair, 0, before)
 
+    steps = {(0, chunk): first_hop(chunk, around(chunk)) for chunk in range(CHUNKS)}
+
     def forward(hop, chunk):
         steps[hop, chunk].wait_recv()
         steps[hop + 1, chunk] = remote(
@@ -427,6 +446,7 @@
 
     forward(0, 0)
     copies[3].wait()
+    left = split(c_both[0])
     diag_ref[...] = d0[...] - mul(left, u_left)
 
     @pl.when(core == 0)
@@ -497,14 +517,6 @@
     diag_came[:QUARTER, QUARTER:HALF] = diag_came[QUARTER:HALF, :QUARTER].T
     swap_corner = remote(diag_came.at[:HALF], corner_came, pair, 25, partner)
 
-    def last_hop(chunk):
-        steps[2, chunk].wait_recv()
-
-        @pl.when(place_x == 0)
-        def _():
-            turn(chunk).start()
-
-    last_hop(0)
     swap_x.wait_recv()
 
     @pl.when(core == 0)
@@ -533,24 +545,14 @@
     m_ref[:HALF, HALF:] = m_ref[HALF:, :HALF].T
     applied = split(mul(split(m_ref[...]), split(n_ref[mine]), NT))
     diag_ref[...] = diag_ref[...] - mul(n, applied)
-    last_hop(1)
     lows[0].wait_recv()
     low_out[...] = mul(split(n_ref[:, :HALF]), split(low_came[:HALF]))
-    last_hop(2)
     rhs_sent.wait_recv()
     rhs_ref[...] = rhs_ref[...] - mul(split(rhs_came[...]), n, NT)
     lows[1].wait_recv()
     for chunk in range(CHUNKS):
-        span = pl.ds(DIRECT + chunk * CHUNK, CHUNK)
-
-        @pl.when(place_x == 0)
-        def _():
-            turn(chunk).wait_recv()
-            low_came[span] = hops[3, chunk]
-
-        @pl.when(place_x != 0)
-        def _():
-            low_came[span] = hops[2, chunk]
+        steps[2, chunk].wait_recv()
+        low_came[pl.ds(DIRECT + chunk * CHUNK, CHUNK)] = hops[2, chunk]
 
     low_out[...] = low_out[...] + mul(split(n_ref[:, HALF:]), split(low_came[HALF:]))
     for copy in (
@@ -559,7 +561,7 @@
     ):
         copy.wait_send()
 
-    @pl.when(place_x == 0)
+    @pl.when(place_x == ROW - 1)
     def _():
         for chunk in range(CHUNKS):
             turn(chunk).wait_send()

time: 60.4 us -> 63.8 us (1.056)
  Pallas kernels: 58.8 us -> 62.1 us
    pallas_call x6, Pallas kernels: 58.8 us -> 62.1 us  [call(): pl.pallas_call(body, out_shape=outs, in_specs=in_specs, out_specs=out_spe...]
where the time goes in v8:
time: 63.8 us; the launch traced here: 63.7 us
  Pallas kernels  62.1 us (97%)
  between operations  0.84 us (1%)
  starting transfers between devices  0.71 us (1%)
    pallas_call x6, Pallas kernels, call(): pl.pallas_call(body, out_shape=outs, in_specs=in_specs, out_specs=out_spe...  62.1 us
  transfers between devices with their start and end apart: 1, of which 0 were waited for; matrix products, arithmetic and copies ran while one was open for 0% of the time, Pallas kernels for 12%

profile of v8, /device:TPU:1, one launch (start us, length us, event | category | flops | bytes accessed | tf_op | source)
XLA Modules:
  0.0 63.7 jit_solution(16788479430567708550)
XLA Ops:
  0.6 6.4 %shard_map.75 = (f32[512,256]{1,0:T(8,128)S(1)}, f32[256,256]{1,0:T(8,128)S(1)}, f32[512,512]{1,0:T(8,128)S(1)}, f32[512,512]{1,0:T(8,128)S(1)}, f32[128,512]{1,...) custom-call(f32[2048,256]{1,0:T(8,128)} %diag.3, ...), custom_call_target="tpu_custom_call" | custom-call | flops 1006632960 | bytes 8916992 | tf_op jit(solution)/shard_map/pallas_call | solution.py:588
  7.0 7.8 %shard_map.76 = (f32[512,512]{1,0:T(8,128)S(1)}, f32[512,512]{1,0:T(8,128)S(1)}, f32[768,256]{1,0:T(8,128)S(1)}, f32[768,256]{1,0:T(8,128)S(1)}) custom-call(f32[512,256]{1,0:T(8,128)S(1)} %get-tuple-element.28.d_own, f32[256,256]{1,0:T(8,128)S(1)} %get-tuple-element.29.d_other, f32[512,512]{1,0:T(8,128)S(1)} %get-tuple-element.30.g_whole, ...), custom_call_target="tpu_custom_call" | custom-call | flops 5368709120 | bytes 6557696 | tf_op jit(solution)/shard_map/pallas_call | solution.py:588
  14.8 2.3 %shard_map.77 = (f32[768,256]{1,0:T(8,128)S(1)}, f32[512,512]{1,0:T(8,128)S(1)}, f32[128,512]{1,0:T(8,128)S(1)}, f32[1792,256]{1,0:T(8,128)S(1)}, f32[512,256]{1,0:T(8,128)S(1)}, /*index=5*/f32[2,64,512]{2,1,0:T(8,128)S(1)}) custom-call(f32[512,512]{1,0:T(8,128)S(1)} %get-tuple-element.35.inverse_ref.first_inverse, f32[512,512]{1,0:T(8,128)S(1)} %get-tuple-element.36.v_ref, ...), custom_call_target="tpu_custom_call" | custom-call | flops 1610612736 | bytes 8912896 | tf_op jit(solution)/shard_map/pallas_call | solution.py:588
  17.2 0.7 %collective-permute-start = (f32[1792,256]{1,0:T(8,128)S(1)}, f32[1792,256]{1,0:T(8,128)S(1)}, u32[]{:S(2)}, u32[]{:S(2)}) collective-permute-start(f32[1792,256]{1,0:T(8,128)S(1)} %get-tuple-element.41.own_ref), channel_id=1, source_target_pairs={{0,1},{1,0},{2,3},{3,2},{4,5},{5,4},{6,7},{7,6},{8,9},{9,8},{10,11... | collective-permute-start | bytes 5505032 | tf_op jit(solution)/shard_map/ppermute | solution.py:612
  17.9 7.4 %shard_map.78.inverse_ref = f32[512,512]{1,0:T(8,128)S(1)} custom-call(f32[512,256]{1,0:T(8,128)S(1)} %get-tuple-element.27.d2_own, f32[768,256]{1,0:T(8,128)S(1)} %get-tuple-element.34.keep_ref, f32[768,256]{1,0:T(8,128)S(1)} %get-tuple-element.40.came_ref), custom_call_target="tpu_custom_call" | custom-call | flops 5368709120 | bytes 3145728 | tf_op jit(solution)/shard_map/pallas_call | solution.py:588
  25.2 0.0 collective-permute-done.came_ref
  25.3 37.0 %shard_map.79 = (f32[512,256]{1,0:T(8,128)S(1)}, f32[512,256]{1,0:T(8,128)S(1)}, f32[64,512]{1,0:T(8,128)S(1)}, f32[64,2048]{1,0:T(8,128)S(1)}) custom-call(f32[512,512]{1,0:T(8,128)S(1)} %shard_map.78.inverse_ref, f32[1792,256]{1,0:T(8,128)S(1)} %get-tuple-element.41.own_ref, f32[1792,256]{1,0:T(8,128)S(1)} %collective-permute-done.came_ref, ...), custom_call_target="tpu_custom_call" | custom-call | flops 2415919104 | bytes 16515072 | tf_op jit(solution)/shard_map/pallas_call | solution.py:588
  62.3 1.2 %shard_map.80 = (f32[512,256]{1,0:T(8,128)}, f32[512,256]{1,0:T(8,128)}, f32[64,512]{1,0:T(8,128)}, f32[64,2048]{1,0:T(8,128)}) custom-call(f32[512,256]{1,0:T(8,128)S(1)} %get-tuple-element.46.refs_0_, f32[512,256]{1,0:T(8,128)S(1)} %get-tuple-element.47.refs_1_, f32[64,512]{1,0:T(8,128)S(1)} %get-tuple-element.48.refs_2_, ...), custom_call_target="tpu_custom_call" | custom-call | bytes 3407872 | tf_op jit(solution)/shard_map/pallas_call | solution.py:588
Async XLA Ops:
  17.2 8.1 %collective-permute-start = (f32[1792,256]{1,0:T(8,128)S(1)}, f32[1792,256]{1,0:T(8,128)S(1)}, u32[]{:S(2)}, u32[]{:S(2)}) collective-permute-start(f32[1792,256]{1,0:T(8,128)S(1)} %get-tuple-element.41.own_ref), channel_id=1, source_target_pairs={{0,1},{1,0},{2,3},{3,2},{4,5},{5,4},{6,7},{7,6},{8,9},{9,8},{10,11... | collective-permute-start | bytes 5505032 | tf_op jit(solution)/shard_map/ppermute | solution.py:612

commit v9 on v6

--- a/solution.py
+++ b/solution.py
@@ -370,7 +370,9 @@
     crossing = lambda: described(diag_send.at[HALF:], diag_came.at[HALF:], 1, after)
     handing = lambda: described(diag_came.at[HALF:], cross_came, 22, partner)
     half_of_own = lambda: described(hw_own.at[:, HALF:], hw_came, 24, partner)
-    turn = lambda chunk: described(hops.at[2, chunk], hops.at[3, chunk], 19 + chunk, row_after)
+    around = lambda chunk: low_send.at[pl.ds(DIRECT + chunk * CHUNK, CHUNK)]
+    first_hop = lambda chunk, source: described(source, hops.at[0, chunk], 10 + chunk, left_chip)
+    turn = lambda chunk: described(around(chunk), hops.at[3, chunk], 19 + chunk, row_after)
 
     @pl.when(core == 0)
     def _():
@@ -393,12 +395,18 @@
         low_send[span] = -mul((right[0][span], right[1][span]), u_left)
 
     low_rows(DIRECT, N - DIRECT)
-    steps = {}
-    for chunk in range(CHUNKS):
-        span = pl.ds(DIRECT + chunk * CHUNK, CHUNK)
-        steps[0, chunk] = remote(
-            low_send.at[span], hops.at[0, chunk], pair, 10 + chunk, left_chip
-        )
+
+    @pl.when(place_x == ROW - 1)
+    def _():
+        for chunk in range(CHUNKS):
+            turn(chunk).start()
+
+    @pl.when(place_x != ROW - 1)
+    def _():
+        for chunk in range(CHUNKS):
+            first_hop(chunk, around(chunk)).start()
+
+    steps = {(0, chunk): first_hop(chunk, around(chunk)) for chunk in range(CHUNKS)}
     lows = []
     for index, (first, count) in enumerate(((0, HALF), (HALF, DIRECT - HALF))):
         span = pl.ds(first, count)
@@ -417,6 +425,12 @@
     y = split(y_ref[...])
     y_back[...] = mul(y, n)
     later = remote(y_back, y_next, pair, 0, before)
+
+    @pl.when(place_x == ROW - 1)
+    def _():
+        for chunk in range(CHUNKS):
+            turn(chunk).wait_recv()
+            first_hop(chunk, hops.at[3, chunk]).start()
 
     def forward(hop, chunk):
         steps[hop, chunk].wait_recv()
@@ -497,14 +511,6 @@
     diag_came[:QUARTER, QUARTER:HALF] = diag_came[QUARTER:HALF, :QUARTER].T
     swap_corner = remote(diag_came.at[:HALF], corner_came, pair, 25, partner)
 
-    def last_hop(chunk):
-        steps[2, chunk].wait_recv()
-
-        @pl.when(place_x == 0)
-        def _():
-            turn(chunk).start()
-
-    last_hop(0)
     swap_x.wait_recv()
 
     @pl.when(core == 0)
@@ -533,24 +539,14 @@
     m_ref[:HALF, HALF:] = m_ref[HALF:, :HALF].T
     applied = split(mul(split(m_ref[...]), split(n_ref[mine]), NT))
     diag_ref[...] = diag_ref[...] - mul(n, applied)
-    last_hop(1)
     lows[0].wait_recv()
     low_out[...] = mul(split(n_ref[:, :HALF]), split(low_came[:HALF]))
-    last_hop(2)
     rhs_sent.wait_recv()
     rhs_ref[...] = rhs_ref[...] - mul(split(rhs_came[...]), n, NT)
     lows[1].wait_recv()
     for chunk in range(CHUNKS):
-        span = pl.ds(DIRECT + chunk * CHUNK, CHUNK)
-
-        @pl.when(place_x == 0)
-        def _():
-            turn(chunk).wait_recv()
-            low_came[span] = hops[3, chunk]
-
-        @pl.when(place_x != 0)
-        def _():
-            low_came[span] = hops[2, chunk]
+        steps[2, chunk].wait_recv()
+        low_came[pl.ds(DIRECT + chunk * CHUNK, CHUNK)] = hops[2, chunk]
 
     low_out[...] = low_out[...] + mul(split(n_ref[:, HALF:]), split(low_came[HALF:]))
     for copy in (
@@ -559,7 +555,7 @@
     ):
         copy.wait_send()
 
-    @pl.when(place_x == 0)
+    @pl.when(place_x == ROW - 1)
     def _():
         for chunk in range(CHUNKS):
             turn(chunk).wait_send()

time: 60.4 us -> 63.6 us (1.053)
  the two profiles are of different devices: /device:TPU:1 before, /device:TPU:5 now
where the time goes in v9:
time: 63.6 us; the launch traced here: 63.5 us
  Pallas kernels  62 us (97%)
  between operations  0.84 us (1%)
  starting transfers between devices  0.71 us (1%)
    pallas_call x6, Pallas kernels, call(): pl.pallas_call(body, out_shape=outs, in_specs=in_specs, out_specs=out_spe...  62 us
  transfers between devices with their start and end apart: 1, of which 0 were waited for; matrix products, arithmetic and copies ran while one was open for 0% of the time, Pallas kernels for 12%

profile of v9, /device:TPU:5, one launch (start us, length us, event | category | flops | bytes accessed | tf_op | source)
XLA Modules:
  0.0 63.5 jit_solution(4102869728579603682)
XLA Ops:
  0.6 3.9 %shard_map.75 = (f32[512,256]{1,0:T(8,128)S(1)}, f32[256,256]{1,0:T(8,128)S(1)}, f32[512,512]{1,0:T(8,128)S(1)}, f32[512,512]{1,0:T(8,128)S(1)}, f32[128,512]{1,...) custom-call(f32[2048,256]{1,0:T(8,128)} %diag.3, ...), custom_call_target="tpu_custom_call" | custom-call | flops 1006632960 | bytes 8916992 | tf_op jit(solution)/shard_map/pallas_call | solution.py:582
  4.5 7.8 %shard_map.76 = (f32[512,512]{1,0:T(8,128)S(1)}, f32[512,512]{1,0:T(8,128)S(1)}, f32[768,256]{1,0:T(8,128)S(1)}, f32[768,256]{1,0:T(8,128)S(1)}) custom-call(f32[512,256]{1,0:T(8,128)S(1)} %get-tuple-element.28.d_own, f32[256,256]{1,0:T(8,128)S(1)} %get-tuple-element.29.d_other, f32[512,512]{1,0:T(8,128)S(1)} %get-tuple-element.30.g_whole, ...), custom_call_target="tpu_custom_call" | custom-call | flops 5368709120 | bytes 6557696 | tf_op jit(solution)/shard_map/pallas_call | solution.py:582
  12.3 2.3 %shard_map.77 = (f32[768,256]{1,0:T(8,128)S(1)}, f32[512,512]{1,0:T(8,128)S(1)}, f32[128,512]{1,0:T(8,128)S(1)}, f32[1792,256]{1,0:T(8,128)S(1)}, f32[512,256]{1,0:T(8,128)S(1)}, /*index=5*/f32[2,64,512]{2,1,0:T(8,128)S(1)}) custom-call(f32[512,512]{1,0:T(8,128)S(1)} %get-tuple-element.35.inverse_ref.first_inverse, f32[512,512]{1,0:T(8,128)S(1)} %get-tuple-element.36.v_ref, ...), custom_call_target="tpu_custom_call" | custom-call | flops 1610612736 | bytes 8912896 | tf_op jit(solution)/shard_map/pallas_call | solution.py:582
  14.6 0.7 %collective-permute-start = (f32[1792,256]{1,0:T(8,128)S(1)}, f32[1792,256]{1,0:T(8,128)S(1)}, u32[]{:S(2)}, u32[]{:S(2)}) collective-permute-start(f32[1792,256]{1,0:T(8,128)S(1)} %get-tuple-element.41.own_ref), channel_id=1, source_target_pairs={{0,1},{1,0},{2,3},{3,2},{4,5},{5,4},{6,7},{7,6},{8,9},{9,8},{10,11... | collective-permute-start | bytes 5505032 | tf_op jit(solution)/shard_map/ppermute | solution.py:606
  15.4 7.4 %shard_map.78.inverse_ref = f32[512,512]{1,0:T(8,128)S(1)} custom-call(f32[512,256]{1,0:T(8,128)S(1)} %get-tuple-element.27.d2_own, f32[768,256]{1,0:T(8,128)S(1)} %get-tuple-element.34.keep_ref, f32[768,256]{1,0:T(8,128)S(1)} %get-tuple-element.40.came_ref), custom_call_target="tpu_custom_call" | custom-call | flops 5368709120 | bytes 3145728 | tf_op jit(solution)/shard_map/pallas_call | solution.py:582
  22.7 0.0 collective-permute-done.came_ref
  22.7 39.4 %shard_map.79 = (f32[512,256]{1,0:T(8,128)S(1)}, f32[512,256]{1,0:T(8,128)S(1)}, f32[64,512]{1,0:T(8,128)S(1)}, f32[64,2048]{1,0:T(8,128)S(1)}) custom-call(f32[512,512]{1,0:T(8,128)S(1)} %shard_map.78.inverse_ref, f32[1792,256]{1,0:T(8,128)S(1)} %get-tuple-element.41.own_ref, f32[1792,256]{1,0:T(8,128)S(1)} %collective-permute-done.came_ref, ...), custom_call_target="tpu_custom_call" | custom-call | flops 2415919104 | bytes 16515072 | tf_op jit(solution)/shard_map/pallas_call | solution.py:582
  62.2 1.2 %shard_map.80 = (f32[512,256]{1,0:T(8,128)}, f32[512,256]{1,0:T(8,128)}, f32[64,512]{1,0:T(8,128)}, f32[64,2048]{1,0:T(8,128)}) custom-call(f32[512,256]{1,0:T(8,128)S(1)} %get-tuple-element.46.refs_0_, f32[512,256]{1,0:T(8,128)S(1)} %get-tuple-element.47.refs_1_, f32[64,512]{1,0:T(8,128)S(1)} %get-tuple-element.48.refs_2_, ...), custom_call_target="tpu_custom_call" | custom-call | bytes 3407872 | tf_op jit(solution)/shard_map/pallas_call | solution.py:582
Async XLA Ops:
  14.6 8.1 %collective-permute-start = (f32[1792,256]{1,0:T(8,128)S(1)}, f32[1792,256]{1,0:T(8,128)S(1)}, u32[]{:S(2)}, u32[]{:S(2)}) collective-permute-start(f32[1792,256]{1,0:T(8,128)S(1)} %get-tuple-element.41.own_ref), channel_id=1, source_target_pairs={{0,1},{1,0},{2,3},{3,2},{4,5},{5,4},{6,7},{7,6},{8,9},{9,8},{10,11... | collective-permute-start | bytes 5505032 | tf_op jit(solution)/shard_map/ppermute | solution.py:606
